TPU v7x, 32 devices: a whole 2x2x4 slice. The times are simulated.
32 devices in a mesh: dp: 4 (over z), row: 2 (over y), col: 4 (over x, core).
Axes of the slice: x: 2, y: 2, z: 4, core: 2. Of those that a mesh axis runs over, the one named last changes fastest.
Arguments:
- tokens: float32 [8, 2048, 768], P(('dp', 'row'), 'col'), may hold values from -4 to 4
- condition: float32 [8, 128], P(('dp', 'row')), may hold values from -3 to 3
- lengths: int32 [8], P(('dp', 'row')), may hold values from 1024 to 2048, as said below
- condition_weight: float32 [128, 4608], P(None, ('dp', 'row')), may hold values from -0.25 to 0.25
- condition_bias: float32 [4608], replicated, may hold values from -1 to 1
- attention_in: float32 [768, 3, 768], P(('dp', 'row'), None, 'col'), may hold values from -0.21875 to 0.21875
- attention_out: float32 [768, 768], P('col', ('dp', 'row')), may hold values from -0.4375 to 0.4375
- up_weight: float32 [768, 3072], P(('dp', 'row'), 'col'), may hold values from -0.21875 to 0.21875
- up_bias: float32 [3072], replicated, may hold values from -1.5 to 1.5
- down_weight: float32 [3072, 768], P('col', ('dp', 'row')), may hold values from -0.109375 to 0.109375
- down_bias: float32 [768], replicated, may hold values from -1.5 to 1.5
- cotangent: float32 [8, 2048, 768], P(('dp', 'row'), 'col'), may hold values from -4 to 4
Outputs:
- output: float32 [8, 2048, 768], P(('dp', 'row'), 'col')
- gradient_tokens: float32 [8, 2048, 768], P(('dp', 'row'), 'col')
- gradient_condition: float32 [8, 128], P(('dp', 'row'))
- gradient_condition_weight: float32 [128, 4608], P(None, ('dp', 'row'))
- gradient_condition_bias: float32 [4608], replicated
- gradient_attention_in: float32 [768, 3, 768], P(('dp', 'row'), None, 'col')
- gradient_attention_out: float32 [768, 768], P('col', ('dp', 'row'))
- gradient_up_weight: float32 [768, 3072], P(('dp', 'row'), 'col')
- gradient_up_bias: float32 [3072], P('col')
- gradient_down_weight: float32 [3072, 768], P('col', ('dp', 'row'))
- gradient_down_bias: float32 [768], replicated
Inputs may be any that keep to these rules, and one draw needn't show every extreme that they name: Row b holds lengths[b] valid tokens in its first slots; some row has 2048 valid tokens and another has 1024.
All inputs are finite; a program needn't handle non-finite values.
Results may differ from a plain program's by a relative error of at most 0.012.
The roundings to bfloat16 on the way count: a program that leaves them out, or rounds other values in their place, can miss the bound.
Values may be sent and summed in bfloat16 or wider, within the bound.
A program may use at most 128 MiB of HBM per device.

v0:
```python
import math

import jax
import jax.numpy as jnp
from jax import lax
from jax.sharding import PartitionSpec as P

HD = 64


EPSILON = 1e-06
MASKED = -1e30
CUBIC = 0.044715
SLOPE = math.sqrt(2.0 / math.pi)


def layer_norm(values):
    center = values - jnp.mean(values, axis=-1, keepdims=True)
    spread = jnp.mean(center * center, axis=-1, keepdims=True)
    return center * lax.rsqrt(spread + EPSILON)


def norm_shift(values, shift, scale):
    return layer_norm(values) * (1.0 + scale) + shift


def gelu_tanh(values):
    return 0.5 * values * (1.0 + jnp.tanh(SLOPE * (values + CUBIC * values * values * values)))


def rotary_tables(length, head_size):
    half = head_size // 2
    exponent = jnp.arange(half).astype(jnp.float32) * (2.0 / head_size)
    frequency = jnp.exp(-math.log(10000.0) * exponent)
    angle = jnp.arange(length).astype(jnp.float32)[:, None] * frequency[None, :]
    return (jnp.cos(angle)[:, None, :], jnp.sin(angle)[:, None, :])


def rotate(values, cosine, sine):
    half = values.shape[-1] // 2
    first = values[..., :half]
    second = values[..., half:]
    return jnp.concatenate(
        [first * cosine - second * sine, second * cosine + first * sine], axis=-1
    )


def shards(
    tokens,
    condition,
    lengths,
    condition_weight,
    condition_bias,
    attention_in,
    attention_out,
    up_weight,
    up_bias,
    down_weight,
    down_bias,
    cotangent,
):
    columns = lax.axis_size("col")
    column_index = lax.axis_index("col")
    rows = tokens.shape[1]
    width = tokens.shape[2]
    length_all = rows * columns
    local_width = attention_in.shape[2]
    heads_here = local_width // HD
    scale = 1.0 / math.sqrt(HD)
    in_full, out_full, up_full, down_full, condition_full = (
        lax.all_gather(attention_in.astype(jnp.bfloat16), ("dp", "row"), axis=0, tiled=True),
        lax.all_gather(attention_out.astype(jnp.bfloat16), ("dp", "row"), axis=1, tiled=True),
        lax.all_gather(up_weight.astype(jnp.bfloat16), ("dp", "row"), axis=0, tiled=True),
        lax.all_gather(down_weight.astype(jnp.bfloat16), ("dp", "row"), axis=1, tiled=True),
        lax.all_gather(condition_weight.astype(jnp.bfloat16), ("dp", "row"), axis=1, tiled=True),
    )
    condition_low = condition.astype(jnp.bfloat16)
    modulation = (
        jnp.dot(condition_low, condition_full, preferred_element_type=jnp.float32)[0]
        + condition_bias
    )
    parts = modulation.reshape(6, width)
    own_rows = tokens[0]
    length = lengths[0]
    position = column_index * rows + jnp.arange(rows)
    valid = (position < length).astype(jnp.float32)
    key_valid = jnp.arange(length_all) < length
    normed, first_pull = jax.vjp(norm_shift, own_rows, parts[0], parts[1])
    normed_all = lax.all_gather(normed.astype(jnp.bfloat16), "col", axis=0, tiled=True)
    projected = jnp.einsum("sd,dte->ste", normed_all, in_full, preferred_element_type=jnp.float32)
    cosine, sine = rotary_tables(length_all, HD)
    query_rows = rotate(projected[:, 0].reshape(length_all, heads_here, HD), cosine, sine).astype(
        jnp.bfloat16
    )
    key_rows = rotate(projected[:, 1].reshape(length_all, heads_here, HD), cosine, sine).astype(
        jnp.bfloat16
    )
    value_rows = projected[:, 2].reshape(length_all, heads_here, HD).astype(jnp.bfloat16)
    block = min(512, length_all)
    count_blocks = length_all // block

    def scores_of(query_block):
        raw = jnp.einsum("qhd,khd->hqk", query_block, key_rows, preferred_element_type=jnp.float32)
        return jnp.where(key_valid[None, None, :], raw * scale, MASKED)

    def forward_block(query_block):
        scores = scores_of(query_block)
        top = jnp.max(scores, axis=-1, keepdims=True)
        weights = jnp.exp(scores - top)
        total = jnp.sum(weights, axis=-1, keepdims=True)
        mixed = jnp.einsum(
            "hqk,khd->qhd",
            (weights / total).astype(jnp.bfloat16),
            value_rows,
            preferred_element_type=jnp.float32,
        )
        return (mixed, (top + jnp.log(total))[..., 0])

    query_blocks = query_rows.reshape(count_blocks, block, heads_here, HD)
    mixed, log_total = lax.map(forward_block, query_blocks)
    mixed_low = mixed.reshape(length_all, local_width).astype(jnp.bfloat16)
    piece = mixed_low
    attention = lax.psum_scatter(
        jnp.dot(piece, out_full, preferred_element_type=jnp.float32),
        "col",
        scatter_dimension=0,
        tiled=True,
    )
    middle = own_rows + parts[2] * attention
    second, second_pull = jax.vjp(norm_shift, middle, parts[3], parts[4])
    second_low = second.astype(jnp.bfloat16)
    hidden_cols = up_full.shape[1]
    second_all = lax.all_gather(second_low, "col", axis=0, tiled=True)
    bias_part = lax.dynamic_slice_in_dim(up_bias, column_index * hidden_cols, hidden_cols)
    before = jnp.dot(second_all, up_full, preferred_element_type=jnp.float32) + bias_part
    hidden, gelu_pull = jax.vjp(gelu_tanh, before)
    hidden_low = hidden.astype(jnp.bfloat16)
    piece = hidden_low
    feed = lax.psum_scatter(
        jnp.dot(piece, down_full, preferred_element_type=jnp.float32),
        "col",
        scatter_dimension=0,
        tiled=True,
    )
    result = middle + parts[5] * (feed + down_bias)
    incoming = cotangent[0] * valid[:, None]
    down_bias_part = jnp.sum(parts[5] * incoming, axis=0)
    gate_feed = jnp.sum(incoming * (feed + down_bias), axis=0)
    feed_back = (parts[5] * incoming).astype(jnp.bfloat16)
    feed_back_all = lax.all_gather(feed_back, "col", axis=0, tiled=True)
    hidden_back = jnp.einsum(
        "sd,fd->sf", feed_back_all, down_full, preferred_element_type=jnp.float32
    )
    down_grad = jnp.einsum(
        "sf,sd->fd", hidden_low, feed_back_all, preferred_element_type=jnp.float32
    )
    before_back = gelu_pull(hidden_back)[0].astype(jnp.bfloat16)
    up_grad = jnp.einsum("sd,sf->df", second_all, before_back, preferred_element_type=jnp.float32)
    up_bias_part = jnp.sum(before_back.astype(jnp.float32), axis=0)
    piece = before_back
    second_back = lax.psum_scatter(
        jnp.einsum("sf,df->sd", piece, up_full, preferred_element_type=jnp.float32),
        "col",
        scatter_dimension=0,
        tiled=True,
    )
    middle_part, shift_feed, scale_feed = second_pull(second_back)
    middle_back = incoming + middle_part
    gate_attention = jnp.sum(middle_back * attention, axis=0)
    attention_back = (parts[2] * middle_back).astype(jnp.bfloat16)
    attention_back_all = lax.all_gather(attention_back, "col", axis=0, tiled=True)
    out_grad = jnp.einsum(
        "sc,sd->cd", mixed_low, attention_back_all, preferred_element_type=jnp.float32
    )
    mixed_back = jnp.einsum(
        "sd,cd->sc", attention_back_all, out_full, preferred_element_type=jnp.float32
    ).astype(jnp.bfloat16)

    def backward_block(carry, item):
        key_sum, value_sum = carry
        query_block, back_block, log_block = item
        scores = scores_of(query_block)
        weights = jnp.exp(scores - log_block[..., None])
        weight_back = jnp.einsum(
            "qhd,khd->hqk", back_block, value_rows, preferred_element_type=jnp.float32
        )
        center = jnp.sum(weights * weight_back, axis=-1, keepdims=True)
        score_back = (weights * (weight_back - center) * scale).astype(jnp.bfloat16)
        query_back = jnp.einsum(
            "hqk,khd->qhd", score_back, key_rows, preferred_element_type=jnp.float32
        )
        key_sum = key_sum + jnp.einsum(
            "hqk,qhd->khd", score_back, query_block, preferred_element_type=jnp.float32
        )
        value_sum = value_sum + jnp.einsum(
            "hqk,qhd->khd",
            weights.astype(jnp.bfloat16),
            back_block,
            preferred_element_type=jnp.float32,
        )
        return ((key_sum, value_sum), query_back)

    zeros = jnp.zeros((length_all, heads_here, HD), jnp.float32)
    back_blocks = mixed_back.reshape(count_blocks, block, heads_here, HD)
    (key_back, value_back), query_back = lax.scan(
        backward_block, (zeros, zeros), (query_blocks, back_blocks, log_total)
    )
    query_back = query_back.reshape(length_all, heads_here, HD)
    projected_back = jnp.stack(
        [
            rotate(query_back, cosine, -sine).reshape(length_all, local_width),
            rotate(key_back, cosine, -sine).reshape(length_all, local_width),
            value_back.reshape(length_all, local_width),
        ],
        axis=1,
    ).astype(jnp.bfloat16)
    in_grad = jnp.einsum(
        "sd,ste->dte", normed_all, projected_back, preferred_element_type=jnp.float32
    )
    piece = projected_back
    normed_back = lax.psum_scatter(
        jnp.einsum("ste,dte->sd", piece, in_full, preferred_element_type=jnp.float32),
        "col",
        scatter_dimension=0,
        tiled=True,
    )
    rows_part, shift_attention, scale_attention = first_pull(normed_back)
    tokens_back = middle_back + rows_part
    modulation_part = jnp.concatenate(
        [shift_attention, scale_attention, gate_attention, shift_feed, scale_feed, gate_feed]
    )
    modulation_back, down_bias_column = lax.psum((modulation_part, down_bias_part), "col")
    condition_back = jnp.dot(
        condition_full.astype(jnp.float32), modulation_back, precision=lax.Precision.HIGHEST
    )
    condition_grad = condition_low.astype(jnp.float32)[0][:, None] * modulation_back[None, :]
    in_grad, out_grad, up_grad, down_grad, condition_grad = (
        lax.psum_scatter(in_grad, ("dp", "row"), scatter_dimension=0, tiled=True),
        lax.psum_scatter(out_grad, ("dp", "row"), scatter_dimension=1, tiled=True),
        lax.psum_scatter(up_grad, ("dp", "row"), scatter_dimension=0, tiled=True),
        lax.psum_scatter(down_grad, ("dp", "row"), scatter_dimension=1, tiled=True),
        lax.psum_scatter(condition_grad, ("dp", "row"), scatter_dimension=1, tiled=True),
    )
    bias_grad, up_bias_grad, down_bias_grad = lax.psum(
        (modulation_back, up_bias_part, down_bias_column), ("dp", "row")
    )
    return (
        result[None],
        tokens_back[None],
        condition_back[None],
        condition_grad,
        bias_grad,
        in_grad,
        out_grad,
        up_grad,
        up_bias_grad,
        down_grad,
        down_bias_grad,
    )


def solution(mesh):
    in_specs = (
        P(("dp", "row"), "col", None),
        P(("dp", "row"), None),
        P(("dp", "row")),
        P(None, ("dp", "row")),
        P(),
        P(("dp", "row"), None, "col"),
        P("col", ("dp", "row")),
        P(("dp", "row"), "col"),
        P(),
        P("col", ("dp", "row")),
        P(),
        P(("dp", "row"), "col", None),
    )
    out_specs = (
        P(("dp", "row"), "col", None),
        P(("dp", "row"), "col", None),
        P(("dp", "row"), None),
        P(None, ("dp", "row")),
        P(),
        P(("dp", "row"), None, "col"),
        P("col", ("dp", "row")),
        P(("dp", "row"), "col"),
        P("col"),
        P("col", ("dp", "row")),
        P(),
    )
    return jax.shard_map(shards, mesh=mesh, in_specs=in_specs, out_specs=out_specs, check_vma=False)
```

profile of v0, /device:TPU:0, one launch (start us, length us, event | category | flops | bytes accessed | tf_op | source)
XLA Modules:
  0.0 1283.8 jit_solution(16584644986181684944)
XLA Ops:
  11.0 43.6 %all-gather.8.cloned.1.call-done = bf16[128,4608]{0,1:T(8,128)(2,1)} async-done(((bf16[128,576]{0,1:T(8,128)(2,1)}), bf16[128,4608]{0,1:T(8,128)(2,1)}) %all-gather.8.cloned.1.call-update) | async-done | bytes 1179664 | tf_op jit(solution)/shard_map/all_gather | solution.py:75
  59.2 35.7 %all_gather.29 = bf16[768,3,192]{2,1,0:T(4,128)(2,1)S(1)} all-gather(bf16[96,3,192]{2,1,0:T(4,128)(2,1)S(1)} %copy.47), channel_id=1, replica_groups=mesh['dp'=4,'row'=2,'col'=4] {'dp','row'}, dimensions={0}, use_global_device_ids=true | all-gather | bytes 995328 | tf_op jit(solution)/shard_map/all_gather | solution.py:71
  97.0 31.3 %all_gather.30 = bf16[192,768]{0,1:T(8,128)(2,1)S(1)} all-gather(bf16[192,96]{0,1:T(8,128)(2,1)} %copy.52), channel_id=1, replica_groups=mesh['dp'=4,'row'=2,'col'=4] {'dp','row'}, dimensions={1}, use_global_device_ids=true | all-gather | bytes 331776 | tf_op jit(solution)/shard_map/all_gather | solution.py:72
  130.1 4.2 fusion.108
  136.9 43.9 %while.28 = (s32[]{:T(128)}, bf16[4,512,3,64]{1,3,2,0:T(8,128)(2,1)}, f32[4,3,512]{2,1,0:T(4,128)}, bf16[4,512,3,64]{1,3,2,0:T(8,128)(2,1)}, bf16[2048,3,64]{0,2...) while((s32[]{:T(128)}, bf16[4,512,3,64]{1,3,2,0:T(8,128)(2,1)}, ...), condition=%wide.region_5.6_spmd.clone, body=%wide.region_2.5_spmd.clone.sunk | while | flops 843055616 | bytes 46266532 | solution.py:120
  189.1 56.8 %reduce-scatter.12.cloned.1.call-done = f32[512,768]{1,0:T(8,128)} async-done(((f32[2048,768]{1,0:T(8,128)}), f32[512,768]{1,0:T(8,128)}) %reduce-scatter.12.cloned.1.call-update) | async-done | bytes 1572880 | tf_op jit(solution)/shard_map/reduce_scatter | solution.py:123
  255.6 34.0 %all-gather.14.cloned.1.call-done = bf16[768,768]{1,0:T(8,128)(2,1)} async-done(((bf16[96,768]{1,0:T(8,128)(2,1)}), bf16[768,768]{1,0:T(8,128)(2,1)}) %all-gather.14.cloned.1.call-update) | async-done | bytes 1179664 | tf_op jit(solution)/shard_map/all_gather | solution.py:73
  289.7 29.2 %all-gather.12.cloned.1.call-done = bf16[2048,768]{1,0:T(8,128)(2,1)} async-done(((bf16[512,768]{1,0:T(8,128)(2,1)}), bf16[2048,768]{1,0:T(8,128)(2,1)}) %all-gather.12.cloned.1.call-update) | async-done | bytes 3145744 | tf_op jit(solution)/shard_map/all_gather | solution.py:133
  318.9 7.5 fusion.110
  326.4 36.3 %all-gather.16.cloned.1.call-done = bf16[768,768]{0,1:T(8,128)(2,1)} async-done(((bf16[768,96]{0,1:T(8,128)(2,1)}), bf16[768,768]{0,1:T(8,128)(2,1)}) %all-gather.16.cloned.1.call-update) | async-done | bytes 1179664 | tf_op jit(solution)/shard_map/all_gather | solution.py:74
  362.6 28.8 %all-gather.18.cloned.1.call-done = bf16[2048,768]{1,0:T(8,128)(2,1)} async-done(((bf16[512,768]{1,0:T(8,128)(2,1)}), bf16[2048,768]{1,0:T(8,128)(2,1)}) %all-gather.18.cloned.1.call-update) | async-done | bytes 3145744 | tf_op jit(solution)/shard_map/all_gather | solution.py:150
  391.4 11.9 convert_reduce_fusion
  404.9 4.5 fusion.112
  410.7 7.2 fusion.111
  418.0 50.5 %reduce-scatter.16.cloned.1.call-done = f32[512,768]{1,0:T(8,128)} async-done(((f32[2048,768]{1,0:T(8,128)}), f32[512,768]{1,0:T(8,128)}) %reduce-scatter.16.cloned.1.call-update) | async-done | bytes 1572880 | tf_op jit(solution)/shard_map/reduce_scatter | solution.py:161
  474.3 55.6 %reduce-scatter.14.cloned.1.call-done = f32[512,768]{1,0:T(8,128)} async-done(((f32[2048,768]{1,0:T(8,128)}), f32[512,768]{1,0:T(8,128)}) %reduce-scatter.14.cloned.1.call-update) | async-done | bytes 1572880 | tf_op jit(solution)/shard_map/reduce_scatter | solution.py:139
  529.9 5.3 multiply_reduce_fusion.9
  537.4 28.6 %all-gather.20.cloned.1.call-done = bf16[2048,768]{1,0:T(8,128)(2,1)} async-done(((bf16[512,768]{1,0:T(8,128)(2,1)}), bf16[2048,768]{1,0:T(8,128)(2,1)}) %all-gather.20.cloned.1.call-update) | async-done | bytes 3145744 | tf_op jit(solution)/shard_map/all_gather | solution.py:171
  573.3 276.0 %while.29 = (s32[]{:T(128)}, f32[2048,3,64]{0,2,1:T(8,128)}, f32[2048,3,64]{0,2,1:T(8,128)}, f32[4,512,3,64]{1,0,3,2:T(4,128)}, bf16[4,512,3,64]{1,3,2,0:T(8,128...) while((s32[]{:T(128)}, f32[2048,3,64]{0,2,1:T(8,128)}, ...), condition=%wide.region_15.16_spmd.clone, body=%wide.region_13.15_spmd.clone.sunk | while | flops 2096636928 | bytes 187615472 | solution.py:205
  582.4 7.3 fusion.180
  589.7 21.7 %fusion.184 = f32[1,512,3,64]{1,3,2,0:T(8,128)S(1)} fusion(bf16[2048,3,64]{0,2,1:T(8,128)(2,1)S(1)} %get-tuple-element.450, f32[3,512,2048]{2,1,0:T(8,128)} %fusion.180, f32[3,512,2048]{2,1,0:T(8,128)} %copy-done, f32[3,512]{1,0:T(4,128)S(1)} %dynamic-slice_bitcast_fusion.2, pred[2048]{0:T(1024)(128)(4,1)S(1)} %iota_compare_fusion.5), kind=kOutput, calls=%fused_computation.40.clone.1 | convolution fusion | flops 437259776 | bytes 26353664 | tf_op jit(solution)/shard_map/while/body/eval_jaxpr/hqk,khd->qhd/dot_general | solution.py:189
  611.3 21.7 %fusion.182 = f32[2048,3,64]{0,2,1:T(8,128)} fusion(f32[3,512,2048]{2,1,0:T(8,128)} %fusion.180, f32[3,512,2048]{2,1,0:T(8,128)} %copy-done, f32[3,512]{1,0:T(4,128)S(1)} %dynamic-slice_bitcast_fusion.2, pred[2048]{0:T(1024)(128)(4,1)S(1)} %iota_compare_fusion.5, f32[2048,3,64]{0,2,1:T(8,128)} %get-tuple-element.434, pred[]{:T(512)S(6)} %compare.3, ...), kind=kOutput, calls=%fused_computation.38.clone.1 | convolution fusion | flops 438046208 | bytes 53694468 | tf_op jit(solution)/shard_map/while/body/eval_jaxpr/hqk,qhd->khd/dot_general | solution.py:192
  633.4 8.6 dynamic_update_slice.21
  645.3 4.1 fusion.183
  651.0 7.3 fusion.180
  658.2 21.7 %fusion.184 = f32[1,512,3,64]{1,3,2,0:T(8,128)S(1)} fusion(bf16[2048,3,64]{0,2,1:T(8,128)(2,1)S(1)} %get-tuple-element.450, f32[3,512,2048]{2,1,0:T(8,128)} %fusion.180, f32[3,512,2048]{2,1,0:T(8,128)} %copy-done, f32[3,512]{1,0:T(4,128)S(1)} %dynamic-slice_bitcast_fusion.2, pred[2048]{0:T(1024)(128)(4,1)S(1)} %iota_compare_fusion.5), kind=kOutput, calls=%fused_computation.40.clone.1 | convolution fusion | flops 437259776 | bytes 26353664 | tf_op jit(solution)/shard_map/while/body/eval_jaxpr/hqk,khd->qhd/dot_general | solution.py:189
  679.9 22.2 %fusion.182 = f32[2048,3,64]{0,2,1:T(8,128)} fusion(f32[3,512,2048]{2,1,0:T(8,128)} %fusion.180, f32[3,512,2048]{2,1,0:T(8,128)} %copy-done, f32[3,512]{1,0:T(4,128)S(1)} %dynamic-slice_bitcast_fusion.2, pred[2048]{0:T(1024)(128)(4,1)S(1)} %iota_compare_fusion.5, f32[2048,3,64]{0,2,1:T(8,128)} %get-tuple-element.434, pred[]{:T(512)S(6)} %compare.3, ...), kind=kOutput, calls=%fused_computation.38.clone.1 | convolution fusion | flops 438046208 | bytes 53694468 | tf_op jit(solution)/shard_map/while/body/eval_jaxpr/hqk,qhd->khd/dot_general | solution.py:192
  702.5 8.6 dynamic_update_slice.21
  720.1 7.3 fusion.180
  727.3 21.7 %fusion.184 = f32[1,512,3,64]{1,3,2,0:T(8,128)S(1)} fusion(bf16[2048,3,64]{0,2,1:T(8,128)(2,1)S(1)} %get-tuple-element.450, f32[3,512,2048]{2,1,0:T(8,128)} %fusion.180, f32[3,512,2048]{2,1,0:T(8,128)} %copy-done, f32[3,512]{1,0:T(4,128)S(1)} %dynamic-slice_bitcast_fusion.2, pred[2048]{0:T(1024)(128)(4,1)S(1)} %iota_compare_fusion.5), kind=kOutput, calls=%fused_computation.40.clone.1 | convolution fusion | flops 437259776 | bytes 26353664 | tf_op jit(solution)/shard_map/while/body/eval_jaxpr/hqk,khd->qhd/dot_general | solution.py:189
  749.0 22.2 %fusion.182 = f32[2048,3,64]{0,2,1:T(8,128)} fusion(f32[3,512,2048]{2,1,0:T(8,128)} %fusion.180, f32[3,512,2048]{2,1,0:T(8,128)} %copy-done, f32[3,512]{1,0:T(4,128)S(1)} %dynamic-slice_bitcast_fusion.2, pred[2048]{0:T(1024)(128)(4,1)S(1)} %iota_compare_fusion.5, f32[2048,3,64]{0,2,1:T(8,128)} %get-tuple-element.434, pred[]{:T(512)S(6)} %compare.3, ...), kind=kOutput, calls=%fused_computation.38.clone.1 | convolution fusion | flops 438046208 | bytes 53694468 | tf_op jit(solution)/shard_map/while/body/eval_jaxpr/hqk,qhd->khd/dot_general | solution.py:192
  771.6 8.6 dynamic_update_slice.21
  789.1 7.3 fusion.180
  796.4 21.7 %fusion.184 = f32[1,512,3,64]{1,3,2,0:T(8,128)S(1)} fusion(bf16[2048,3,64]{0,2,1:T(8,128)(2,1)S(1)} %get-tuple-element.450, f32[3,512,2048]{2,1,0:T(8,128)} %fusion.180, f32[3,512,2048]{2,1,0:T(8,128)} %copy-done, f32[3,512]{1,0:T(4,128)S(1)} %dynamic-slice_bitcast_fusion.2, pred[2048]{0:T(1024)(128)(4,1)S(1)} %iota_compare_fusion.5), kind=kOutput, calls=%fused_computation.40.clone.1 | convolution fusion | flops 437259776 | bytes 26353664 | tf_op jit(solution)/shard_map/while/body/eval_jaxpr/hqk,khd->qhd/dot_general | solution.py:189
  818.1 22.2 %fusion.182 = f32[2048,3,64]{0,2,1:T(8,128)} fusion(f32[3,512,2048]{2,1,0:T(8,128)} %fusion.180, f32[3,512,2048]{2,1,0:T(8,128)} %copy-done, f32[3,512]{1,0:T(4,128)S(1)} %dynamic-slice_bitcast_fusion.2, pred[2048]{0:T(1024)(128)(4,1)S(1)} %iota_compare_fusion.5, f32[2048,3,64]{0,2,1:T(8,128)} %get-tuple-element.434, pred[]{:T(512)S(6)} %compare.3, ...), kind=kOutput, calls=%fused_computation.38.clone.1 | convolution fusion | flops 438046208 | bytes 53694468 | tf_op jit(solution)/shard_map/while/body/eval_jaxpr/hqk,qhd->khd/dot_general | solution.py:192
  840.7 8.6 dynamic_update_slice.21
  855.3 4.6 convolution_bitcast_fusion
  865.2 7.4 fusion.114
  872.6 7.1 fusion.115
  880.8 6.8 fusion.92
  888.3 30.7 %reduce-scatter.18.cloned.1.call-done = f32[512,768]{1,0:T(8,128)} async-done(((f32[2048,768]{1,0:T(8,128)}), f32[512,768]{1,0:T(8,128)}) %reduce-scatter.18.cloned.1.call-update) | async-done | bytes 1572880 | tf_op jit(solution)/shard_map/reduce_scatter | solution.py:221
  921.1 10.3 all-reduce.1
  934.4 50.9 %reduce-scatter.28.cloned.1.call-done = f32[96,192]{1,0:T(8,128)} async-done(((f32[768,192]{1,0:T(8,128)}), f32[96,192]{1,0:T(8,128)}) %reduce-scatter.28.cloned.1.call-update) | async-done | bytes 73744
  987.0 35.8 %all-reduce = (f32[4608]{0:T(1024)}, f32[768]{0:T(1024)}, f32[768]{0:T(1024)}) all-reduce(f32[4608]{0:T(1024)S(1)} %get-tuple-element.246, f32[768]{0:T(1024)S(1)} %copy-done.48, f32[768]{0:T(1024)S(1)} %get-tuple-element.247), channel_id=1, replica_groups=mesh['dp'=4,'row'=2,'col'=4] {'dp','row'}, use_global_device_ids=true, to_apply=%region_27.28 | all-reduce | flops 6144 | bytes 49152 | tf_op jit(solution)/shard_map/psum | solution.py:244
  1026.6 31.8 %reduce-scatter.24.cloned.1.call-done = f32[96,768]{1,0:T(8,128)} async-done(((f32[768,768]{1,0:T(8,128)}), f32[96,768]{1,0:T(8,128)}) %reduce-scatter.24.cloned.1.call-update) | async-done | bytes 294928 | tf_op jit(solution)/shard_map/reduce_scatter | solution.py:240
  1058.4 72.7 %reduce-scatter.26.cloned.1.call-done = f32[768,96]{0,1:T(8,128)} async-done(((f32[768,768]{0,1:T(8,128)}), f32[768,96]{0,1:T(8,128)}) %reduce-scatter.26.cloned.1.call-update) | async-done | bytes 294928 | tf_op jit(solution)/shard_map/reduce_scatter | solution.py:241
  1131.1 73.0 %reduce-scatter.22.cloned.1.call-done = f32[96,3,192]{2,0,1:T(8,128)} async-done(((f32[768,3,192]{2,0,1:T(8,128)}), f32[96,3,192]{2,0,1:T(8,128)}) %reduce-scatter.22.cloned.1.call-update) | async-done | bytes 221200 | tf_op jit(solution)/shard_map/reduce_scatter | solution.py:238
  1204.1 72.7 %reduce-scatter.20.cloned.1.call-done = f32[128,576]{0,1:T(8,128)} async-done(((f32[128,4608]{0,1:T(8,128)}), f32[128,576]{0,1:T(8,128)}) %reduce-scatter.20.cloned.1.call-update) | async-done | bytes 294928 | tf_op jit(solution)/shard_map/reduce_scatter | solution.py:242
  (280 shorter events, 150.3 us)
Async XLA Ops:
  7.2 3.5 copy-start.1
  7.2 47.5 %copy-start.49 = (f32[1,128]{1,0:T(1,128)S(1)}, f32[1,128]{1,0:T(1,128)}, u32[]{:S(2)}) copy-start(f32[1,128]{1,0:T(1,128)} %param.17) | copy-start | bytes 1540
  7.2 47.4 %all-gather.8.cloned.1.call-start = ((), (), s32[]{:S(2)}) async-start(), calls=%async_computation.9 | async-start | bytes 1327104 | tf_op jit(solution)/shard_map/all_gather | solution.py:75
  9.0 47.4 %copy-start.37 = (f32[4608]{0:T(1024)S(1)}, f32[4608]{0:T(1024)}, u32[]{:S(2)}) copy-start(f32[4608]{0:T(1024)} %param.20) | copy-start | bytes 55300
  9.0 121.0 %all-gather.10.cloned.1.call-start = ((), (), s32[]{:S(2)}) async-start(), calls=%async_computation.10 | async-start | bytes 3932160 | tf_op jit(solution)/shard_map/all_gather | solution.py:89
  10.6 47.5 %copy-start.32 = (f32[512]{0:T(512)}, f32[512]{0:T(512)S(1)}, u32[]{:S(2)}) copy-start(f32[512]{0:T(512)S(1)} %broadcast_multiply_fusion.2) | copy-start | bytes 6148
  11.0 43.7 %copy-start.38 = (f32[512]{0:T(512)}, f32[512]{0:T(512)S(1)}, u32[]{:S(2)}) copy-start(f32[512]{0:T(512)S(1)} %multiply_reduce_fusion.8) | copy-start | bytes 6148
  11.0 47.3 %copy-start.29 = (f32[192,96]{1,0:T(8,128)S(1)}, f32[192,96]{1,0:T(8,128)}, u32[]{:S(2)}) copy-start(f32[192,96]{1,0:T(8,128)} %param.22) | copy-start | bytes 221188
  11.0 48.0 %copy-start.28 = (f32[96,3,192]{2,0,1:T(8,128)S(1)}, f32[96,3,192]{2,0,1:T(8,128)}, u32[]{:S(2)}) copy-start(f32[96,3,192]{2,0,1:T(8,128)} %param.21) | copy-start | bytes 663556
  11.0 47.3 %copy-start.34 = (f32[512]{0:T(512)}, f32[512]{0:T(512)S(1)}, u32[]{:S(2)}) copy-start(f32[512]{0:T(512)S(1)} %fusion.96) | copy-start | bytes 6148
  58.2 187.7 %reduce-scatter.12.cloned.1.call-start = ((), (), s32[]{:S(2)}) async-start(), calls=%async_computation.11 | async-start | bytes 7864320 | tf_op jit(solution)/shard_map/reduce_scatter | solution.py:123
  130.1 4.7 copy-start.15
  173.4 2.8 copy-start.24
  187.3 102.3 %all-gather.14.cloned.1.call-start = ((), (), s32[]{:S(2)}) async-start(), calls=%async_computation.13 | async-start | bytes 1327104 | tf_op jit(solution)/shard_map/all_gather | solution.py:73
  189.1 129.8 %all-gather.12.cloned.1.call-start = ((), (), s32[]{:S(2)}) async-start(), calls=%async_computation.12 | async-start | bytes 3932160 | tf_op jit(solution)/shard_map/all_gather | solution.py:133
  245.9 3.2 copy-start.42
  247.6 6.1 copy-start.9
  250.3 112.3 %all-gather.16.cloned.1.call-start = ((), (), s32[]{:S(2)}) async-start(), calls=%async_computation.14 | async-start | bytes 1327104 | tf_op jit(solution)/shard_map/all_gather | solution.py:74
  252.4 139.0 %all-gather.18.cloned.1.call-start = ((), (), s32[]{:S(2)}) async-start(), calls=%async_computation.16 | async-start | bytes 3932160 | tf_op jit(solution)/shard_map/all_gather | solution.py:150
  254.8 213.7 %reduce-scatter.16.cloned.1.call-start = ((), (), s32[]{:S(2)}) async-start(), calls=%async_computation.17 | async-start | bytes 7864320 | tf_op jit(solution)/shard_map/reduce_scatter | solution.py:161
  326.4 78.5 %copy-start.51 = (bf16[768,768]{1,0:T(8,128)(2,1)S(1)}, bf16[768,768]{1,0:T(8,128)(2,1)}, u32[]{:S(2)}) copy-start(bf16[768,768]{1,0:T(8,128)(2,1)} %all-gather.14.cloned.1.call-done) | copy-start | bytes 3538948
  409.5 120.4 %reduce-scatter.14.cloned.1.call-start = ((), (), s32[]{:S(2)}) async-start(), calls=%async_computation.15 | async-start | bytes 7864320 | tf_op jit(solution)/shard_map/reduce_scatter | solution.py:139
  417.9 50.5 %copy-start.4 = (f32[512,768]{1,0:T(8,128)S(1)}, f32[512,768]{1,0:T(8,128)}, u32[]{:S(2)}) copy-start(f32[512,768]{1,0:T(8,128)} %copy-done.3) | copy-start | bytes 4718596
  417.9 148.0 %all-gather.20.cloned.1.call-start = ((), (), s32[]{:S(2)}) async-start(), calls=%async_computation.18 | async-start | bytes 3932160 | tf_op jit(solution)/shard_map/all_gather | solution.py:171
  468.5 3.4 copy-start.11
  537.3 381.6 %reduce-scatter.18.cloned.1.call-start = ((), (), s32[]{:S(2)}) async-start(), calls=%async_computation.19 | async-start | bytes 7864320 | tf_op jit(solution)/shard_map/reduce_scatter | solution.py:221
  569.9 3.4 copy-start.8
  576.7 4.5 copy-start
  645.3 4.5 copy-start
  714.4 4.5 copy-start
  783.4 4.5 copy-start
  859.9 125.5 %reduce-scatter.28.cloned.1.call-start = ((), (), s32[]{:S(2)}) async-start(), calls=%async_computation.24 | async-start | bytes 884736
  865.1 193.3 %reduce-scatter.24.cloned.1.call-start = ((), (), s32[]{:S(2)}) async-start(), calls=%async_computation.22 | async-start | bytes 2654208 | tf_op jit(solution)/shard_map/reduce_scatter | solution.py:240
  872.6 258.6 %reduce-scatter.26.cloned.1.call-start = ((), (), s32[]{:S(2)}) async-start(), calls=%async_computation.23 | async-start | bytes 2654208 | tf_op jit(solution)/shard_map/reduce_scatter | solution.py:241
  879.7 324.4 %reduce-scatter.22.cloned.1.call-start = ((), (), s32[]{:S(2)}) async-start(), calls=%async_computation.21 | async-start | bytes 2654208 | tf_op jit(solution)/shard_map/reduce_scatter | solution.py:238
  887.6 31.3 %copy-start.2 = (f32[1,512,768]{2,1,0:T(8,128)S(1)}, f32[1,512,768]{2,1,0:T(8,128)}, u32[]{:S(2)}) copy-start(f32[1,512,768]{2,1,0:T(8,128)} %param.16) | copy-start | bytes 4718596
  887.6 31.3 %copy-start.31 = (f32[768]{0:T(1024)S(1)}, f32[768]{0:T(1024)}, u32[]{:S(2)}) copy-start(f32[768]{0:T(1024)} %copy-done.30) | copy-start | bytes 9220
  887.6 31.3 %copy-start.33 = (f32[512]{0:T(512)S(1)}, f32[512]{0:T(512)}, u32[]{:S(2)}) copy-start(f32[512]{0:T(512)} %copy-done.32) | copy-start | bytes 6148
  887.6 31.3 %copy-start.35 = (f32[512]{0:T(512)S(1)}, f32[512]{0:T(512)}, u32[]{:S(2)}) copy-start(f32[512]{0:T(512)} %copy-done.34) | copy-start | bytes 6148
  887.6 33.4 %copy-start.46 = (f32[768]{0:T(1024)S(1)}, f32[768]{0:T(1024)}, u32[]{:S(2)}) copy-start(f32[768]{0:T(1024)} %get-tuple-element.272) | copy-start | bytes 9220
  887.6 33.4 %copy-start.44 = (f32[768]{0:T(1024)S(1)}, f32[768]{0:T(1024)}, u32[]{:S(2)}) copy-start(f32[768]{0:T(1024)} %get-tuple-element.207) | copy-start | bytes 9220
  887.6 33.4 %copy-start.43 = (f32[768]{0:T(1024)S(1)}, f32[768]{0:T(1024)}, u32[]{:S(2)}) copy-start(f32[768]{0:T(1024)} %get-tuple-element.201) | copy-start | bytes 9220
  887.7 33.4 %copy-start.45 = (f32[768]{0:T(1024)S(1)}, f32[768]{0:T(1024)}, u32[]{:S(2)}) copy-start(f32[768]{0:T(1024)} %get-tuple-element.206) | copy-start | bytes 9220
  887.7 33.4 %copy-start.47 = (f32[768]{0:T(1024)S(1)}, f32[768]{0:T(1024)}, u32[]{:S(2)}) copy-start(f32[768]{0:T(1024)} %get-tuple-element.205) | copy-start | bytes 9220
  887.7 389.1 %reduce-scatter.20.cloned.1.call-start = ((), (), s32[]{:S(2)}) async-start(), calls=%async_computation.20 | async-start | bytes 2654208 | tf_op jit(solution)/shard_map/reduce_scatter | solution.py:242
  931.4 55.6 %copy-start.48 = (f32[768]{0:T(1024)S(1)}, f32[768]{0:T(1024)}, u32[]{:S(2)}) copy-start(f32[768]{0:T(1024)} %get-tuple-element.248) | copy-start | bytes 9220
  931.4 91.5 %copy-start.39 = (f32[512]{0:T(512)S(1)}, f32[512]{0:T(512)}, u32[]{:S(2)}) copy-start(f32[512]{0:T(512)} %copy-done.38) | copy-start | bytes 6148
  931.4 91.5 %copy-start.10 = (f32[512,768]{1,0:T(8,128)S(1)}, f32[512,768]{1,0:T(8,128)}, u32[]{:S(2)}) copy-start(f32[512,768]{1,0:T(8,128)} %reduce-scatter.18.cloned.1.call-done) | copy-start | bytes 4718596
  (37 other events, 53.9 us)
Sparse Core Ops, SparseCore 0:
  10.8 43.8 all-gather.7
  58.3 27.1 all-gather.9
  187.5 58.3 reduce-scatter.11
  248.5 41.0 all-gather.13
  291.6 27.1 all-gather.11
  321.5 41.1 all-gather.15
  364.2 27.1 all-gather.17
  409.6 58.8 reduce-scatter.15
  471.0 58.8 reduce-scatter.13
  537.4 28.4 all-gather.19
  860.0 58.8 reduce-scatter.17
  922.1 63.2 reduce-scatter.27
  989.4 68.9 reduce-scatter.23
  1062.3 68.7 reduce-scatter.25
  1135.0 69.0 reduce-scatter.21
  1208.0 68.7 reduce-scatter.19
where the time goes:
time: 1290 us; the launch traced here: 1280 us
  waiting for transfers between devices  696 us (54%)
  matrix products  330 us (26%)
  blocking collectives  113 us (9%)
  local copies, waits for them, and re-layouts  73.7 us (6%)
  other arithmetic  54.2 us (4%)
  between operations  15.7 us (1%)
    dot_general x4, matrix products, backward_block(): jnp.einsum('hqk,qhd->khd', score_back, query_block, preferred_element_typ...  88.3 us
    dot_general x4, matrix products, backward_block(): jnp.einsum('hqk,khd->qhd', score_back, key_rows, preferred_element_type=j...  86.7 us
    reduce_scatter x1, waiting for transfers between devices, shards(): lax.psum_scatter(in_grad, ('dp', 'row'), scatter_dimension=0, tiled=True)  73 us
    reduce_scatter x1, waiting for transfers between devices, shards(): lax.psum_scatter(condition_grad, ('dp', 'row'), scatter_dimension=1, tile...  72.7 us
    reduce_scatter x1, waiting for transfers between devices, shards(): lax.psum_scatter(down_grad, ('dp', 'row'), scatter_dimension=1, tiled=True)  72.7 us
    reduce_scatter x1, waiting for transfers between devices, shards(): lax.psum_scatter(jnp.dot(piece, out_full, preferred_element_type=jnp.floa...  56.8 us
    reduce_scatter x1, waiting for transfers between devices, shards(): lax.psum_scatter(jnp.dot(piece, down_full, preferred_element_type=jnp.flo...  55.6 us
    unnamed x17, waiting for transfers between devices  51.2 us
  transfers between devices with their start and end apart: 16, of which 15 were waited for; matrix products, arithmetic and copies ran while one was open for 5% of the time, Pallas kernels for 0%

commit v1 on v0

v1 whole, which is shorter than its diff:
```python
import functools
import math

import jax
import jax.numpy as jnp
import numpy as np
from jax import lax
from jax.experimental import pallas as pl
from jax.experimental.pallas import tpu as pltpu
from jax.sharding import PartitionSpec as P

HD = 64
AUG = 128
EPSILON = 1e-06
MASKED = -1e30
CUBIC = 0.044715
SLOPE = math.sqrt(2.0 / math.pi)
SCALE = 1.0 / math.sqrt(HD)
UNIT = SCALE * math.log2(math.e)
F32 = jnp.float32
BF16 = jnp.bfloat16
VMEM_LIMIT = 60 << 20


def layer_norm(values):
    center = values - jnp.mean(values, axis=-1, keepdims=True)
    spread = jnp.mean(center * center, axis=-1, keepdims=True)
    return center * lax.rsqrt(spread + EPSILON)


def norm_shift(values, shift, scale):
    return layer_norm(values) * (1.0 + scale) + shift


def gelu_tanh(values):
    return 0.5 * values * (1.0 + jnp.tanh(SLOPE * (values + CUBIC * values * values * values)))


def rotary_tables(length):
    half = HD // 2
    exponent = np.arange(half, dtype=np.float32) * np.float32(2.0 / HD)
    frequency = np.exp(np.float32(-math.log(10000.0)) * exponent).astype(np.float32)
    angle = frequency[:, None] * np.arange(length, dtype=np.float32)[None, :]
    angle = angle.astype(np.float32).astype(np.float64)
    return np.cos(angle).astype(np.float32), np.sin(angle).astype(np.float32)


def contract(left, right, left_axis, right_axis):
    return lax.dot_general(
        left,
        right,
        (((left_axis,), (right_axis,)), ((), ())),
        preferred_element_type=F32,
    )


def block_at(index, size):
    return pl.ds(pl.multiple_of(index * size, size), size)


def split_three(values):
    high = values.astype(BF16)
    rest = values - high.astype(F32)
    middle = rest.astype(BF16)
    low = (rest - middle.astype(F32)).astype(BF16)
    return high.astype(F32), middle.astype(F32), low.astype(F32)


def augment(rows, extras):
    n = rows.shape[1]
    extras = [jnp.broadcast_to(e, (1, n)) for e in extras]
    pad = jnp.zeros((AUG - HD - len(extras), n), F32)
    return jnp.concatenate([rows] + extras + [pad], axis=0)


def project_rotate(heads, size, normed, weight_t, cosine, sine, bias, qkv, query, key):
    length = normed.shape[0]
    half = HD // 2

    def step(i, _):
        here = block_at(i, size)
        both = contract(weight_t[...], normed[here, :], 1, 1)
        c, s = cosine[:, here], sine[:, here]
        one = jnp.ones((1, size), F32)
        for h in range(heads):
            for t in range(3):
                at = (t * heads + h) * HD
                if t == 2:
                    qkv[t * heads + h, :, here] = both[at : at + HD].astype(BF16)
                    continue
                a, b = both[at : at + half], both[at + half : at + HD]
                turned = jnp.concatenate([a * c - b * s, b * c + a * s], axis=0)
                qkv[t * heads + h, :, here] = turned.astype(BF16)
                if t == 0:
                    query[h, :, here] = augment(turned, [one]).astype(BF16)
                else:
                    wide = augment(turned, [bias[:, here], one, one, one])
                    key[h, here, :] = wide.T.astype(BF16)
        return 0

    lax.fori_loop(0, length // size, step, 0)


def attend_block(heads, here, query, key, value_t, mixed_t, log_total):
    scores = [contract(key[h], query[h, :, here], 1, 0) for h in range(heads)]
    for h in range(heads):
        top = jnp.max(scores[h], axis=0, keepdims=True)
        weights = jnp.exp2((scores[h] - top) * UNIT)
        total = jnp.sum(weights, axis=0, keepdims=True)
        out = contract(value_t[h], weights.astype(BF16), 1, 0) * (1.0 / total)
        mixed_t[h, :, here] = out.astype(BF16)
        log_total[h, :, here] = top * UNIT + jnp.log2(total)


def attention_forward_kernel(
    heads, normed, weight, cosine, sine, bias, qkv, mixed_t, log_total, weight_t, query, key
):
    length = normed.shape[0]
    weight_t[...] = weight[...].astype(F32).T.astype(BF16)
    size = min(512, length)
    project_rotate(heads, size, normed, weight_t, cosine, sine, bias, qkv, query, key)

    def step(i, _):
        attend_block(
            heads, block_at(i, size), query, key, qkv.at[pl.ds(2 * heads, heads)], mixed_t, log_total
        )
        return 0

    lax.fori_loop(0, length // size, step, 0)


def attention_forward(heads, normed, weight, cosine, sine, bias):
    length, width = normed.shape
    vmem = pl.BlockSpec(memory_space=pltpu.VMEM)
    return pl.pallas_call(
        functools.partial(attention_forward_kernel, heads),
        out_shape=[
            jax.ShapeDtypeStruct((3 * heads, HD, length), BF16),
            jax.ShapeDtypeStruct((heads, HD, length), BF16),
            jax.ShapeDtypeStruct((heads, 1, length), F32),
        ],
        in_specs=[vmem] * 5,
        out_specs=[vmem] * 3,
        scratch_shapes=[
            pltpu.VMEM((3 * heads * HD, width), BF16),
            pltpu.VMEM((heads, AUG, length), BF16),
            pltpu.VMEM((heads, length, AUG), BF16),
        ],
        compiler_params=pltpu.CompilerParams(vmem_limit_bytes=VMEM_LIMIT),
    )(normed, weight, cosine, sine, bias)


def prepare_backward(heads, h, size, length, qkv, bias, log_total, mixed_t, back_t, query, key, value, back):
    def step(i, _):
        here = block_at(i, size)
        one = jnp.ones((1, size), F32)
        zero = jnp.zeros((1, size), F32)
        logs = split_three(log_total[h, :, here] * (-1.0 / UNIT))
        query[h, :, here] = augment(qkv[h, :, here].astype(F32), [one, *logs]).astype(BF16)
        keys = augment(qkv[heads + h, :, here].astype(F32), [bias[:, here], one, one, one])
        key[h, here, :] = keys.T.astype(BF16)
        values = augment(qkv[2 * heads + h, :, here].astype(F32), [zero, one, one, one])
        value[h, here, :] = values.T.astype(BF16)
        grad = back_t[h, :, here].astype(F32)
        center = jnp.sum(grad * mixed_t[h, :, here].astype(F32), axis=0, keepdims=True)
        back[h, :, here] = augment(grad, [zero, *split_three(-center)]).astype(BF16)
        return 0

    lax.fori_loop(0, length // size, step, 0)


def attention_backward_kernel(
    heads, qkv, bias, log_total, mixed_t, back_t, cosine, sine, out, query, key, value, back, key_sum, value_sum
):
    length = qkv.shape[2]
    size = min(512, length)
    half = HD // 2

    def turn_back(rows, here):
        c, s = cosine[:, here], sine[:, here]
        a, b = rows[:half], rows[half:]
        return jnp.concatenate([a * c + b * s, b * c - a * s], axis=0)

    for h in range(heads):
        prepare_backward(heads, h, size, length, qkv, bias, log_total, mixed_t, back_t, query, key, value, back)
    key_sum[...] = jnp.zeros_like(key_sum)
    value_sum[...] = jnp.zeros_like(value_sum)

    def step(i, _):
        here = block_at(i, size)
        for h in range(heads):
            q, d = query[h, :, here], back[h, :, here]
            weights = jnp.exp2(contract(key[h], q, 1, 0) * UNIT)
            grads = (weights * contract(value[h], d, 1, 0)).astype(BF16)
            value_sum[h] += contract(d[:HD], weights.astype(BF16), 1, 1)
            key_sum[h] += contract(q[:HD], grads, 1, 1)
            query_back = contract(qkv[heads + h], grads, 1, 0) * SCALE
            out[h, :, here] = turn_back(query_back, here).astype(BF16)
        return 0

    lax.fori_loop(0, length // size, step, 0)

    def finish(i, _):
        here = block_at(i, size)
        for h in range(heads):
            out[heads + h, :, here] = turn_back(key_sum[h, :, here] * SCALE, here).astype(BF16)
            out[2 * heads + h, :, here] = value_sum[h, :, here].astype(BF16)
        return 0

    lax.fori_loop(0, length // size, finish, 0)


def attention_backward(heads, qkv, bias, log_total, mixed_t, back_t, cosine, sine):
    length = qkv.shape[2]
    vmem = pl.BlockSpec(memory_space=pltpu.VMEM)
    return pl.pallas_call(
        functools.partial(attention_backward_kernel, heads),
        out_shape=jax.ShapeDtypeStruct((3 * heads, HD, length), BF16),
        in_specs=[vmem] * 7,
        out_specs=vmem,
        scratch_shapes=[
            pltpu.VMEM((heads, AUG, length), BF16),
            pltpu.VMEM((heads, length, AUG), BF16),
            pltpu.VMEM((heads, length, AUG), BF16),
            pltpu.VMEM((heads, AUG, length), BF16),
            pltpu.VMEM((heads, HD, length), F32),
            pltpu.VMEM((heads, HD, length), F32),
        ],
        compiler_params=pltpu.CompilerParams(vmem_limit_bytes=VMEM_LIMIT),
    )(qkv, bias, log_total, mixed_t, back_t, cosine, sine)


def shards(
    tokens,
    condition,
    lengths,
    condition_weight,
    condition_bias,
    attention_in,
    attention_out,
    up_weight,
    up_bias,
    down_weight,
    down_bias,
    cotangent,
):
    columns = lax.axis_size("col")
    column_index = lax.axis_index("col")
    rows = tokens.shape[1]
    width = tokens.shape[2]
    length_all = rows * columns
    local_width = attention_in.shape[2]
    heads = local_width // HD
    group = ("dp", "row")
    in_full, out_full, up_full, down_full = (
        lax.all_gather(attention_in.astype(BF16), group, axis=0, tiled=True),
        lax.all_gather(attention_out.astype(BF16), group, axis=1, tiled=True),
        lax.all_gather(up_weight.astype(BF16), group, axis=0, tiled=True),
        lax.all_gather(down_weight.astype(BF16), group, axis=1, tiled=True),
    )
    condition_low = condition.astype(BF16)
    condition_all = lax.all_gather(condition_low, group, axis=0, tiled=True)
    weight_low = condition_weight.astype(BF16)
    pieces = jnp.dot(condition_all, weight_low, preferred_element_type=F32)
    modulation = lax.all_to_all(pieces, group, 0, 0, tiled=True).reshape(-1) + condition_bias
    parts = modulation.reshape(6, width)
    own_rows = tokens[0]
    length = lengths[0]
    position = column_index * rows + jnp.arange(rows)
    valid = (position < length).astype(F32)
    bias = jnp.where(jnp.arange(length_all) < length, 0.0, MASKED).astype(F32)[None]
    cosine, sine = (jnp.asarray(table) for table in rotary_tables(length_all))
    normed, first_pull = jax.vjp(norm_shift, own_rows, parts[0], parts[1])
    normed_all = lax.all_gather(normed.astype(BF16), "col", axis=0, tiled=True)
    qkv, mixed_t, log_total = attention_forward(
        heads, normed_all, in_full.reshape(width, 3 * local_width), cosine, sine, bias
    )
    mixed_rows = mixed_t.reshape(local_width, length_all)
    attention = lax.psum_scatter(
        jnp.einsum("cs,cd->sd", mixed_rows, out_full, preferred_element_type=F32).astype(BF16),
        "col",
        scatter_dimension=0,
        tiled=True,
    ).astype(F32)
    middle = own_rows + parts[2] * attention
    second, second_pull = jax.vjp(norm_shift, middle, parts[3], parts[4])
    second_low = second.astype(BF16)
    hidden_cols = up_full.shape[1]
    second_all = lax.all_gather(second_low, "col", axis=0, tiled=True)
    bias_part = lax.dynamic_slice_in_dim(up_bias, column_index * hidden_cols, hidden_cols)
    before = jnp.dot(second_all, up_full, preferred_element_type=F32) + bias_part
    hidden, gelu_pull = jax.vjp(gelu_tanh, before)
    hidden_low = hidden.astype(BF16)
    feed = lax.psum_scatter(
        jnp.dot(hidden_low, down_full, preferred_element_type=F32).astype(BF16),
        "col",
        scatter_dimension=0,
        tiled=True,
    ).astype(F32)
    result = middle + parts[5] * (feed + down_bias)
    incoming = cotangent[0] * valid[:, None]
    down_bias_part = jnp.sum(parts[5] * incoming, axis=0)
    gate_feed = jnp.sum(incoming * (feed + down_bias), axis=0)
    feed_back = (parts[5] * incoming).astype(BF16)
    feed_back_all = lax.all_gather(feed_back, "col", axis=0, tiled=True)
    hidden_back = jnp.einsum("sd,fd->sf", feed_back_all, down_full, preferred_element_type=F32)
    down_grad = jnp.einsum("sf,sd->fd", hidden_low, feed_back_all, preferred_element_type=F32)
    before_back = gelu_pull(hidden_back)[0].astype(BF16)
    up_grad = jnp.einsum("sd,sf->df", second_all, before_back, preferred_element_type=F32)
    up_bias_part = jnp.sum(before_back.astype(F32), axis=0)
    second_back = lax.psum_scatter(
        jnp.einsum("sf,df->sd", before_back, up_full, preferred_element_type=F32).astype(BF16),
        "col",
        scatter_dimension=0,
        tiled=True,
    ).astype(F32)
    middle_part, shift_feed, scale_feed = second_pull(second_back)
    middle_back = incoming + middle_part
    gate_attention = jnp.sum(middle_back * attention, axis=0)
    attention_back = (parts[2] * middle_back).astype(BF16)
    attention_back_all = lax.all_gather(attention_back, "col", axis=0, tiled=True)
    out_grad = jnp.einsum("cs,sd->cd", mixed_rows, attention_back_all, preferred_element_type=F32)
    mixed_back = jnp.einsum("sd,cd->cs", attention_back_all, out_full, preferred_element_type=F32)
    projected_back = attention_backward(
        heads,
        qkv,
        bias,
        log_total,
        mixed_t,
        mixed_back.astype(BF16).reshape(heads, HD, length_all),
        cosine,
        sine,
    ).reshape(3, local_width, length_all)
    in_grad = jnp.einsum("sd,tes->dte", normed_all, projected_back, preferred_element_type=F32)
    normed_back = lax.psum_scatter(
        jnp.einsum("tes,dte->sd", projected_back, in_full, preferred_element_type=F32).astype(BF16),
        "col",
        scatter_dimension=0,
        tiled=True,
    ).astype(F32)
    rows_part, shift_attention, scale_attention = first_pull(normed_back)
    tokens_back = middle_back + rows_part
    modulation_part = jnp.concatenate(
        [shift_attention, scale_attention, gate_attention, shift_feed, scale_feed, gate_feed]
    )
    modulation_back, down_bias_column = lax.psum((modulation_part, down_bias_part), "col")
    count = lax.axis_size(group)
    spread = modulation_back.reshape(count, -1)
    mine = lax.all_to_all(spread, group, 0, 0, tiled=True)
    highest = lax.Precision.HIGHEST
    condition_grad = jnp.einsum("bc,bm->cm", condition_all.astype(F32), mine, precision=highest)
    condition_back = lax.psum_scatter(
        jnp.einsum("bm,cm->bc", mine, weight_low.astype(F32), precision=highest),
        group,
        scatter_dimension=0,
        tiled=True,
    )
    in_grad, out_grad, up_grad, down_grad = (
        lax.psum_scatter(in_grad.astype(BF16), group, scatter_dimension=0, tiled=True).astype(F32),
        lax.psum_scatter(out_grad.astype(BF16), group, scatter_dimension=1, tiled=True).astype(F32),
        lax.psum_scatter(up_grad.astype(BF16), group, scatter_dimension=0, tiled=True).astype(F32),
        lax.psum_scatter(down_grad.astype(BF16), group, scatter_dimension=1, tiled=True).astype(F32),
    )
    bias_grad, up_bias_grad, down_bias_grad = lax.psum(
        (modulation_back, up_bias_part, down_bias_column), group
    )
    return (
        result[None],
        tokens_back[None],
        condition_back,
        condition_grad,
        bias_grad,
        in_grad,
        out_grad,
        up_grad,
        up_bias_grad,
        down_grad,
        down_bias_grad,
    )


def solution(mesh):
    in_specs = (
        P(("dp", "row"), "col", None),
        P(("dp", "row"), None),
        P(("dp", "row")),
        P(None, ("dp", "row")),
        P(),
        P(("dp", "row"), None, "col"),
        P("col", ("dp", "row")),
        P(("dp", "row"), "col"),
        P(),
        P("col", ("dp", "row")),
        P(),
        P(("dp", "row"), "col", None),
    )
    out_specs = (
        P(("dp", "row"), "col", None),
        P(("dp", "row"), "col", None),
        P(("dp", "row"), None),
        P(None, ("dp", "row")),
        P(),
        P(("dp", "row"), None, "col"),
        P("col", ("dp", "row")),
        P(("dp", "row"), "col"),
        P("col"),
        P("col", ("dp", "row")),
        P(),
    )
    return jax.shard_map(shards, mesh=mesh, in_specs=in_specs, out_specs=out_specs, check_vma=False)
```

time: 1290 us -> 786 us (0.61)
  matrix products: 330 us -> 70.9 us
  waiting for transfers between devices: 696 us -> 437 us
  Pallas kernels: 0 us -> 61.6 us
  local copies, waits for them, and re-layouts: 73.7 us -> 16.8 us
  other arithmetic: 54.2 us -> 33.6 us
  blocking collectives: 113 us -> 131 us
    dot_general x38 -> x12, matrix products: 302 us -> 52.5 us  [the longest x1 8.8 us: shards(): jnp.dot(hidden_low, down_full, preferred_element_type=F32).astype(BF16)]
    reduce_scatter x8 -> x7, waiting for transfers between devices: 444 us -> 260 us  [the longest x1 65.6 us: shards(): lax.psum_scatter(in_grad.astype(BF16), group, scatter_dimension=0, tiled=...]
    all_gather x4 -> x3, waiting for transfers between devices: 114 us -> 36.6 us  [the longest x1 36.6 us: shards(): lax.all_gather(down_weight.astype(BF16), group, axis=1, tiled=True)]
    pallas_call x0 -> x2, Pallas kernels: none -> 61.6 us  [the longest x1 38.6 us: attention_backward(): pl.pallas_call(functools.partial(attention_backward_kernel, heads), out_s...]
    dynamic_update_slice x8 -> x0, local copies, waits for them, and re-layouts: 36.1 us -> none  [shards(): mixed, log_total = lax.map(forward_block, query_blocks)]
    psum x1 -> x0, blocking collectives: 35.8 us -> none  [shards(): lax.psum((modulation_back, up_bias_part, down_bias_column), ('dp', 'row'))]
    unnamed x0 -> x1, blocking collectives: none -> 34.4 us
    all_gather x2 -> x3, blocking collectives: 67 us -> 86.7 us  [the longest x1 33.4 us: shards(): lax.all_gather(attention_in.astype(BF16), group, axis=0, tiled=True)]
  transfers between devices with their start and end apart: 16 -> 16, of which waited for: 15 -> 13; matrix products, arithmetic and copies ran while one was open for 5% -> 8% of each run, Pallas kernels for 0% -> 5%
where the time goes in v1:
time: 786 us; the launch traced here: 779 us
  waiting for transfers between devices  437 us (56%)
  blocking collectives  131 us (17%)
  matrix products  70.9 us (9%)
  Pallas kernels  61.6 us (8%)
  other arithmetic  33.6 us (4%)
  local copies, waits for them, and re-layouts  16.8 us (2%)
  between operations  16.8 us (2%)
  starting transfers between devices  10.7 us (1%)
    reduce_scatter x1, waiting for transfers between devices, shards(): lax.psum_scatter(in_grad.astype(BF16), group, scatter_dimension=0, tiled=...  65.6 us
    unnamed x15, waiting for transfers between devices  62.9 us
    reduce_scatter x1, waiting for transfers between devices, shards(): lax.psum_scatter(up_grad.astype(BF16), group, scatter_dimension=0, tiled=...  49.3 us
    pallas_call x1, Pallas kernels, attention_backward(): pl.pallas_call(functools.partial(attention_backward_kernel, heads), out_s...  38.6 us
    reduce_scatter x1, waiting for transfers between devices, shards(): lax.psum_scatter(jnp.einsum('tes,dte->sd', projected_back, in_full, prefe...  37.6 us
    reduce_scatter x1, waiting for transfers between devices, shards(): lax.psum_scatter(jnp.einsum('sf,df->sd', before_back, up_full, preferred_...  37.6 us
    all_gather x1, waiting for transfers between devices, shards(): lax.all_gather(down_weight.astype(BF16), group, axis=1, tiled=True)  36.6 us
    reduce_scatter x1, waiting for transfers between devices, shards(): lax.psum_scatter(jnp.dot(hidden_low, down_full, preferred_element_type=F3...  35.5 us
  transfers between devices with their start and end apart: 16, of which 13 were waited for; matrix products, arithmetic and copies ran while one was open for 8% of the time, Pallas kernels for 5%

profile of v1, /device:TPU:0, one launch (start us, length us, event | category | flops | bytes accessed | tf_op | source)
XLA Modules:
  0.0 778.7 jit_solution(12370271724761381175)
XLA Ops:
  8.8 22.3 %all-gather = bf16[8,1,128]{2,1,0:T(2,128)(2,1)S(1)} all-gather(bf16[1,1,128]{2,1,0:T(2,128)(2,1)S(1)} %convert_bitcast_fusion), channel_id=1, replica_groups=mesh['dp'=4,'row'=2,'col'=4] {'dp','row'}, dimensions={0}, use_global_device_ids=true | all-gather | bytes 2304 | tf_op jit(solution)/shard_map/all_gather | solution.py:262
  33.4 3.3 all-to-all-start
  36.8 1.6 reduce_sum.140
  39.3 4.0 all-to-all-done
  46.0 33.4 %all_gather.29 = bf16[768,3,192]{2,0,1:T(8,128)(2,1)S(1)} all-gather(bf16[96,3,192]{2,0,1:T(8,128)(2,1)S(1)} %convert_element_type.105), channel_id=1, replica_groups=mesh['dp'=4,'row'=2,'col'=4] {'dp','row'}, dimensions={0}, use_global_device_ids=true | all-gather | bytes 995328 | tf_op jit(solution)/shard_map/all_gather | solution.py:256
  79.4 1.4 copy.29
  80.8 2.2 copy.30.weight
  83.1 31.0 %all_gather.30 = bf16[192,768]{0,1:T(8,128)(2,1)S(1)} all-gather(bf16[192,96]{0,1:T(8,128)(2,1)S(1)} %copy.31), channel_id=1, replica_groups=mesh['dp'=4,'row'=2,'col'=4] {'dp','row'}, dimensions={1}, use_global_device_ids=true | all-gather | bytes 331776 | tf_op jit(solution)/shard_map/all_gather | solution.py:257
  114.8 23.0 %shard_map.221 = (bf16[9,64,2048]{2,1,0:T(8,128)(2,1)}, bf16[3,64,2048]{2,1,0:T(8,128)(2,1)}, f32[3,1,2048]{2,1,0:T(1,128)}) custom-call(bf16[2048,768]{1,0:T(8,128)(2,1)} %all-gather.8.cloned.1.call-done.normed, bf16[768,576]{1,0:T(8,128)(2,1)} %copy.30.weight, f32[32,2048]{1,0:T(8,128)} %constant.43.clone.cosine, f32[32,2048]{1,0:T(8,128)} %constant.44.clone.sine, ...), custom_call_target="tpu_custom_call" | custom-call | tf_op jit(solution)/shard_map/pallas_call | solution.py:135
  137.8 3.8 convolution_convert_fusion.2
  143.3 34.1 %reduce-scatter.11.cloned.1.call-done = bf16[512,768]{1,0:T(8,128)(2,1)} async-done(((bf16[2048,768]{1,0:T(8,128)(2,1)}), bf16[512,768]{1,0:T(8,128)(2,1)}) %reduce-scatter.11.cloned.1.call-update) | async-done | bytes 786448 | tf_op jit(solution)/shard_map/reduce_scatter | solution.py:279
  177.5 1.4 fusion.38
  181.6 1.6 convert_element_type.112
  185.2 27.6 %all-gather.10.cloned.1.call-done = bf16[2048,768]{1,0:T(8,128)(2,1)} async-done(((bf16[512,768]{1,0:T(8,128)(2,1)}), bf16[2048,768]{1,0:T(8,128)(2,1)}) %all-gather.10.cloned.1.call-update) | async-done | bytes 3145744 | tf_op jit(solution)/shard_map/all_gather | solution.py:289
  212.7 7.5 fusion.41
  220.2 36.6 %all-gather.14.cloned.1.call-done = bf16[768,768]{0,1:T(8,128)(2,1)} async-done(((bf16[768,96]{0,1:T(8,128)(2,1)}), bf16[768,768]{0,1:T(8,128)(2,1)}) %all-gather.14.cloned.1.call-update) | async-done | bytes 1179664 | tf_op jit(solution)/shard_map/all_gather | solution.py:259
  256.8 8.8 %convolution_convert_fusion.1 = bf16[2048,768]{1,0:T(8,128)(2,1)} fusion(bf16[768,768]{0,1:T(8,128)(2,1)} %all-gather.14.cloned.1.call-done, f32[2048,768]{1,0:T(8,128)} %fusion.41, f32[768]{0:T(1024)} %dynamic_slice.3), kind=kOutput, calls=%fused_computation.14 | convolution fusion | flops 2433220608 | bytes 10619904 | tf_op jit(solution)/shard_map/dot_general | solution.py:295
  266.3 35.5 %reduce-scatter.13.cloned.1.call-done = bf16[512,768]{1,0:T(8,128)(2,1)} async-done(((bf16[2048,768]{1,0:T(8,128)(2,1)}), bf16[512,768]{1,0:T(8,128)(2,1)}) %reduce-scatter.13.cloned.1.call-update) | async-done | bytes 786448 | tf_op jit(solution)/shard_map/reduce_scatter | solution.py:294
  301.8 3.5 multiply_reduce_fusion.3
  305.4 28.6 %all-gather.16.cloned.1.call-done = bf16[2048,768]{1,0:T(8,128)(2,1)} async-done(((bf16[512,768]{1,0:T(8,128)(2,1)}), bf16[2048,768]{1,0:T(8,128)(2,1)}) %all-gather.16.cloned.1.call-update) | async-done | bytes 3145744 | tf_op jit(solution)/shard_map/all_gather | solution.py:305
  334.1 10.4 %convert_reduce_fusion = (f32[768]{0:T(1024)}, bf16[2048,768]{1,0:T(8,128)(2,1)S(1)}) fusion(f32[2048,768]{1,0:T(8,128)} %fusion.41, f32[768]{0:T(1024)} %dynamic_slice.3, bf16[2048,768]{1,0:T(8,128)(2,1)} %all-gather.16.cloned.1.call-done, bf16[768,768]{0,1:T(8,128)(2,1)} %all-gather.14.cloned.1.call-done), kind=kOutput, calls=%fused_computation.11 | convolution fusion | flops 2458385664 | bytes 13768704 | tf_op jit(solution)/shard_map/sd,fd->sf/dot_general | solution.py:306
  344.5 1.6 copy-done.40
  346.1 4.0 convolution_convert_fusion
  350.4 37.6 %reduce-scatter.15.cloned.1.call-done = bf16[512,768]{1,0:T(8,128)(2,1)} async-done(((bf16[2048,768]{1,0:T(8,128)(2,1)}), bf16[512,768]{1,0:T(8,128)(2,1)}) %reduce-scatter.15.cloned.1.call-update) | async-done | bytes 786448 | tf_op jit(solution)/shard_map/reduce_scatter | solution.py:311
  388.0 1.6 fusion.13
  390.5 2.1 fusion.16
  392.7 2.6 fusion.15
  397.5 8.1 %convolution_convert_fusion.4 = bf16[768,768]{0,1:T(8,128)(2,1)} fusion(bf16[2048,768]{1,0:T(8,128)(2,1)} %all-gather.16.cloned.1.call-done, f32[2048,768]{1,0:T(8,128)} %fusion.41, f32[768]{0:T(1024)S(1)} %copy-done.36), kind=kOutput, calls=%fused_computation.52 | convolution fusion | flops 2432237568 | bytes 10619904 | tf_op jit(solution)/shard_map/sf,sd->fd/dot_general | solution.py:307
  405.7 6.7 convolution_convert_fusion.5
  412.5 13.6 %all-gather.18.cloned.1.call-done = bf16[2048,768]{1,0:T(8,128)(2,1)} async-done(((bf16[512,768]{1,0:T(8,128)(2,1)}), bf16[2048,768]{1,0:T(8,128)(2,1)}) %all-gather.18.cloned.1.call-update) | async-done | bytes 3145744 | tf_op jit(solution)/shard_map/all_gather | solution.py:321
  426.1 2.7 convolution_convert_fusion.6
  430.1 4.0 convolution_convert_fusion.3
  434.1 38.6 %shard_map.222 = bf16[9,64,2048]{2,1,0:T(8,128)(2,1)} custom-call(bf16[9,64,2048]{2,1,0:T(8,128)(2,1)} %get-tuple-element.15.qkv, f32[1,2048]{1,0:T(1,128)} %compare_select_fusion.bias, f32[3,1,2048]{2,1,0:T(1,128)} %get-tuple-element.16.log_total, bf16[3,64,2048]{2,1,0:T(8,128)(2,1)} %get-tuple-element.14.mixed_t, bf16[3,64,2048]{2,1,0:T(8,128)(2,1)} %bitcast.90, ...), custom_call_target="tpu_custom_call" | custom-call | tf_op jit(solution)/shard_map/pallas_call | solution.py:216
  472.7 6.4 fusion.18
  479.4 6.1 bitcast_convert_fusion
  486.7 1.6 convert_element_type.133
  488.4 49.3 %reduce-scatter.21.cloned.1.call-done = bf16[96,768]{1,0:T(8,128)(2,1)} async-done(((bf16[768,768]{1,0:T(8,128)(2,1)}), bf16[96,768]{1,0:T(8,128)(2,1)}) %reduce-scatter.21.cloned.1.call-update) | async-done | bytes 147472 | tf_op jit(solution)/shard_map/reduce_scatter | solution.py:361
  537.7 1.6 convert_element_type.130
  539.3 62.7 %reduce-scatter.25.cloned.1.call-done = bf16[96,192]{1,0:T(8,128)(2,1)} async-done(((bf16[768,192]{1,0:T(8,128)(2,1)}), bf16[96,192]{1,0:T(8,128)(2,1)}) %reduce-scatter.25.cloned.1.call-update) | async-done | bytes 36880
  603.6 65.6 %reduce-scatter.19.cloned.1.call-done = bf16[96,3,192]{2,0,1:T(8,128)(2,1)} async-done(((bf16[768,3,192]{2,0,1:T(8,128)(2,1)}), bf16[96,3,192]{2,0,1:T(8,128)(2,1)}) %reduce-scatter.19.cloned.1.call-update) | async-done | bytes 110608 | tf_op jit(solution)/shard_map/reduce_scatter | solution.py:359
  669.2 1.6 convert_element_type.126
  670.9 37.6 %reduce-scatter.17.cloned.1.call-done = bf16[512,768]{1,0:T(8,128)(2,1)} async-done(((bf16[2048,768]{1,0:T(8,128)(2,1)}), bf16[512,768]{1,0:T(8,128)(2,1)}) %reduce-scatter.17.cloned.1.call-update) | async-done | bytes 786448 | tf_op jit(solution)/shard_map/reduce_scatter | solution.py:335
  708.5 1.6 fusion.12
  711.1 10.3 %all-reduce.2 = (f32[4608]{0:T(1024)S(1)}, f32[768]{0:T(1024)S(1)}) all-reduce(f32[4608]{0:T(1024)S(1)} %constant_dynamic-update-slice_fusion, f32[768]{0:T(1024)S(1)} %copy-done.35), channel_id=1, replica_groups=mesh['dp'=4,'row'=2,'col'=4] {'col'}, use_global_device_ids=true, to_apply=%region_18.19 | all-reduce | flops 5376 | bytes 43008 | tf_op jit(solution)/shard_map/psum | solution.py:346
  722.1 5.6 all-to-all-start.1
  727.8 2.8 add_bitcast_fusion
  730.6 3.7 all-to-all-done.1
  734.5 34.4 %all-reduce.1 = (f32[8,128]{1,0:T(8,128)S(1)}, f32[4608]{0:T(1024)}, f32[768]{0:T(1024)}, f32[768]{0:T(1024)}) all-reduce(f32[8,128]{1,0:T(8,128)S(1)} %fusion.21, f32[4608]{0:T(1024)S(1)} %get-tuple-element.29, f32[768]{0:T(1024)S(1)} %copy-done.37, ...), channel_id=6, replica_groups=mesh['dp'=4,'row'=2,'col'=4] {'dp','row'}, use_global_device_ids=true, to_apply=%region_19.20.clone | all-reduce | flops 7168 | bytes 57344
  (154 shorter events, 25.6 us)
Async XLA Ops:
  8.0 30.4 %copy-start = (f32[1,512,768]{2,1,0:T(8,128)S(1)}, f32[1,512,768]{2,1,0:T(8,128)}, u32[]{:S(2)}) copy-start(f32[1,512,768]{2,1,0:T(8,128)} %param.14) | copy-start | bytes 4718596
  33.4 9.9 %all-to-all-start = ((f32[8,1,576]{2,1,0:T(1,128)}), f32[8,1,576]{2,1,0:T(1,128)S(1)}, u32[]{:S(2)}, u32[]{:S(2)}) async-start(f32[8,1,576]{2,1,0:T(1,128)} %copy.28), calls=%async_computation | async-start | bytes 40960 | tf_op jit(solution)/shard_map/all_to_all | solution.py:265
  36.8 6.7 copy-start.22
  36.8 78.0 %all-gather.8.cloned.1.call-start = ((), (), s32[]{:S(2)}) async-start(), calls=%async_computation.10 | async-start | bytes 3932160 | tf_op jit(solution)/shard_map/all_gather | solution.py:274
  39.3 6.0 copy-start.18
  44.1 133.4 %copy-start.16 = (f32[768]{0:T(1024)}, f32[768]{0:T(1024)S(1)}, u32[]{:S(2)}) copy-start(f32[768]{0:T(1024)S(1)} %get-tuple-element.44) | copy-start | bytes 9220
  44.1 1.9 copy-start.12
  45.3 132.1 %reduce-scatter.11.cloned.1.call-start = ((), (), s32[]{:S(2)}) async-start(), calls=%async_computation.11 | async-start | bytes 3932160 | tf_op jit(solution)/shard_map/reduce_scatter | solution.py:279
  79.4 3.6 copy-start.7
  79.4 3.6 copy-start.14
  141.6 43.5 %all-gather.12.cloned.1.call-start = ((), (), s32[]{:S(2)}) async-start(), calls=%async_computation.13 | async-start | bytes 1327104 | tf_op jit(solution)/shard_map/all_gather | solution.py:258
  143.3 69.5 %all-gather.10.cloned.1.call-start = ((), (), s32[]{:S(2)}) async-start(), calls=%async_computation.12 | async-start | bytes 3932160 | tf_op jit(solution)/shard_map/all_gather | solution.py:289
  178.9 1.5 copy-start.28
  181.6 75.3 %all-gather.14.cloned.1.call-start = ((), (), s32[]{:S(2)}) async-start(), calls=%async_computation.14 | async-start | bytes 1327104 | tf_op jit(solution)/shard_map/all_gather | solution.py:259
  183.3 118.5 %reduce-scatter.13.cloned.1.call-start = ((), (), s32[]{:S(2)}) async-start(), calls=%async_computation.15 | async-start | bytes 3932160 | tf_op jit(solution)/shard_map/reduce_scatter | solution.py:294
  265.6 68.4 %all-gather.16.cloned.1.call-start = ((), (), s32[]{:S(2)}) async-start(), calls=%async_computation.16 | async-start | bytes 3932160 | tf_op jit(solution)/shard_map/all_gather | solution.py:305
  305.4 82.6 %reduce-scatter.15.cloned.1.call-start = ((), (), s32[]{:S(2)}) async-start(), calls=%async_computation.17 | async-start | bytes 3932160 | tf_op jit(solution)/shard_map/reduce_scatter | solution.py:311
  334.1 12.0 %copy-start.38 = (bf16[768,768]{1,0:T(8,128)(2,1)S(1)}, bf16[768,768]{1,0:T(8,128)(2,1)}, u32[]{:S(2)}) copy-start(bf16[768,768]{1,0:T(8,128)(2,1)} %all-gather.12.cloned.1.call-done) | copy-start | bytes 3538948
  344.5 1.6 copy-start.40
  350.1 76.0 %all-gather.18.cloned.1.call-start = ((), (), s32[]{:S(2)}) async-start(), calls=%async_computation.18 | async-start | bytes 3932160 | tf_op jit(solution)/shard_map/all_gather | solution.py:321
  388.0 2.5 copy-start.5
  388.0 4.7 copy-start.10
  389.6 3.0 copy-start.6
  389.6 3.0 copy-start.9
  389.6 3.0 copy-start.15
  389.6 3.0 copy-start.21
  389.7 3.0 copy-start.26
  389.7 3.0 copy-start.27
  392.7 3.8 copy-start.17
  395.3 1.1 copy-start.1
  396.4 1.1 copy-start.36
  397.5 89.3 %reduce-scatter.23.cloned.1.call-start = ((), (), s32[]{:S(2)}) async-start(), calls=%async_computation.22 | async-start | bytes 1327104 | tf_op jit(solution)/shard_map/reduce_scatter | solution.py:362
  405.6 20.5 %copy-start.4 = (bf16[3,64,2048]{2,1,0:T(8,128)(2,1)S(1)}, bf16[3,64,2048]{2,1,0:T(8,128)(2,1)}, u32[]{:S(2)}) copy-start(bf16[3,64,2048]{2,1,0:T(8,128)(2,1)} %get-tuple-element.14.mixed_t) | copy-start | bytes 2359300
  405.7 132.0 %reduce-scatter.21.cloned.1.call-start = ((), (), s32[]{:S(2)}) async-start(), calls=%async_computation.21 | async-start | bytes 1327104 | tf_op jit(solution)/shard_map/reduce_scatter | solution.py:361
  412.5 189.5 %reduce-scatter.25.cloned.1.call-start = ((), (), s32[]{:S(2)}) async-start(), calls=%async_computation.23 | async-start | bytes 442368
  429.8 239.4 %reduce-scatter.19.cloned.1.call-start = ((), (), s32[]{:S(2)}) async-start(), calls=%async_computation.20 | async-start | bytes 1327104 | tf_op jit(solution)/shard_map/reduce_scatter | solution.py:359
  472.7 6.7 copy-start.8
  479.1 229.4 %reduce-scatter.17.cloned.1.call-start = ((), (), s32[]{:S(2)}) async-start(), calls=%async_computation.19 | async-start | bytes 3932160 | tf_op jit(solution)/shard_map/reduce_scatter | solution.py:335
  539.3 170.7 %copy-start.24 = (f32[512]{0:T(512)S(1)}, f32[512]{0:T(512)}, u32[]{:S(2)}) copy-start(f32[512]{0:T(512)} %copy-done.23) | copy-start | bytes 6148
  539.3 170.8 %copy-start.19 = (f32[512]{0:T(512)S(1)}, f32[512]{0:T(512)}, u32[]{:S(2)}) copy-start(f32[512]{0:T(512)} %copy-done.18) | copy-start | bytes 6148
  708.5 1.7 copy-start.3
  710.1 1.0 copy-start.31
  710.1 1.0 copy-start.35
  710.1 17.6 %copy-start.2 = (f32[512,768]{1,0:T(8,128)S(1)}, f32[512,768]{1,0:T(8,128)}, u32[]{:S(2)}) copy-start(f32[512,768]{1,0:T(8,128)} %copy-done.1) | copy-start | bytes 4718596
  722.1 12.3 %all-to-all-start.1 = ((f32[8,1,576]{2,1,0:T(1,128)}), f32[8,1,576]{2,1,0:T(1,128)S(1)}, u32[]{:S(2)}, u32[]{:S(2)}) async-start(f32[8,1,576]{2,1,0:T(1,128)} %all_to_all.16), calls=%async_computation.5 | async-start | bytes 40960 | tf_op jit(solution)/shard_map/all_to_all | solution.py:349
  727.8 6.6 copy-start.11
  727.8 6.8 copy-start.37
  727.8 42.3 %copy-start.30 = (bf16[8,1,128]{2,1,0:T(2,128)(2,1)S(1)}, bf16[8,1,128]{2,1,0:T(2,128)(2,1)}, u32[]{:S(2)}) copy-start(bf16[8,1,128]{2,1,0:T(2,128)(2,1)} %copy-done.29) | copy-start | bytes 6148
  (9 other events, 6.9 us)
Sparse Core Ops, SparseCore 0:
  45.4 25.7 all-gather.7
  141.8 35.6 reduce-scatter.10
  305.5 28.5 all-gather.15
  397.6 28.4 all-gather.17
Sparse Core Ops, SparseCore 1:
  144.9 39.0 all-gather.11
  186.0 26.7 all-gather.9
  215.4 41.4 all-gather.13
  265.7 36.0 reduce-scatter.12
  350.2 37.7 reduce-scatter.14
  405.7 64.7 reduce-scatter.22
  473.8 63.8 reduce-scatter.20
  540.8 61.1 reduce-scatter.24
  605.3 63.9 reduce-scatter.18
  671.8 36.6 reduce-scatter.16

commit v2 on v1

--- a/solution.py
+++ b/solution.py
@@ -73,34 +73,6 @@
     return jnp.concatenate([rows] + extras + [pad], axis=0)
 
 
-def project_rotate(heads, size, normed, weight_t, cosine, sine, bias, qkv, query, key):
-    length = normed.shape[0]
-    half = HD // 2
-
-    def step(i, _):
-        here = block_at(i, size)
-        both = contract(weight_t[...], normed[here, :], 1, 1)
-        c, s = cosine[:, here], sine[:, here]
-        one = jnp.ones((1, size), F32)
-        for h in range(heads):
-            for t in range(3):
-                at = (t * heads + h) * HD
-                if t == 2:
-                    qkv[t * heads + h, :, here] = both[at : at + HD].astype(BF16)
-                    continue
-                a, b = both[at : at + half], both[at + half : at + HD]
-                turned = jnp.concatenate([a * c - b * s, b * c + a * s], axis=0)
-                qkv[t * heads + h, :, here] = turned.astype(BF16)
-                if t == 0:
-                    query[h, :, here] = augment(turned, [one]).astype(BF16)
-                else:
-                    wide = augment(turned, [bias[:, here], one, one, one])
-                    key[h, here, :] = wide.T.astype(BF16)
-        return 0
-
-    lax.fori_loop(0, length // size, step, 0)
-
-
 def attend_block(heads, here, query, key, value_t, mixed_t, log_total):
     scores = [contract(key[h], query[h, :, here], 1, 0) for h in range(heads)]
     for h in range(heads):
@@ -110,44 +82,6 @@
         out = contract(value_t[h], weights.astype(BF16), 1, 0) * (1.0 / total)
         mixed_t[h, :, here] = out.astype(BF16)
         log_total[h, :, here] = top * UNIT + jnp.log2(total)
-
-
-def attention_forward_kernel(
-    heads, normed, weight, cosine, sine, bias, qkv, mixed_t, log_total, weight_t, query, key
-):
-    length = normed.shape[0]
-    weight_t[...] = weight[...].astype(F32).T.astype(BF16)
-    size = min(512, length)
-    project_rotate(heads, size, normed, weight_t, cosine, sine, bias, qkv, query, key)
-
-    def step(i, _):
-        attend_block(
-            heads, block_at(i, size), query, key, qkv.at[pl.ds(2 * heads, heads)], mixed_t, log_total
-        )
-        return 0
-
-    lax.fori_loop(0, length // size, step, 0)
-
-
-def attention_forward(heads, normed, weight, cosine, sine, bias):
-    length, width = normed.shape
-    vmem = pl.BlockSpec(memory_space=pltpu.VMEM)
-    return pl.pallas_call(
-        functools.partial(attention_forward_kernel, heads),
-        out_shape=[
-            jax.ShapeDtypeStruct((3 * heads, HD, length), BF16),
-            jax.ShapeDtypeStruct((heads, HD, length), BF16),
-            jax.ShapeDtypeStruct((heads, 1, length), F32),
-        ],
-        in_specs=[vmem] * 5,
-        out_specs=[vmem] * 3,
-        scratch_shapes=[
-            pltpu.VMEM((3 * heads * HD, width), BF16),
-            pltpu.VMEM((heads, AUG, length), BF16),
-            pltpu.VMEM((heads, length, AUG), BF16),
-        ],
-        compiler_params=pltpu.CompilerParams(vmem_limit_bytes=VMEM_LIMIT),
-    )(normed, weight, cosine, sine, bias)
 
 
 def prepare_backward(heads, h, size, length, qkv, bias, log_total, mixed_t, back_t, query, key, value, back):
@@ -230,7 +164,566 @@
     )(qkv, bias, log_total, mixed_t, back_t, cosine, sine)
 
 
+MESH = pl.DeviceIdType.MESH
+
+
+def flip(index, bit):
+    return index + bit - 2 * bit * lax.rem(lax.div(index, bit), 2)
+
+
+def flips(index, bits):
+    for bit in bits:
+        index = flip(index, bit)
+    return index
+
+
+def doubling(sizes):
+    steps = []
+    for axis, stride in (("dp", sizes["row"]), ("row", 1)):
+        bit = sizes[axis] // 2
+        while bit:
+            steps.append((axis, bit, bit * stride))
+            bit //= 2
+    return steps
+
+
+def subsets(bits):
+    out = [()]
+    for bit in bits:
+        out = out + [kept + (bit,) for kept in out]
+    return out
+
+
+def send_copy(source, target, send, receive, peer):
+    return pltpu.make_async_remote_copy(
+        src_ref=source, dst_ref=target, send_sem=send, recv_sem=receive, device_id=peer, device_id_type=MESH
+    )
+
+
+def greet(peers):
+    barrier = pltpu.get_barrier_semaphore()
+    for peer in peers:
+        pl.semaphore_signal(barrier, inc=1, device_id=peer, device_id_type=MESH)
+    pl.semaphore_wait(barrier, len(peers))
+
+
+def shard_number(sizes):
+    return lax.axis_index("dp") * sizes["row"] + lax.axis_index("row")
+
+
+def doubling_peers(sizes):
+    return [{axis: flip(lax.axis_index(axis), bit)} for axis, bit, _ in doubling(sizes)]
+
+
+def col_peers():
+    me = lax.axis_index("col")
+    return [{"col": flip(me, 1)}, {"col": flip(me, 2)}]
+
+
+class ShardGather:
+    def __init__(self, sizes, shard, full, sems):
+        self.steps = doubling(sizes)
+        self.rows = shard.shape[0]
+        self.shard, self.full, self.sems = shard, full, sems
+        self.me = shard_number(sizes)
+
+    def slot(self, number):
+        return self.full.at[pl.ds(pl.multiple_of(number * self.rows, self.rows), self.rows), :]
+
+    def copies(self, k, arriving):
+        axis, bit, stride = self.steps[k]
+        peer = {axis: flip(lax.axis_index(axis), bit)}
+        out = []
+        for i, kept in enumerate(subsets([s[2] for s in self.steps[:k]])):
+            number = flips(self.me, kept + ((stride,) if arriving else ()))
+            source = self.slot(number)
+            if not arriving and not kept:
+                source = self.shard
+            at = 2**k - 1 + i
+            out.append(send_copy(source, self.slot(number), self.sems.at[0, at], self.sems.at[1, at], peer))
+        return out
+
+    def keep(self):
+        self.slot(self.me)[...] = self.shard[...]
+
+    def start(self, k):
+        for copy in self.copies(k, False):
+            copy.start()
+
+    def arrived(self, k):
+        for copy in self.copies(k, True):
+            copy.wait_recv()
+
+    def advance(self, k):
+        if 0 < k <= len(self.steps):
+            self.arrived(k - 1)
+        if k < len(self.steps):
+            self.start(k)
+
+    def close(self):
+        for k in range(len(self.steps)):
+            for copy in self.copies(k, False):
+                copy.wait_send()
+
+    @staticmethod
+    def semaphores(count):
+        return pltpu.SemaphoreType.DMA((2, count - 1))
+
+
+class ShardScatter:
+    def __init__(self, sizes, total, out_buf, in_buf, sems):
+        self.steps = doubling(sizes)[::-1]
+        self.rows = out_buf.shape[1]
+        self.total, self.out_buf, self.in_buf, self.sems = total, out_buf, in_buf, sems
+        self.me = shard_number(sizes)
+        self.first = [0]
+        for k in range(len(self.steps)):
+            self.first.append(self.first[-1] + 2 ** (len(self.steps) - 1 - k))
+
+    def part(self, number):
+        return pl.ds(pl.multiple_of(number * self.rows, self.rows), self.rows)
+
+    def rest(self, k):
+        return subsets([s[2] for s in self.steps[k + 1 :]])
+
+    def copy(self, k, i):
+        axis, bit, _ = self.steps[k]
+        at = self.first[k] + i
+        peer = {axis: flip(lax.axis_index(axis), bit)}
+        return send_copy(self.out_buf.at[at], self.in_buf.at[at], self.sems.at[0, at], self.sems.at[1, at], peer)
+
+    def start(self, k):
+        stride = self.steps[k][2]
+        for i, kept in enumerate(self.rest(k)):
+            number = flips(self.me, (stride,) + kept)
+            self.out_buf[self.first[k] + i] = self.total[self.part(number), :].astype(BF16)
+            copy = self.copy(k, i)
+            copy.start()
+
+    def arrived(self, k):
+        for i, kept in enumerate(self.rest(k)):
+            self.copy(k, i).wait_recv()
+            here = self.part(flips(self.me, kept))
+            self.total[here, :] = self.total[here, :] + self.in_buf[self.first[k] + i].astype(F32)
+
+    def advance(self, k):
+        if 0 < k <= len(self.steps):
+            self.arrived(k - 1)
+        if k < len(self.steps):
+            self.start(k)
+
+    def close(self):
+        for k in range(len(self.steps)):
+            for i in range(len(self.rest(k))):
+                self.copy(k, i).wait_send()
+
+    @staticmethod
+    def scratch(count, rows, width):
+        return [
+            pltpu.VMEM((count - 1, rows, width), BF16),
+            pltpu.VMEM((count - 1, rows, width), BF16),
+            pltpu.SemaphoreType.DMA((2, count - 1)),
+        ]
+
+
+class ColumnGather:
+    def __init__(self, full, chunks, sems):
+        self.full, self.chunks, self.sems = full, chunks, sems
+        self.me = lax.axis_index("col")
+        self.rows = full.shape[1] // chunks
+
+    def chunk(self, slot, j):
+        return self.full.at[slot, pl.ds(j * self.rows, self.rows), :]
+
+    def copy(self, kind, j, slot):
+        peer = {"col": flip(self.me, 2 if kind == 1 else 1)}
+        here = self.chunk(slot, j)
+        return send_copy(here, here, self.sems.at[0, kind, j], self.sems.at[1, kind, j], peer)
+
+    def start(self, j):
+        for kind in (1, 0):
+            copy = self.copy(kind, j, self.me)
+            copy.start()
+
+    def partner(self, j):
+        self.copy(0, j, flip(self.me, 1)).wait_recv()
+
+    def across(self, j):
+        there = flip(self.me, 2)
+        self.copy(1, j, there).wait_recv()
+        copy = self.copy(2, j, there)
+        copy.start()
+
+    def diagonal(self, j):
+        self.copy(2, j, flips(self.me, (1, 2))).wait_recv()
+
+    def close(self):
+        for j in range(self.chunks):
+            for kind in range(3):
+                self.copy(kind, j, self.me).wait_send()
+
+    @staticmethod
+    def semaphores(chunks):
+        return pltpu.SemaphoreType.DMA((2, 3, chunks))
+
+
+class ColumnScatter:
+    def __init__(self, pair_out, pair_in, far_out, far_in, kept, chunks, sems):
+        self.pair_out, self.pair_in, self.far_out, self.far_in = pair_out, pair_in, far_out, far_in
+        self.kept, self.chunks, self.sems = kept, chunks, sems
+        self.rows = kept.shape[0] // chunks
+        me = lax.axis_index("col")
+        self.near, self.far = {"col": flip(me, 1)}, {"col": flip(me, 2)}
+
+    def at(self, j):
+        return pl.ds(j * self.rows, self.rows)
+
+    def pair(self, which, j):
+        return send_copy(
+            self.pair_out.at[which, self.at(j), :],
+            self.pair_in.at[which, self.at(j), :],
+            self.sems.at[0, which, j],
+            self.sems.at[1, which, j],
+            self.near,
+        )
+
+    def cross(self, j):
+        return send_copy(
+            self.far_out.at[self.at(j), :],
+            self.far_in.at[self.at(j), :],
+            self.sems.at[0, 2, j],
+            self.sems.at[1, 2, j],
+            self.far,
+        )
+
+    def begin(self, copy):
+        copy.start()
+
+    def give_diagonal(self, j, value):
+        self.pair_out[1, self.at(j), :] = value.astype(BF16)
+        self.begin(self.pair(1, j))
+
+    def give_across(self, j, value):
+        self.pair(1, j).wait_recv()
+        self.far_out[self.at(j), :] = (value + self.pair_in[1, self.at(j), :].astype(F32)).astype(BF16)
+        self.begin(self.cross(j))
+
+    def give_partner(self, j, value):
+        self.pair_out[0, self.at(j), :] = value.astype(BF16)
+        self.begin(self.pair(0, j))
+
+    def give_own(self, j, value):
+        self.pair(0, j).wait_recv()
+        self.kept[self.at(j), :] = value + self.pair_in[0, self.at(j), :].astype(F32)
+
+    def result(self, j):
+        self.cross(j).wait_recv()
+        return self.kept[self.at(j), :] + self.far_in[self.at(j), :].astype(F32)
+
+    def close(self):
+        for j in range(self.chunks):
+            self.pair(0, j).wait_send()
+            self.pair(1, j).wait_send()
+            self.cross(j).wait_send()
+
+    @staticmethod
+    def scratch(rows, width, chunks):
+        return [
+            pltpu.VMEM((2, rows, width), BF16),
+            pltpu.VMEM((2, rows, width), BF16),
+            pltpu.VMEM((rows, width), BF16),
+            pltpu.VMEM((rows, width), BF16),
+            pltpu.VMEM((rows, width), F32),
+            pltpu.SemaphoreType.DMA((2, 3, chunks)),
+        ]
+
+
+def other_peers(sizes):
+    number = shard_number(sizes)
+    total = sizes["dp"] * sizes["row"]
+    bits = [stride for _, _, stride in doubling(sizes)]
+    out = []
+    for kept in subsets(bits)[1:]:
+        peer = {}
+        for axis, bit, stride in doubling(sizes):
+            if stride in kept:
+                peer[axis] = flip(peer.get(axis, lax.axis_index(axis)), bit)
+        out.append((flips(number, kept), peer))
+    assert len(out) == total - 1
+    return out
+
+
+def start_kernel(
+    sizes, heads, chunks,
+    condition, condition_weight, condition_bias, tokens, in_shard, out_shard, cosine, sine, cotangent, valid,
+    modulation, normed, qkv, out_full, feed_back, bias_part,
+    condition_all, pieces, arrived, in_full, out_t, in_t, unit, sems_tiny, sems_in, sems_out, sems_col,
+):
+    count = sizes["dp"] * sizes["row"]
+    number = shard_number(sizes)
+    rows, width = tokens.shape
+    others = other_peers(sizes)
+    greet([peer for _, peer in others] + col_peers())
+    gather_in = ShardGather(sizes, in_shard, in_full, sems_in)
+    gather_out = ShardGather(sizes, out_shard, out_t, sems_out)
+    gather_col = ColumnGather(normed, chunks, sems_col)
+
+    def condition_copy(i, slot):
+        return send_copy(
+            condition, condition_all.at[slot], sems_tiny.at[0, i], sems_tiny.at[1, i], others[i][1]
+        )
+
+    def piece_copy(i, mine, slot):
+        return send_copy(
+            pieces.at[mine], arrived.at[slot], sems_tiny.at[2, i], sems_tiny.at[3, i], others[i][1]
+        )
+
+    for i in range(count - 1):
+        condition_copy(i, number).start()
+    gather_in.start(0)
+    gather_out.start(0)
+    condition_all[number] = condition[...]
+    gather_in.keep()
+    gather_out.keep()
+    size = rows // chunks
+
+    def normal(j, _):
+        here = block_at(j, size)
+        unit[here, :] = layer_norm(tokens[here, :])
+        return 0
+
+    lax.fori_loop(0, chunks, normal, 0)
+    for i in range(count - 1):
+        condition_copy(i, others[i][0]).wait_recv()
+    stacked = jnp.concatenate([condition_all[b] for b in range(count)], axis=0)
+    product = contract(stacked.astype(BF16), condition_weight[...], 1, 0)
+    for b in range(count):
+        pieces[b] = product[b : b + 1]
+    for i in range(count - 1):
+        piece_copy(i, others[i][0], number).start()
+    arrived[number] = pieces[number]
+    gather_in.advance(1)
+    gather_out.advance(1)
+    for i in range(count - 1):
+        piece_copy(i, number, others[i][0]).wait_recv()
+    line = jnp.concatenate([arrived[b] for b in range(count)], axis=1) + condition_bias[...]
+    parts = [line[:, t * width : (t + 1) * width] for t in range(6)]
+    for t in range(6):
+        modulation[t : t + 1, :] = parts[t]
+    for j in range(chunks):
+        here = pl.ds(j * size, size)
+        value = unit[here, :] * (1.0 + parts[1]) + parts[0]
+        normed[gather_col.me, here, :] = value.astype(BF16)
+        gather_col.start(j)
+    gather_in.advance(2)
+    gather_out.advance(2)
+    total = jnp.zeros((1, width), F32)
+    for j in range(chunks):
+        here = pl.ds(j * size, size)
+        value = parts[5] * (cotangent[here, :] * valid[here, :])
+        feed_back[here, :] = value.astype(BF16)
+        total = total + jnp.sum(value, axis=0, keepdims=True)
+    bias_part[...] = total
+    steps = len(gather_in.steps)
+    for k in range(3, steps + 1):
+        gather_in.advance(k)
+        gather_out.advance(k)
+    in_t[...] = in_full[...].astype(F32).T.astype(BF16)
+    out_full[...] = out_t[...].astype(F32).T.astype(BF16)
+
+    def project(slot):
+        here = pl.ds(pl.multiple_of(slot * rows, rows), rows)
+        both = contract(in_t[...], normed[slot], 1, 1)
+        half = HD // 2
+        c, s = cosine[:, here], sine[:, here]
+        for h in range(heads):
+            for t in range(3):
+                at = (t * heads + h) * HD
+                a, b = both[at : at + half], both[at + half : at + HD]
+                if t < 2:
+                    a, b = a * c - b * s, b * c + a * s
+                qkv[t * heads + h, :, here] = jnp.concatenate([a, b], axis=0).astype(BF16)
+
+    me = gather_col.me
+    far = flip(me, 2)
+
+    def steps_of(i, _):
+        @pl.when(i == 1)
+        def _():
+            for j in range(chunks):
+                gather_col.partner(j)
+
+        @pl.when(i == 2)
+        def _():
+            for j in range(chunks):
+                gather_col.across(j)
+
+        @pl.when(i == 3)
+        def _():
+            for j in range(chunks):
+                gather_col.diagonal(j)
+
+        project(flip_by(me, i))
+        return 0
+
+    lax.fori_loop(0, 4, steps_of, 0)
+    for i in range(count - 1):
+        condition_copy(i, number).wait_send()
+        piece_copy(i, others[i][0], number).wait_send()
+    gather_in.close()
+    gather_out.close()
+    gather_col.close()
+
+
+def flip_by(index, pattern):
+    out = 0
+    for bit in (1, 2):
+        a, b = lax.rem(lax.div(index, bit), 2), lax.rem(lax.div(pattern, bit), 2)
+        out = out + bit * (a + b - 2 * a * b)
+    return out
+
+
+def start(sizes, heads, condition, condition_weight, condition_bias, tokens, in_shard, out_shard, cosine, sine, cotangent, valid):
+    count = sizes["dp"] * sizes["row"]
+    rows, width = tokens.shape
+    length = cosine.shape[1]
+    chunks = 2
+    vmem = pl.BlockSpec(memory_space=pltpu.VMEM)
+    piece = condition_weight.shape[1]
+    local = heads * HD
+    return pl.pallas_call(
+        functools.partial(start_kernel, sizes, heads, chunks),
+        out_shape=[
+            jax.ShapeDtypeStruct((6, width), F32),
+            jax.ShapeDtypeStruct((4, rows, width), BF16),
+            jax.ShapeDtypeStruct((3 * heads, HD, length), BF16),
+            jax.ShapeDtypeStruct((local, width), BF16),
+            jax.ShapeDtypeStruct((rows, width), BF16),
+            jax.ShapeDtypeStruct((1, width), F32),
+        ],
+        in_specs=[vmem] * 10,
+        out_specs=[vmem] * 6,
+        scratch_shapes=[
+            pltpu.VMEM((count,) + condition.shape, F32),
+            pltpu.VMEM((count, 1, piece), F32),
+            pltpu.VMEM((count, 1, piece), F32),
+            pltpu.VMEM((width, 3 * local), BF16),
+            pltpu.VMEM((width, local), BF16),
+            pltpu.VMEM((3 * local, width), BF16),
+            pltpu.VMEM((rows, width), F32),
+            pltpu.SemaphoreType.DMA((4, count - 1)),
+            ShardGather.semaphores(count),
+            ShardGather.semaphores(count),
+            ColumnGather.semaphores(chunks),
+        ],
+        compiler_params=pltpu.CompilerParams(
+            vmem_limit_bytes=VMEM_LIMIT, collective_id=0, has_side_effects=True
+        ),
+    )(condition, condition_weight, condition_bias, tokens, in_shard, out_shard, cosine, sine, cotangent, valid)
+
+
+def attention_kernel(
+    sizes, heads, chunks,
+    qkv, bias, out_full, feed_back, up_shard, down_shard,
+    attention, mixed_t, log_total, feed_back_all, up_full, down_t,
+    query, key, pair_out, pair_in, far_out, far_in, kept, sems_scatter, sems_col, sems_up, sems_down,
+):
+    rows = feed_back.shape[0]
+    length = qkv.shape[2]
+    greet(doubling_peers(sizes) + col_peers())
+    gather_up = ShardGather(sizes, up_shard, up_full, sems_up)
+    gather_down = ShardGather(sizes, down_shard, down_t, sems_down)
+    gather_col = ColumnGather(feed_back_all, chunks, sems_col)
+    scatter = ColumnScatter(pair_out, pair_in, far_out, far_in, kept, 1, sems_scatter)
+    me = gather_col.me
+    gather_up.start(0)
+    gather_down.start(0)
+    feed_back_all[me] = feed_back[...]
+    for j in range(chunks):
+        gather_col.start(j)
+    gather_up.keep()
+    gather_down.keep()
+
+    def prepare(i, _):
+        here = block_at(i, rows)
+        one = jnp.ones((1, rows), F32)
+        for h in range(heads):
+            query[h, :, here] = augment(qkv[h, :, here].astype(F32), [one]).astype(BF16)
+            keys = augment(qkv[heads + h, :, here].astype(F32), [bias[:, here], one, one, one])
+            key[h, here, :] = keys.T.astype(BF16)
+        return 0
+
+    lax.fori_loop(0, length // rows, prepare, 0)
+    steps = len(gather_up.steps)
+
+    def step(i, _):
+        here = block_at(flip_by(me, 3 - i), rows)
+        attend_block(heads, here, query, key, qkv.at[pl.ds(2 * heads, heads)], mixed_t, log_total)
+        value = contract(mixed_t[:, :, here].reshape(heads * HD, rows), out_full[...], 0, 0)
+        for order, give in enumerate(
+            (scatter.give_diagonal, scatter.give_across, scatter.give_partner, scatter.give_own)
+        ):
+
+            @pl.when(i == order)
+            def _():
+                give(0, value)
+                if order < 3:
+                    gather_up.advance(order + 1)
+                    gather_down.advance(order + 1)
+
+        return 0
+
+    lax.fori_loop(0, 4, step, 0)
+    for k in range(4, steps + 1):
+        gather_up.advance(k)
+        gather_down.advance(k)
+    for j in range(chunks):
+        gather_col.across(j)
+    for j in range(chunks):
+        gather_col.partner(j)
+        gather_col.diagonal(j)
+    attention[...] = scatter.result(0)
+    gather_up.close()
+    gather_down.close()
+    gather_col.close()
+    scatter.close()
+
+
+def attend(sizes, heads, qkv, bias, out_full, feed_back, up_shard, down_shard):
+    count = sizes["dp"] * sizes["row"]
+    rows, width = feed_back.shape
+    length = qkv.shape[2]
+    chunks = 2
+    hidden = up_shard.shape[1]
+    vmem = pl.BlockSpec(memory_space=pltpu.VMEM)
+    return pl.pallas_call(
+        functools.partial(attention_kernel, sizes, heads, chunks),
+        out_shape=[
+            jax.ShapeDtypeStruct((rows, width), F32),
+            jax.ShapeDtypeStruct((heads, HD, length), BF16),
+            jax.ShapeDtypeStruct((heads, 1, length), F32),
+            jax.ShapeDtypeStruct((4, rows, width), BF16),
+            jax.ShapeDtypeStruct((width, hidden), BF16),
+            jax.ShapeDtypeStruct((width, hidden), BF16),
+        ],
+        in_specs=[vmem] * 6,
+        out_specs=[vmem] * 6,
+        scratch_shapes=[
+            pltpu.VMEM((heads, AUG, length), BF16),
+            pltpu.VMEM((heads, length, AUG), BF16),
+            *ColumnScatter.scratch(rows, width, 1),
+            ColumnGather.semaphores(chunks),
+            ShardGather.semaphores(count),
+            ShardGather.semaphores(count),
+        ],
+        compiler_params=pltpu.CompilerParams(
+            vmem_limit_bytes=VMEM_LIMIT, collective_id=1, has_side_effects=True
+        ),
+    )(qkv, bias, out_full, feed_back, up_shard, down_shard)
+
+
 def shards(
+    sizes,
     tokens,
     condition,
     lengths,
@@ -252,36 +745,33 @@
     local_width = attention_in.shape[2]
     heads = local_width // HD
     group = ("dp", "row")
-    in_full, out_full, up_full, down_full = (
-        lax.all_gather(attention_in.astype(BF16), group, axis=0, tiled=True),
-        lax.all_gather(attention_out.astype(BF16), group, axis=1, tiled=True),
-        lax.all_gather(up_weight.astype(BF16), group, axis=0, tiled=True),
-        lax.all_gather(down_weight.astype(BF16), group, axis=1, tiled=True),
-    )
+    in_shard = attention_in.reshape(attention_in.shape[0], 3 * local_width).astype(BF16)
+    out_shard = attention_out.T.astype(BF16)
+    up_shard = up_weight.astype(BF16)
+    down_shard = down_weight.T.astype(BF16)
     condition_low = condition.astype(BF16)
-    condition_all = lax.all_gather(condition_low, group, axis=0, tiled=True)
     weight_low = condition_weight.astype(BF16)
-    pieces = jnp.dot(condition_all, weight_low, preferred_element_type=F32)
-    modulation = lax.all_to_all(pieces, group, 0, 0, tiled=True).reshape(-1) + condition_bias
-    parts = modulation.reshape(6, width)
     own_rows = tokens[0]
     length = lengths[0]
     position = column_index * rows + jnp.arange(rows)
     valid = (position < length).astype(F32)
     bias = jnp.where(jnp.arange(length_all) < length, 0.0, MASKED).astype(F32)[None]
     cosine, sine = (jnp.asarray(table) for table in rotary_tables(length_all))
-    normed, first_pull = jax.vjp(norm_shift, own_rows, parts[0], parts[1])
-    normed_all = lax.all_gather(normed.astype(BF16), "col", axis=0, tiled=True)
-    qkv, mixed_t, log_total = attention_forward(
-        heads, normed_all, in_full.reshape(width, 3 * local_width), cosine, sine, bias
-    )
+    parts, normed_blocks, qkv, out_full, feed_back, down_bias_part = start(
+        sizes, heads, condition_low.astype(F32), weight_low, condition_bias[None], own_rows,
+        in_shard, out_shard, cosine, sine, cotangent[0], valid[:, None],
+    )
+    down_bias_part = down_bias_part[0]
+    normed_all = normed_blocks.reshape(length_all, width)
+    _, first_pull = jax.vjp(norm_shift, own_rows, parts[0], parts[1])
+    attention, mixed_t, log_total, feed_back_blocks, up_full, down_t = attend(
+        sizes, heads, qkv, bias, out_full, feed_back, up_shard, down_shard
+    )
+    in_full = lax.all_gather(in_shard, group, axis=0, tiled=True).reshape(width, 3, local_width)
+    condition_all = lax.all_gather(condition_low, group, axis=0, tiled=True)
     mixed_rows = mixed_t.reshape(local_width, length_all)
-    attention = lax.psum_scatter(
-        jnp.einsum("cs,cd->sd", mixed_rows, out_full, preferred_element_type=F32).astype(BF16),
-        "col",
-        scatter_dimension=0,
-        tiled=True,
-    ).astype(F32)
+    down_full = down_t.T
+    feed_back_all = feed_back_blocks.reshape(length_all, width)
     middle = own_rows + parts[2] * attention
     second, second_pull = jax.vjp(norm_shift, middle, parts[3], parts[4])
     second_low = second.astype(BF16)
@@ -299,10 +789,7 @@
     ).astype(F32)
     result = middle + parts[5] * (feed + down_bias)
     incoming = cotangent[0] * valid[:, None]
-    down_bias_part = jnp.sum(parts[5] * incoming, axis=0)
     gate_feed = jnp.sum(incoming * (feed + down_bias), axis=0)
-    feed_back = (parts[5] * incoming).astype(BF16)
-    feed_back_all = lax.all_gather(feed_back, "col", axis=0, tiled=True)
     hidden_back = jnp.einsum("sd,fd->sf", feed_back_all, down_full, preferred_element_type=F32)
     down_grad = jnp.einsum("sf,sd->fd", hidden_low, feed_back_all, preferred_element_type=F32)
     before_back = gelu_pull(hidden_back)[0].astype(BF16)
@@ -380,6 +867,7 @@
 
 
 def solution(mesh):
+    sizes = {axis: mesh.shape[axis] for axis in ("dp", "row", "col")}
     in_specs = (
         P(("dp", "row"), "col", None),
         P(("dp", "row"), None),
@@ -407,4 +895,4 @@
         P("col", ("dp", "row")),
         P(),
     )
-    return jax.shard_map(shards, mesh=mesh, in_specs=in_specs, out_specs=out_specs, check_vma=False)
+    return jax.shard_map(functools.partial(shards, sizes), mesh=mesh, in_specs=in_specs, out_specs=out_specs, check_vma=False)

time: 786 us -> 675 us (0.86)
  waiting for transfers between devices: 437 us -> 287 us
  Pallas kernels: 61.6 us -> 145 us
  blocking collectives: 131 us -> 99.1 us
  matrix products: 70.9 us -> 61.5 us
    pallas_call x1 -> x2, Pallas kernels: 23 us -> 106 us  [the longest x1 61.7 us: attend(): pl.pallas_call(functools.partial(attention_kernel, sizes, heads, chunks),...]
    all_gather x4 -> x0, waiting for transfers between devices: 65.2 us -> none  [the longest x1 36.6 us: shards(): lax.all_gather(down_weight.astype(BF16), group, axis=1, tiled=True)]
    reduce_scatter x1, waiting for transfers between devices: 49.3 us -> 0.01 us  [shards(): lax.psum_scatter(up_grad.astype(BF16), group, scatter_dimension=0, tiled=...]
    reduce_scatter x1 -> x0, waiting for transfers between devices: 34.1 us -> none  [shards(): lax.psum_scatter(jnp.einsum('cs,cd->sd', mixed_rows, out_full, preferred_...]
    all_gather x2 -> x1, blocking collectives: 64.4 us -> 33.9 us  [shards(): lax.all_gather(in_shard, group, axis=0, tiled=True)]
    reduce_scatter x1, waiting for transfers between devices: 0.01 us -> 21.2 us  [shards(): lax.psum_scatter(down_grad.astype(BF16), group, scatter_dimension=1, tile...]
    reduce_scatter x1, starting transfers between devices: 0.04 us -> 12.1 us  [shards(): lax.psum_scatter(up_grad.astype(BF16), group, scatter_dimension=0, tiled=...]
    all_gather x1, waiting for transfers between devices: 13.6 us -> 1.62 us  [shards(): lax.all_gather(attention_back, 'col', axis=0, tiled=True)]
  transfers between devices with their start and end apart: 16 -> 10, of which waited for: 13 -> 9; matrix products, arithmetic and copies ran while one was open for 8% -> 9% of each run, Pallas kernels for 5% -> 6%
where the time goes in v2:
time: 675 us; the launch traced here: 668 us
  waiting for transfers between devices  287 us (43%)
  Pallas kernels  145 us (21%)
  blocking collectives  99.1 us (15%)
  matrix products  61.5 us (9%)
  other arithmetic  28.4 us (4%)
  starting transfers between devices  18.3 us (3%)
  between operations  15.1 us (2%)
  local copies, waits for them, and re-layouts  13.7 us (2%)
    reduce_scatter x1, waiting for transfers between devices, shards(): lax.psum_scatter(in_grad.astype(BF16), group, scatter_dimension=0, tiled=...  65.6 us
    unnamed x10, waiting for transfers between devices  62.9 us
    pallas_call x1, Pallas kernels, attend(): pl.pallas_call(functools.partial(attention_kernel, sizes, heads, chunks),...  61.7 us
    pallas_call x1, Pallas kernels, start(): pl.pallas_call(functools.partial(start_kernel, sizes, heads, chunks), out...  44.3 us
    pallas_call x1, Pallas kernels, attention_backward(): pl.pallas_call(functools.partial(attention_backward_kernel, heads), out_s...  38.6 us
    reduce_scatter x1, waiting for transfers between devices, shards(): lax.psum_scatter(jnp.dot(hidden_low, down_full, preferred_element_type=F3...  38 us
    reduce_scatter x1, waiting for transfers between devices, shards(): lax.psum_scatter(jnp.einsum('tes,dte->sd', projected_back, in_full, prefe...  37.8 us
    unnamed x1, blocking collectives  34.5 us
  transfers between devices with their start and end apart: 10, of which 9 were waited for; matrix products, arithmetic and copies ran while one was open for 9% of the time, Pallas kernels for 6%

profile of v2, /device:TPU:0, one launch (start us, length us, event | category | flops | bytes accessed | tf_op | source)
XLA Modules:
  0.0 667.9 jit_solution(15161025391884557308)
XLA Ops:
  7.9 1.2 convert_bitcast_fusion.2
  9.7 1.3 broadcast_in_dim.22.condition_bias
  11.1 1.6 copy.44
  12.7 1.0 convert_element_type.105
  14.6 1.6 convert_element_type.110.up_shard
  18.5 44.3 %shard_map.221 = (f32[6,768]{1,0:T(8,128)}, bf16[4,512,768]{2,1,0:T(8,128)(2,1)}, bf16[9,64,2048]{2,1,0:T(8,128)(2,1)}, bf16[192,768]{1,0:T(8,128)(2,1)}, bf16[512,768]{1,0:T(8,128)(2,1)}, /*index=5*/f32[1,768]{1,0:T(1,128)}) custom-call(f32[1,128]{1,0:T(1,128)} %get-tuple-element.65.condition, bf16[128,576]{1,0:T(8,128)(2,1)} %copy.42.condition_weight, ...), custom_call_target="tpu_custom_call" | custom-call | tf_op jit(solution)/shard_map/pallas_call | solution.py:594
  62.7 1.0 add_reduce_fusion
  63.7 61.7 %shard_map.222 = (f32[512,768]{1,0:T(8,128)}, bf16[3,64,2048]{2,1,0:T(8,128)(2,1)}, f32[3,1,2048]{2,1,0:T(1,128)}, bf16[4,512,768]{2,1,0:T(8,128)(2,1)}, bf16[76...) custom-call(bf16[9,64,2048]{2,1,0:T(8,128)(2,1)} %get-tuple-element.24.qkv, f32[1,2048]{1,0:T(1,128)} %compare_select_fusion.bias, ...), custom_call_target="tpu_custom_call" | custom-call | tf_op jit(solution)/shard_map/pallas_call | solution.py:699
  125.5 1.7 fusion.28
  127.5 1.2 add_convert_fusion
  129.8 27.3 %all-gather.4.cloned.1.call-done = bf16[2048,768]{1,0:T(8,128)(2,1)} async-done(((bf16[512,768]{1,0:T(8,128)(2,1)}), bf16[2048,768]{1,0:T(8,128)(2,1)}) %all-gather.4.cloned.1.call-update) | async-done | bytes 3145744 | tf_op jit(solution)/shard_map/all_gather | solution.py:779
  157.1 5.0 fusion.29
  162.1 8.4 %convert_reduce_fusion = (f32[768]{0:T(1024)S(1)}, bf16[2048,768]{1,0:T(8,128)(2,1)S(1)}) fusion(f32[2048,768]{1,0:T(8,128)S(1)} %fusion.29, f32[768]{0:T(1024)S(1)} %dynamic_slice.3, bf16[2048,768]{1,0:T(8,128)(2,1)S(1)} %bitcast.86, bf16[768,768]{1,0:T(8,128)(2,1)S(1)} %copy-done.14), kind=kOutput, calls=%fused_computation.11 | convolution fusion | flops 2458385664 | bytes 13768704 | tf_op jit(solution)/shard_map/sd,fd->sf/dot_general | solution.py:793
  170.6 1.7 copy-done.17
  172.2 4.0 convolution_convert_fusion
  176.3 8.8 %convolution_convert_fusion.1 = bf16[2048,768]{1,0:T(8,128)(2,1)} fusion(bf16[768,768]{1,0:T(8,128)(2,1)} %get-tuple-element.29, f32[2048,768]{1,0:T(8,128)} %copy-done.18, f32[768]{0:T(1024)S(1)} %dynamic_slice.3), kind=kOutput, calls=%fused_computation.14 | convolution fusion | flops 2433220608 | bytes 10619904 | tf_op jit(solution)/shard_map/dot_general | solution.py:785
  185.2 29.1 %reduce-scatter.12.cloned.1.call-done = bf16[512,768]{1,0:T(8,128)(2,1)} async-done(((bf16[2048,768]{1,0:T(8,128)(2,1)}), bf16[512,768]{1,0:T(8,128)(2,1)}) %reduce-scatter.12.cloned.1.call-update) | async-done | bytes 786448 | tf_op jit(solution)/shard_map/reduce_scatter | solution.py:798
  214.3 1.6 fusion.11
  216.8 38.0 %reduce-scatter.10.cloned.1.call-done = bf16[512,768]{1,0:T(8,128)(2,1)} async-done(((bf16[2048,768]{1,0:T(8,128)(2,1)}), bf16[512,768]{1,0:T(8,128)(2,1)}) %reduce-scatter.10.cloned.1.call-update) | async-done | bytes 786448 | tf_op jit(solution)/shard_map/reduce_scatter | solution.py:784
  254.8 3.7 multiply_reduce_fusion.1
  258.5 1.1 copy-done.1
  259.6 1.0 multiply_convert_fusion.1
  260.6 12.1 %reduce-scatter.18.cloned.1.call-start = ((), (), s32[]{:S(2)}) async-start(), calls=%async_computation.14 | async-start | bytes 1327104 | tf_op jit(solution)/shard_map/reduce_scatter | solution.py:848
  272.7 6.6 convolution_convert_fusion.4
  279.4 8.2 %convolution_convert_fusion.3 = bf16[768,768]{0,1:T(8,128)(2,1)} fusion(bf16[2048,768]{1,0:T(8,128)(2,1)} %bitcast.85, f32[2048,768]{1,0:T(8,128)} %copy-done.18, f32[768]{0:T(1024)S(1)} %dynamic_slice.3), kind=kOutput, calls=%fused_computation.43 | convolution fusion | flops 2432237568 | bytes 10619904 | tf_op jit(solution)/shard_map/sf,sd->fd/dot_general | solution.py:794
  287.7 1.6 all-gather.6.cloned.1.call-done
  289.3 2.7 convolution_convert_fusion.6
  292.9 4.0 convolution_convert_fusion.2
  296.9 38.6 %shard_map.223 = bf16[9,64,2048]{2,1,0:T(8,128)(2,1)} custom-call(bf16[9,64,2048]{2,1,0:T(8,128)(2,1)} %get-tuple-element.24.qkv, f32[1,2048]{1,0:T(1,128)} %compare_select_fusion.bias, f32[3,1,2048]{2,1,0:T(1,128)} %get-tuple-element.31.log_total, bf16[3,64,2048]{2,1,0:T(8,128)(2,1)} %get-tuple-element.32.mixed_t, bf16[3,64,2048]{2,1,0:T(8,128)(2,1)} %bitcast.76, ...), custom_call_target="tpu_custom_call" | custom-call | tf_op jit(solution)/shard_map/pallas_call | solution.py:150
  335.6 6.3 convolution_convert_fusion.5
  342.0 33.9 %all_gather.14 = bf16[768,576]{1,0:T(8,128)(2,1)S(1)} all-gather(bf16[96,576]{1,0:T(8,128)(2,1)S(1)} %copy-done.8), channel_id=1, replica_groups=mesh['dp'=4,'row'=2,'col'=4] {'dp','row'}, dimensions={0}, use_global_device_ids=true | all-gather | bytes 995328 | tf_op jit(solution)/shard_map/all_gather | solution.py:770
  376.5 6.0 bitcast_convert_fusion
  383.8 20.5 %all-gather = bf16[8,1,128]{2,1,0:T(2,128)(2,1)S(1)} all-gather(bf16[1,1,128]{2,1,0:T(2,128)(2,1)S(1)} %get-tuple-element.64), channel_id=1, replica_groups=mesh['dp'=4,'row'=2,'col'=4] {'dp','row'}, dimensions={0}, use_global_device_ids=true | all-gather | bytes 2304 | tf_op jit(solution)/shard_map/all_gather | solution.py:771
  404.3 1.6 convert_element_type.130
  405.9 21.2 %reduce-scatter.20.cloned.1.call-done = bf16[768,96]{0,1:T(8,128)(2,1)} async-done(((bf16[768,768]{0,1:T(8,128)(2,1)}), bf16[768,96]{0,1:T(8,128)(2,1)}) %reduce-scatter.20.cloned.1.call-update) | async-done | bytes 147472 | tf_op jit(solution)/shard_map/reduce_scatter | solution.py:849
  427.1 1.6 convert_element_type.133
  428.8 62.8 %reduce-scatter.22.cloned.1.call-done = bf16[96,192]{1,0:T(8,128)(2,1)} async-done(((bf16[768,192]{1,0:T(8,128)(2,1)}), bf16[96,192]{1,0:T(8,128)(2,1)}) %reduce-scatter.22.cloned.1.call-update) | async-done | bytes 36880
  493.1 65.6 %reduce-scatter.16.cloned.1.call-done = bf16[96,3,192]{2,0,1:T(8,128)(2,1)} async-done(((bf16[768,3,192]{2,0,1:T(8,128)(2,1)}), bf16[96,3,192]{2,0,1:T(8,128)(2,1)}) %reduce-scatter.16.cloned.1.call-update) | async-done | bytes 110608 | tf_op jit(solution)/shard_map/reduce_scatter | solution.py:846
  558.7 1.6 convert_element_type.126
  560.4 37.8 %reduce-scatter.14.cloned.1.call-done = bf16[512,768]{1,0:T(8,128)(2,1)} async-done(((bf16[2048,768]{1,0:T(8,128)(2,1)}), bf16[512,768]{1,0:T(8,128)(2,1)}) %reduce-scatter.14.cloned.1.call-update) | async-done | bytes 786448 | tf_op jit(solution)/shard_map/reduce_scatter | solution.py:822
  598.1 1.8 multiply_reduce_fusion.2
  600.9 10.3 %all-reduce.2 = (f32[4608]{0:T(1024)S(1)}, f32[768]{0:T(1024)S(1)}) all-reduce(f32[4608]{0:T(1024)S(1)} %constant_dynamic-update-slice_fusion, f32[768]{0:T(1024)S(1)} %reduce.6), channel_id=1, replica_groups=mesh['dp'=4,'row'=2,'col'=4] {'col'}, use_global_device_ids=true, to_apply=%region_17.18 | all-reduce | flops 5376 | bytes 43008 | tf_op jit(solution)/shard_map/psum | solution.py:833
  611.9 5.6 all-to-all-start
  617.5 2.8 add_bitcast_fusion
  620.4 3.7 all-to-all-done
  624.4 34.5 %all-reduce.1 = (f32[8,128]{1,0:T(8,128)S(1)}, f32[4608]{0:T(1024)}, f32[768]{0:T(1024)}, f32[768]{0:T(1024)}) all-reduce(f32[8,128]{1,0:T(8,128)S(1)} %fusion.16, f32[4608]{0:T(1024)S(1)} %get-tuple-element.52, f32[768]{0:T(1024)S(1)} %get-tuple-element.54, ...), channel_id=5, replica_groups=mesh['dp'=4,'row'=2,'col'=4] {'dp','row'}, use_global_device_ids=true, to_apply=%region_18.19.clone | all-reduce | flops 7168 | bytes 57344
  658.8 1.1 constant_dynamic-slice_fusion
  660.0 1.1 convolution_bitcast_fusion
  (88 shorter events, 12.7 us)
Async XLA Ops:
  7.2 9.1 %copy-start.9 = (f32[768,96]{0,1:T(8,128)S(1)}, f32[768,96]{0,1:T(8,128)}, u32[]{:S(2)}) copy-start(f32[768,96]{0,1:T(8,128)} %param.23) | copy-start | bytes 884740
  7.2 9.7 %copy-start.10 = (f32[128,576]{0,1:T(8,128)S(1)}, f32[128,576]{0,1:T(8,128)}, u32[]{:S(2)}) copy-start(f32[128,576]{0,1:T(8,128)} %param.17) | copy-start | bytes 884740
  7.2 149.9 %all-gather.4.cloned.1.call-start = ((), (), s32[]{:S(2)}) async-start(), calls=%async_computation.8 | async-start | bytes 3932160 | tf_op jit(solution)/shard_map/all_gather | solution.py:779
  63.7 61.8 %copy-start = (f32[1,512,768]{2,1,0:T(8,128)S(1)}, f32[1,512,768]{2,1,0:T(8,128)}, u32[]{:S(2)}) copy-start(f32[1,512,768]{2,1,0:T(8,128)} %param.14) | copy-start | bytes 4718596
  128.7 85.6 %reduce-scatter.12.cloned.1.call-start = ((), (), s32[]{:S(2)}) async-start(), calls=%async_computation.10 | async-start | bytes 3932160 | tf_op jit(solution)/shard_map/reduce_scatter | solution.py:798
  157.1 5.0 copy-start.13
  157.1 5.0 copy-start.14
  162.1 8.4 %copy-start.18 = (f32[2048,768]{1,0:T(8,128)}, f32[2048,768]{1,0:T(8,128)S(1)}, u32[]{:S(2)}) copy-start(f32[2048,768]{1,0:T(8,128)S(1)} %fusion.29) | copy-start | bytes 18874372
  162.1 10.1 %copy-start.15 = (bf16[768,768]{1,0:T(8,128)(2,1)S(1)}, bf16[768,768]{1,0:T(8,128)(2,1)}, u32[]{:S(2)}) copy-start(bf16[768,768]{1,0:T(8,128)(2,1)} %get-tuple-element.28) | copy-start | bytes 3538948
  170.6 1.7 copy-start.17
  176.3 78.5 %reduce-scatter.10.cloned.1.call-start = ((), (), s32[]{:S(2)}) async-start(), calls=%async_computation.9 | async-start | bytes 3932160 | tf_op jit(solution)/shard_map/reduce_scatter | solution.py:784
  185.2 104.1 %all-gather.6.cloned.1.call-start = ((), (), s32[]{:S(2)}) async-start(), calls=%async_computation.11 | async-start | bytes 3932160 | tf_op jit(solution)/shard_map/all_gather | solution.py:808
  214.3 1.6 copy-start.4
  215.9 38.9 %copy-start.11 = (f32[768]{0:T(1024)S(1)}, f32[768]{0:T(1024)}, u32[]{:S(2)}) copy-start(f32[768]{0:T(1024)} %param.24) | copy-start | bytes 9220
  258.5 1.1 copy-start.1
  260.6 143.7 %reduce-scatter.18.cloned.1.call-start = ((), (), s32[]{:S(2)}) async-start(), calls=%async_computation.14 | async-start | bytes 1327104 | tf_op jit(solution)/shard_map/reduce_scatter | solution.py:848
  279.3 10.0 %copy-start.5 = (bf16[3,64,2048]{2,1,0:T(8,128)(2,1)S(1)}, bf16[3,64,2048]{2,1,0:T(8,128)(2,1)}, u32[]{:S(2)}) copy-start(bf16[3,64,2048]{2,1,0:T(8,128)(2,1)} %get-tuple-element.32.mixed_t) | copy-start | bytes 2359300
  279.3 147.8 %reduce-scatter.20.cloned.1.call-start = ((), (), s32[]{:S(2)}) async-start(), calls=%async_computation.15 | async-start | bytes 1327104 | tf_op jit(solution)/shard_map/reduce_scatter | solution.py:849
  287.6 203.9 %reduce-scatter.22.cloned.1.call-start = ((), (), s32[]{:S(2)}) async-start(), calls=%async_computation.16 | async-start | bytes 442368
  289.3 3.6 copy-start.7
  335.5 223.2 %reduce-scatter.16.cloned.1.call-start = ((), (), s32[]{:S(2)}) async-start(), calls=%async_computation.13 | async-start | bytes 1327104 | tf_op jit(solution)/shard_map/reduce_scatter | solution.py:846
  335.6 6.4 copy-start.8
  341.9 256.2 %reduce-scatter.14.cloned.1.call-start = ((), (), s32[]{:S(2)}) async-start(), calls=%async_computation.12 | async-start | bytes 3932160 | tf_op jit(solution)/shard_map/reduce_scatter | solution.py:822
  382.6 0.7 copy-start.16
  382.6 1.2 copy-start.12
  598.1 1.8 copy-start.3
  599.9 17.6 %copy-start.2 = (f32[512,768]{1,0:T(8,128)S(1)}, f32[512,768]{1,0:T(8,128)}, u32[]{:S(2)}) copy-start(f32[512,768]{1,0:T(8,128)} %copy-done.1) | copy-start | bytes 4718596
  611.9 12.2 %all-to-all-start = ((f32[8,1,576]{2,1,0:T(1,128)}), f32[8,1,576]{2,1,0:T(1,128)S(1)}, u32[]{:S(2)}, u32[]{:S(2)}) async-start(f32[8,1,576]{2,1,0:T(1,128)} %all_to_all.8), calls=%async_computation.3 | async-start | bytes 40960 | tf_op jit(solution)/shard_map/all_to_all | solution.py:836
  617.5 6.6 copy-start.6
Sparse Core Ops, SparseCore 0:
  128.8 28.2 all-gather.3
  176.4 37.8 reduce-scatter.11
  216.8 37.8 reduce-scatter.9
  260.8 28.4 all-gather.5
  292.5 66.9 reduce-scatter.17
  362.7 64.3 reduce-scatter.19
  430.4 61.0 reduce-scatter.21
  494.9 63.7 reduce-scatter.15
  561.2 36.8 reduce-scatter.13

commit v3 on v2

--- a/solution.py
+++ b/solution.py
@@ -103,67 +103,6 @@
     lax.fori_loop(0, length // size, step, 0)
 
 
-def attention_backward_kernel(
-    heads, qkv, bias, log_total, mixed_t, back_t, cosine, sine, out, query, key, value, back, key_sum, value_sum
-):
-    length = qkv.shape[2]
-    size = min(512, length)
-    half = HD // 2
-
-    def turn_back(rows, here):
-        c, s = cosine[:, here], sine[:, here]
-        a, b = rows[:half], rows[half:]
-        return jnp.concatenate([a * c + b * s, b * c - a * s], axis=0)
-
-    for h in range(heads):
-        prepare_backward(heads, h, size, length, qkv, bias, log_total, mixed_t, back_t, query, key, value, back)
-    key_sum[...] = jnp.zeros_like(key_sum)
-    value_sum[...] = jnp.zeros_like(value_sum)
-
-    def step(i, _):
-        here = block_at(i, size)
-        for h in range(heads):
-            q, d = query[h, :, here], back[h, :, here]
-            weights = jnp.exp2(contract(key[h], q, 1, 0) * UNIT)
-            grads = (weights * contract(value[h], d, 1, 0)).astype(BF16)
-            value_sum[h] += contract(d[:HD], weights.astype(BF16), 1, 1)
-            key_sum[h] += contract(q[:HD], grads, 1, 1)
-            query_back = contract(qkv[heads + h], grads, 1, 0) * SCALE
-            out[h, :, here] = turn_back(query_back, here).astype(BF16)
-        return 0
-
-    lax.fori_loop(0, length // size, step, 0)
-
-    def finish(i, _):
-        here = block_at(i, size)
-        for h in range(heads):
-            out[heads + h, :, here] = turn_back(key_sum[h, :, here] * SCALE, here).astype(BF16)
-            out[2 * heads + h, :, here] = value_sum[h, :, here].astype(BF16)
-        return 0
-
-    lax.fori_loop(0, length // size, finish, 0)
-
-
-def attention_backward(heads, qkv, bias, log_total, mixed_t, back_t, cosine, sine):
-    length = qkv.shape[2]
-    vmem = pl.BlockSpec(memory_space=pltpu.VMEM)
-    return pl.pallas_call(
-        functools.partial(attention_backward_kernel, heads),
-        out_shape=jax.ShapeDtypeStruct((3 * heads, HD, length), BF16),
-        in_specs=[vmem] * 7,
-        out_specs=vmem,
-        scratch_shapes=[
-            pltpu.VMEM((heads, AUG, length), BF16),
-            pltpu.VMEM((heads, length, AUG), BF16),
-            pltpu.VMEM((heads, length, AUG), BF16),
-            pltpu.VMEM((heads, AUG, length), BF16),
-            pltpu.VMEM((heads, HD, length), F32),
-            pltpu.VMEM((heads, HD, length), F32),
-        ],
-        compiler_params=pltpu.CompilerParams(vmem_limit_bytes=VMEM_LIMIT),
-    )(qkv, bias, log_total, mixed_t, back_t, cosine, sine)
-
-
 MESH = pl.DeviceIdType.MESH
 
 
@@ -271,10 +210,10 @@
 
 
 class ShardScatter:
-    def __init__(self, sizes, total, out_buf, in_buf, sems):
+    def __init__(self, sizes, source, total, out_buf, in_buf, sems):
         self.steps = doubling(sizes)[::-1]
         self.rows = out_buf.shape[1]
-        self.total, self.out_buf, self.in_buf, self.sems = total, out_buf, in_buf, sems
+        self.source, self.total, self.out_buf, self.in_buf, self.sems = source, total, out_buf, in_buf, sems
         self.me = shard_number(sizes)
         self.first = [0]
         for k in range(len(self.steps)):
@@ -292,19 +231,21 @@
         peer = {axis: flip(lax.axis_index(axis), bit)}
         return send_copy(self.out_buf.at[at], self.in_buf.at[at], self.sems.at[0, at], self.sems.at[1, at], peer)
 
+    def held(self, k):
+        return self.source if k == 0 else self.total
+
     def start(self, k):
         stride = self.steps[k][2]
         for i, kept in enumerate(self.rest(k)):
             number = flips(self.me, (stride,) + kept)
-            self.out_buf[self.first[k] + i] = self.total[self.part(number), :].astype(BF16)
-            copy = self.copy(k, i)
-            copy.start()
+            self.out_buf[self.first[k] + i] = self.held(k)[self.part(number), :].astype(BF16)
+            self.copy(k, i).start()
 
     def arrived(self, k):
         for i, kept in enumerate(self.rest(k)):
             self.copy(k, i).wait_recv()
             here = self.part(flips(self.me, kept))
-            self.total[here, :] = self.total[here, :] + self.in_buf[self.first[k] + i].astype(F32)
+            self.total[here, :] = self.held(k)[here, :].astype(F32) + self.in_buf[self.first[k] + i].astype(F32)
 
     def advance(self, k):
         if 0 < k <= len(self.steps):
@@ -312,6 +253,9 @@
         if k < len(self.steps):
             self.start(k)
 
+    def result(self):
+        return self.total[self.part(self.me), :]
+
     def close(self):
         for k in range(len(self.steps)):
             for i in range(len(self.rest(k))):
@@ -320,6 +264,7 @@
     @staticmethod
     def scratch(count, rows, width):
         return [
+            pltpu.VMEM((count * rows, width), F32),
             pltpu.VMEM((count - 1, rows, width), BF16),
             pltpu.VMEM((count - 1, rows, width), BF16),
             pltpu.SemaphoreType.DMA((2, count - 1)),
@@ -456,8 +401,8 @@
 def start_kernel(
     sizes, heads, chunks,
     condition, condition_weight, condition_bias, tokens, in_shard, out_shard, cosine, sine, cotangent, valid,
-    modulation, normed, qkv, out_full, feed_back, bias_part,
-    condition_all, pieces, arrived, in_full, out_t, in_t, unit, sems_tiny, sems_in, sems_out, sems_col,
+    modulation, normed, qkv, out_full, feed_back, bias_part, in_t, condition_all,
+    pieces, arrived, in_full, out_t, unit, sems_tiny, sems_in, sems_out, sems_col,
 ):
     count = sizes["dp"] * sizes["row"]
     number = shard_number(sizes)
@@ -600,16 +545,16 @@
             jax.ShapeDtypeStruct((local, width), BF16),
             jax.ShapeDtypeStruct((rows, width), BF16),
             jax.ShapeDtypeStruct((1, width), F32),
+            jax.ShapeDtypeStruct((3 * local, width), BF16),
+            jax.ShapeDtypeStruct((count,) + condition.shape, F32),
         ],
         in_specs=[vmem] * 10,
-        out_specs=[vmem] * 6,
+        out_specs=[vmem] * 8,
         scratch_shapes=[
-            pltpu.VMEM((count,) + condition.shape, F32),
             pltpu.VMEM((count, 1, piece), F32),
             pltpu.VMEM((count, 1, piece), F32),
             pltpu.VMEM((width, 3 * local), BF16),
             pltpu.VMEM((width, local), BF16),
-            pltpu.VMEM((3 * local, width), BF16),
             pltpu.VMEM((rows, width), F32),
             pltpu.SemaphoreType.DMA((4, count - 1)),
             ShardGather.semaphores(count),
@@ -722,6 +667,264 @@
     )(qkv, bias, out_full, feed_back, up_shard, down_shard)
 
 
+def contract_exact(left, right, left_axis, right_axis):
+    return lax.dot_general(
+        left,
+        right,
+        (((left_axis,), (right_axis,)), ((), ())),
+        precision=lax.Precision.HIGHEST,
+        preferred_element_type=F32,
+    )
+
+
+def finish_kernel(
+    sizes, heads, chunks,
+    qkv, bias, log_total, mixed_t, back_t, cosine, sine, normed, in_t, up_source, down_source, out_source,
+    tokens, middle_back, parts, others, down_part, up_part, condition_all, condition_weight,
+    tokens_back, condition_back, condition_grad, bias_grad, up_bias, down_bias, in_grad, out_grad, up_grad, down_grad,
+    turned, query, key, value, back, key_sum, value_sum, in_source,
+    in_total, in_out, in_in, in_sems, up_total, up_out, up_in, up_sems,
+    down_total, down_out, down_in, down_sems, out_total, out_out, out_in, out_sems,
+    pair_out, pair_in, far_out, far_in, kept, col_sems,
+    line_out, line_in, up_all, pieces, arrived, backs, collected, tiny_sems, line_sems,
+):
+    count = sizes["dp"] * sizes["row"]
+    number = shard_number(sizes)
+    length = qkv.shape[2]
+    rows, width = tokens.shape
+    half = HD // 2
+    piece = condition_weight.shape[1]
+    cond = condition_weight.shape[0]
+    peers = other_peers(sizes)
+    greet([peer for _, peer in peers] + col_peers())
+    me = lax.axis_index("col")
+    near, far = col_peers()
+    scatter_up = ShardScatter(sizes, up_source, up_total, up_out, up_in, up_sems)
+    scatter_down = ShardScatter(sizes, down_source, down_total, down_out, down_in, down_sems)
+    scatter_out = ShardScatter(sizes, out_source, out_total, out_out, out_in, out_sems)
+    scatter_in = ShardScatter(sizes, in_source, in_total, in_out, in_in, in_sems)
+    column = ColumnScatter(pair_out, pair_in, far_out, far_in, kept, chunks, col_sems)
+
+    def tiny(kind, i, source, target):
+        return send_copy(source, target, tiny_sems.at[0, kind, i], tiny_sems.at[1, kind, i], peers[i][1])
+
+    def up_copy(i, slot):
+        return tiny(0, i, up_part, up_all.at[slot])
+
+    def piece_copy(i, mine, slot):
+        return tiny(1, i, pieces.at[mine], arrived.at[slot])
+
+    def back_copy(i, mine, slot):
+        return tiny(2, i, backs.at[mine], collected.at[slot])
+
+    def line_copy(k):
+        return send_copy(line_out.at[k], line_in.at[k], line_sems.at[0, k], line_sems.at[1, k], (near, far)[k])
+
+    scatter_up.start(0)
+    scatter_down.start(0)
+    scatter_out.start(0)
+    for i in range(count - 1):
+        up_copy(i, number).start()
+    up_all[number] = up_part[...]
+
+    def turn_back(values, here):
+        c, s = cosine[:, here], sine[:, here]
+        a, b = values[:half], values[half:]
+        return jnp.concatenate([a * c + b * s, b * c - a * s], axis=0)
+
+    for h in range(heads):
+        prepare_backward(heads, h, rows, length, qkv, bias, log_total, mixed_t, back_t, query, key, value, back)
+    key_sum[...] = jnp.zeros_like(key_sum)
+    value_sum[...] = jnp.zeros_like(value_sum)
+
+    def step(i, _):
+        here = block_at(i, rows)
+        for h in range(heads):
+            q, d = query[h, :, here], back[h, :, here]
+            weights = jnp.exp2(contract(key[h], q, 1, 0) * UNIT)
+            grads = (weights * contract(value[h], d, 1, 0)).astype(BF16)
+            value_sum[h] += contract(d[:HD], weights.astype(BF16), 1, 1)
+            key_sum[h] += contract(q[:HD], grads, 1, 1)
+            query_back = contract(qkv[heads + h], grads, 1, 0) * SCALE
+            turned[h, :, here] = turn_back(query_back, here).astype(BF16)
+
+        @pl.when(i == 1)
+        def _():
+            scatter_up.advance(1)
+
+        @pl.when(i == 2)
+        def _():
+            scatter_down.advance(1)
+            scatter_out.advance(1)
+            scatter_up.advance(2)
+
+        return 0
+
+    lax.fori_loop(0, 4, step, 0)
+
+    def finish_block(i, _):
+        here = block_at(i, rows)
+        for h in range(heads):
+            turned[heads + h, :, here] = turn_back(key_sum[h, :, here] * SCALE, here).astype(BF16)
+            turned[2 * heads + h, :, here] = value_sum[h, :, here].astype(BF16)
+        return 0
+
+    lax.fori_loop(0, 4, finish_block, 0)
+    scatter_down.advance(2)
+    scatter_out.advance(2)
+    in_source[...] = contract(
+        normed[...], turned[...].reshape(3 * heads * HD, length), 0, 1
+    )
+    scatter_in.start(0)
+    size = rows // chunks
+
+    def part_of(slot, j):
+        start_at = pl.multiple_of(slot * rows + j * size, size)
+        block = turned[:, :, pl.ds(start_at, size)].reshape(3 * heads * HD, size)
+        return contract(block, in_t[...], 0, 0)
+
+    for j in range(chunks):
+        column.give_diagonal(j, part_of(flips(me, (1, 2)), j))
+    for j in range(chunks):
+        column.give_across(j, part_of(flip(me, 2), j))
+    scatter_up.advance(3)
+    for j in range(chunks):
+        column.give_partner(j, part_of(flip(me, 1), j))
+    scatter_in.advance(1)
+    for j in range(chunks):
+        column.give_own(j, part_of(me, j))
+    scatter_down.advance(3)
+    scatter_out.advance(3)
+    scatter_in.advance(2)
+    shift_sum = jnp.zeros((1, width), F32)
+    scale_sum = jnp.zeros((1, width), F32)
+    for j in range(chunks):
+        here = pl.ds(j * size, size)
+        own = tokens[here, :]
+        center = own - jnp.mean(own, axis=-1, keepdims=True)
+        inverse = lax.rsqrt(jnp.mean(center * center, axis=-1, keepdims=True) + EPSILON)
+        unit = center * inverse
+        grad = column.result(j)
+        scaled = grad * (1.0 + parts[1:2, :])
+        inner = scaled - jnp.mean(scaled, axis=-1, keepdims=True) - unit * jnp.mean(scaled * unit, axis=-1, keepdims=True)
+        tokens_back[here, :] = middle_back[here, :] + inverse * inner
+        shift_sum = shift_sum + jnp.sum(grad, axis=0, keepdims=True)
+        scale_sum = scale_sum + jnp.sum(grad * unit, axis=0, keepdims=True)
+    line_out[0] = jnp.concatenate([shift_sum, scale_sum, others[...], down_part[...]], axis=1)
+    line_copy(0).start()
+    scatter_in.advance(3)
+    steps = len(scatter_in.steps)
+    for k in range(4, steps + 1):
+        for one in (scatter_up, scatter_down, scatter_out, scatter_in):
+            one.advance(k)
+    line_copy(0).wait_recv()
+    line_out[1] = line_out[0] + line_in[0]
+    line_copy(1).start()
+    up_grad[...] = scatter_up.result()
+    down_grad[...] = scatter_down.result()
+    out_grad[...] = scatter_out.result()
+    in_grad[...] = scatter_in.result()
+    for i in range(count - 1):
+        up_copy(i, peers[i][0]).wait_recv()
+    up_bias[...] = jnp.sum(jnp.concatenate([up_all[b] for b in range(count)], axis=0), axis=0, keepdims=True)
+    line_copy(1).wait_recv()
+    line = line_out[1] + line_in[1]
+    split = 6 * width
+    for b in range(count):
+        pieces[b] = jnp.concatenate([line[:, b * piece : (b + 1) * piece], line[:, split:]], axis=1)
+    for i in range(count - 1):
+        piece_copy(i, peers[i][0], number).start()
+    arrived[number] = pieces[number]
+    for i in range(count - 1):
+        piece_copy(i, number, peers[i][0]).wait_recv()
+    stacked = jnp.concatenate([arrived[b] for b in range(count)], axis=0)
+    mine = stacked[:, :piece]
+    down_bias[...] = jnp.sum(stacked[:, piece:], axis=0, keepdims=True)
+    bias_piece = jnp.sum(mine, axis=0, keepdims=True)
+    back_rows = contract_exact(mine, condition_weight[...].astype(F32), 1, 1)
+    for b in range(count):
+        backs[b] = jnp.concatenate([back_rows[b : b + 1], bias_piece], axis=1)
+    for i in range(count - 1):
+        back_copy(i, peers[i][0], number).start()
+    collected[number] = backs[number]
+    conditions = jnp.concatenate([condition_all[b] for b in range(count)], axis=0)
+    condition_grad[...] = contract_exact(conditions, mine, 0, 0)
+    for i in range(count - 1):
+        back_copy(i, number, peers[i][0]).wait_recv()
+    gathered = [collected[b] for b in range(count)]
+    bias_grad[...] = jnp.concatenate([one[:, cond:] for one in gathered], axis=1)
+    condition_back[...] = jnp.sum(
+        jnp.concatenate([one[:, :cond] for one in gathered], axis=0), axis=0, keepdims=True
+    )
+    for i in range(count - 1):
+        up_copy(i, number).wait_send()
+        piece_copy(i, peers[i][0], number).wait_send()
+        back_copy(i, peers[i][0], number).wait_send()
+    for k in range(2):
+        line_copy(k).wait_send()
+    for one in (scatter_up, scatter_down, scatter_out, scatter_in):
+        one.close()
+    column.close()
+
+
+def finish(sizes, heads, qkv, bias, log_total, mixed_t, back_t, cosine, sine, normed, in_t, up_source, down_source,
+           out_source, tokens, middle_back, parts, others, down_part, up_part, condition_all, condition_weight):
+    count = sizes["dp"] * sizes["row"]
+    length = qkv.shape[2]
+    rows, width = tokens.shape
+    chunks = 2
+    local = heads * HD
+    hidden = up_source.shape[1]
+    cond, piece = condition_weight.shape
+    share = width // count
+    vmem = pl.BlockSpec(memory_space=pltpu.VMEM)
+    return pl.pallas_call(
+        functools.partial(finish_kernel, sizes, heads, chunks),
+        out_shape=[
+            jax.ShapeDtypeStruct((rows, width), F32),
+            jax.ShapeDtypeStruct((1, cond), F32),
+            jax.ShapeDtypeStruct((cond, piece), F32),
+            jax.ShapeDtypeStruct((1, 6 * width), F32),
+            jax.ShapeDtypeStruct((1, hidden), F32),
+            jax.ShapeDtypeStruct((1, width), F32),
+            jax.ShapeDtypeStruct((share, 3 * local), F32),
+            jax.ShapeDtypeStruct((share, local), F32),
+            jax.ShapeDtypeStruct((share, hidden), F32),
+            jax.ShapeDtypeStruct((share, hidden), F32),
+        ],
+        in_specs=[vmem] * 20,
+        out_specs=[vmem] * 10,
+        scratch_shapes=[
+            pltpu.VMEM((3 * heads, HD, length), BF16),
+            pltpu.VMEM((heads, AUG, length), BF16),
+            pltpu.VMEM((heads, length, AUG), BF16),
+            pltpu.VMEM((heads, length, AUG), BF16),
+            pltpu.VMEM((heads, AUG, length), BF16),
+            pltpu.VMEM((heads, HD, length), F32),
+            pltpu.VMEM((heads, HD, length), F32),
+            pltpu.VMEM((width, 3 * local), F32),
+            *ShardScatter.scratch(count, share, 3 * local),
+            *ShardScatter.scratch(count, share, hidden),
+            *ShardScatter.scratch(count, share, hidden),
+            *ShardScatter.scratch(count, share, local),
+            *ColumnScatter.scratch(rows, width, chunks),
+            pltpu.VMEM((2, 1, 7 * width), F32),
+            pltpu.VMEM((2, 1, 7 * width), F32),
+            pltpu.VMEM((count, 1, hidden), F32),
+            pltpu.VMEM((count, 1, piece + width), F32),
+            pltpu.VMEM((count, 1, piece + width), F32),
+            pltpu.VMEM((count, 1, cond + piece), F32),
+            pltpu.VMEM((count, 1, cond + piece), F32),
+            pltpu.SemaphoreType.DMA((2, 3, count - 1)),
+            pltpu.SemaphoreType.DMA((2, 2)),
+        ],
+        compiler_params=pltpu.CompilerParams(
+            vmem_limit_bytes=VMEM_LIMIT, collective_id=2, has_side_effects=True
+        ),
+    )(qkv, bias, log_total, mixed_t, back_t, cosine, sine, normed, in_t, up_source, down_source, out_source,
+      tokens, middle_back, parts, others, down_part, up_part, condition_all, condition_weight)
+
+
 def shards(
     sizes,
     tokens,
@@ -744,7 +947,6 @@
     length_all = rows * columns
     local_width = attention_in.shape[2]
     heads = local_width // HD
-    group = ("dp", "row")
     in_shard = attention_in.reshape(attention_in.shape[0], 3 * local_width).astype(BF16)
     out_shard = attention_out.T.astype(BF16)
     up_shard = up_weight.astype(BF16)
@@ -757,18 +959,14 @@
     valid = (position < length).astype(F32)
     bias = jnp.where(jnp.arange(length_all) < length, 0.0, MASKED).astype(F32)[None]
     cosine, sine = (jnp.asarray(table) for table in rotary_tables(length_all))
-    parts, normed_blocks, qkv, out_full, feed_back, down_bias_part = start(
+    parts, normed_blocks, qkv, out_full, feed_back, down_bias_part, in_t, condition_all = start(
         sizes, heads, condition_low.astype(F32), weight_low, condition_bias[None], own_rows,
         in_shard, out_shard, cosine, sine, cotangent[0], valid[:, None],
     )
-    down_bias_part = down_bias_part[0]
     normed_all = normed_blocks.reshape(length_all, width)
-    _, first_pull = jax.vjp(norm_shift, own_rows, parts[0], parts[1])
     attention, mixed_t, log_total, feed_back_blocks, up_full, down_t = attend(
         sizes, heads, qkv, bias, out_full, feed_back, up_shard, down_shard
     )
-    in_full = lax.all_gather(in_shard, group, axis=0, tiled=True).reshape(width, 3, local_width)
-    condition_all = lax.all_gather(condition_low, group, axis=0, tiled=True)
     mixed_rows = mixed_t.reshape(local_width, length_all)
     down_full = down_t.T
     feed_back_all = feed_back_blocks.reshape(length_all, width)
@@ -791,7 +989,7 @@
     incoming = cotangent[0] * valid[:, None]
     gate_feed = jnp.sum(incoming * (feed + down_bias), axis=0)
     hidden_back = jnp.einsum("sd,fd->sf", feed_back_all, down_full, preferred_element_type=F32)
-    down_grad = jnp.einsum("sf,sd->fd", hidden_low, feed_back_all, preferred_element_type=F32)
+    down_grad = jnp.einsum("sd,sf->df", feed_back_all, hidden_low, preferred_element_type=F32)
     before_back = gelu_pull(hidden_back)[0].astype(BF16)
     up_grad = jnp.einsum("sd,sf->df", second_all, before_back, preferred_element_type=F32)
     up_bias_part = jnp.sum(before_back.astype(F32), axis=0)
@@ -806,63 +1004,29 @@
     gate_attention = jnp.sum(middle_back * attention, axis=0)
     attention_back = (parts[2] * middle_back).astype(BF16)
     attention_back_all = lax.all_gather(attention_back, "col", axis=0, tiled=True)
-    out_grad = jnp.einsum("cs,sd->cd", mixed_rows, attention_back_all, preferred_element_type=F32)
+    out_grad = jnp.einsum("sd,cs->dc", attention_back_all, mixed_rows, preferred_element_type=F32)
     mixed_back = jnp.einsum("sd,cd->cs", attention_back_all, out_full, preferred_element_type=F32)
-    projected_back = attention_backward(
-        heads,
-        qkv,
-        bias,
-        log_total,
-        mixed_t,
-        mixed_back.astype(BF16).reshape(heads, HD, length_all),
-        cosine,
-        sine,
-    ).reshape(3, local_width, length_all)
-    in_grad = jnp.einsum("sd,tes->dte", normed_all, projected_back, preferred_element_type=F32)
-    normed_back = lax.psum_scatter(
-        jnp.einsum("tes,dte->sd", projected_back, in_full, preferred_element_type=F32).astype(BF16),
-        "col",
-        scatter_dimension=0,
-        tiled=True,
-    ).astype(F32)
-    rows_part, shift_attention, scale_attention = first_pull(normed_back)
-    tokens_back = middle_back + rows_part
-    modulation_part = jnp.concatenate(
-        [shift_attention, scale_attention, gate_attention, shift_feed, scale_feed, gate_feed]
-    )
-    modulation_back, down_bias_column = lax.psum((modulation_part, down_bias_part), "col")
-    count = lax.axis_size(group)
-    spread = modulation_back.reshape(count, -1)
-    mine = lax.all_to_all(spread, group, 0, 0, tiled=True)
-    highest = lax.Precision.HIGHEST
-    condition_grad = jnp.einsum("bc,bm->cm", condition_all.astype(F32), mine, precision=highest)
-    condition_back = lax.psum_scatter(
-        jnp.einsum("bm,cm->bc", mine, weight_low.astype(F32), precision=highest),
-        group,
-        scatter_dimension=0,
-        tiled=True,
-    )
-    in_grad, out_grad, up_grad, down_grad = (
-        lax.psum_scatter(in_grad.astype(BF16), group, scatter_dimension=0, tiled=True).astype(F32),
-        lax.psum_scatter(out_grad.astype(BF16), group, scatter_dimension=1, tiled=True).astype(F32),
-        lax.psum_scatter(up_grad.astype(BF16), group, scatter_dimension=0, tiled=True).astype(F32),
-        lax.psum_scatter(down_grad.astype(BF16), group, scatter_dimension=1, tiled=True).astype(F32),
-    )
-    bias_grad, up_bias_grad, down_bias_grad = lax.psum(
-        (modulation_back, up_bias_part, down_bias_column), group
+    others = jnp.concatenate([gate_attention, shift_feed, scale_feed, gate_feed])[None]
+    (
+        tokens_back, condition_back, condition_grad, bias_grad, up_bias_grad, down_bias_grad,
+        in_grad, out_grad, up_grad, down_grad,
+    ) = finish(
+        sizes, heads, qkv, bias, log_total, mixed_t, mixed_back.astype(BF16).reshape(heads, HD, length_all),
+        cosine, sine, normed_all, in_t, up_grad, down_grad, out_grad, own_rows, middle_back, parts,
+        others, down_bias_part, up_bias_part[None], condition_all, weight_low,
     )
     return (
         result[None],
         tokens_back[None],
         condition_back,
         condition_grad,
-        bias_grad,
-        in_grad,
-        out_grad,
+        bias_grad[0],
+        in_grad.reshape(attention_in.shape),
+        out_grad.T,
         up_grad,
-        up_bias_grad,
-        down_grad,
-        down_bias_grad,
+        up_bias_grad[0],
+        down_grad.T,
+        down_bias_grad[0],
     )
 
 

time: 675 us -> 408 us (0.60)
  waiting for transfers between devices: 287 us -> 113 us
  blocking collectives: 99.1 us -> 0 us
  Pallas kernels: 145 us -> 197 us
  matrix products: 61.5 us -> 41.6 us
  starting transfers between devices: 18.3 us -> 0.55 us
  other arithmetic: 28.4 us -> 18.2 us
    reduce_scatter x4 -> x0, waiting for transfers between devices: 125 us -> none  [the longest x1 65.6 us: shards(): lax.psum_scatter(in_grad.astype(BF16), group, scatter_dimension=0, tiled=...]
    unnamed x10 -> x4, waiting for transfers between devices: 62.9 us -> 0.07 us
    all_gather x2 -> x0, blocking collectives: 54.4 us -> none  [the longest x1 33.9 us: shards(): lax.all_gather(in_shard, group, axis=0, tiled=True)]
    pallas_call x1, Pallas kernels: 38.6 us -> 91.5 us  [finish(): pl.pallas_call(functools.partial(finish_kernel, sizes, heads, chunks), ou...]
    unnamed x1 -> x0, blocking collectives: 34.5 us -> none
    dot_general x6 -> x2, matrix products: 24.6 us -> 8.97 us  [the longest x1 7.05 us: shards(): jnp.einsum('sd,sf->df', feed_back_all, hidden_low, preferred_element_type...]
    all_gather x1, waiting for transfers between devices: 1.62 us -> 16 us  [shards(): lax.all_gather(attention_back, 'col', axis=0, tiled=True)]
    reduce_scatter x4 -> x0, starting transfers between devices: 12.2 us -> none  [the longest x1 12.1 us: shards(): lax.psum_scatter(up_grad.astype(BF16), group, scatter_dimension=0, tiled=...]
  transfers between devices with their start and end apart: 10 -> 4, of which waited for: 9 -> 4; matrix products, arithmetic and copies ran while one was open for 9% -> 6% of each run, Pallas kernels for 6% -> 0%
where the time goes in v3:
time: 408 us; the launch traced here: 402 us
  Pallas kernels  197 us (48%)
  waiting for transfers between devices  113 us (28%)
  matrix products  41.6 us (10%)
  other arithmetic  18.2 us (4%)
  local copies, waits for them, and re-layouts  16 us (4%)
  between operations  15.2 us (4%)
    pallas_call x1, Pallas kernels, finish(): pl.pallas_call(functools.partial(finish_kernel, sizes, heads, chunks), ou...  91.5 us
    pallas_call x1, Pallas kernels, attend(): pl.pallas_call(functools.partial(attention_kernel, sizes, heads, chunks),...  61.7 us
    pallas_call x1, Pallas kernels, start(): pl.pallas_call(functools.partial(start_kernel, sizes, heads, chunks), out...  44.3 us
    reduce_scatter x1, waiting for transfers between devices, shards(): lax.psum_scatter(jnp.dot(hidden_low, down_full, preferred_element_type=F3...  37.8 us
    reduce_scatter x1, waiting for transfers between devices, shards(): lax.psum_scatter(jnp.einsum('sf,df->sd', before_back, up_full, preferred_...  31.5 us
    all_gather x1, waiting for transfers between devices, shards(): second_all = lax.all_gather(second_low, 'col', axis=0, tiled=True)  27.4 us
    all_gather x1, waiting for transfers between devices, shards(): lax.all_gather(attention_back, 'col', axis=0, tiled=True)  16 us
    unnamed x59, local copies, waits for them, and re-layouts  11.9 us
  transfers between devices with their start and end apart: 4, of which 4 were waited for; matrix products, arithmetic and copies ran while one was open for 6% of the time, Pallas kernels for 0%

profile of v3, /device:TPU:0, one launch (start us, length us, event | category | flops | bytes accessed | tf_op | source)
XLA Modules:
  0.0 401.7 jit_solution(3316644667397707025)
XLA Ops:
  8.0 1.8 copy.41.condition_weight
  9.7 1.0 convert_element_type.73
  10.9 0.8 copy.45.in_shard
  11.7 1.6 copy.43
  13.3 0.6 broadcast_in_dim.38.condition_bias
  13.9 0.5 convert_convert_fusion.condition
  14.4 0.6 compare_select_fusion.bias
  15.0 0.7 convert_bitcast_fusion.down_shard
  15.7 0.7 convert_element_type.78.up_shard
  16.4 0.7 fusion.10.valid
  17.1 44.3 %shard_map.221 = (f32[6,768]{1,0:T(8,128)}, bf16[4,512,768]{2,1,0:T(8,128)(2,1)}, bf16[9,64,2048]{2,1,0:T(8,128)(2,1)}, bf16[192,768]{1,0:T(8,128)(2,1)}, bf16[5...) custom-call(f32[1,128]{1,0:T(1,128)} %convert_convert_fusion.condition, ...), custom_call_target="tpu_custom_call" | custom-call | tf_op jit(solution)/shard_map/pallas_call | solution.py:539
  61.4 0.9 slice_reduce_fusion.1
  62.3 61.7 %shard_map.222 = (f32[512,768]{1,0:T(8,128)}, bf16[3,64,2048]{2,1,0:T(8,128)(2,1)}, f32[3,1,2048]{2,1,0:T(1,128)}, bf16[4,512,768]{2,1,0:T(8,128)(2,1)}, bf16[76...) custom-call(bf16[9,64,2048]{2,1,0:T(8,128)(2,1)} %get-tuple-element.36.qkv, f32[1,2048]{1,0:T(1,128)} %compare_select_fusion.bias, ...), custom_call_target="tpu_custom_call" | custom-call | tf_op jit(solution)/shard_map/pallas_call | solution.py:644
  124.1 1.7 fusion.15
  125.8 0.3 multiply_reduce_fusion.2
  126.1 1.2 add_convert_fusion
  127.5 0.8 dynamic_slice.3
  128.3 27.4 %all-gather.3.cloned.1.call-done = bf16[2048,768]{1,0:T(8,128)(2,1)} async-done(((bf16[512,768]{1,0:T(8,128)(2,1)}), bf16[2048,768]{1,0:T(8,128)(2,1)}) %all-gather.3.cloned.1.call-update) | async-done | bytes 3145744 | tf_op jit(solution)/shard_map/all_gather | solution.py:977
  155.7 5.0 %fusion.16 = f32[2048,768]{1,0:T(8,128)S(1)} fusion(bf16[2048,768]{1,0:T(8,128)(2,1)} %all-gather.3.cloned.1.call-done, bf16[768,768]{1,0:T(8,128)(2,1)} %get-tuple-element.40), kind=kOutput, calls=%fused_computation.52 | convolution fusion | flops 2415919104 | bytes 10616832 | tf_op jit(solution)/shard_map/dot_general | solution.py:979
  160.8 9.0 %convert_reduce_fusion = (f32[768]{0:T(1024)S(1)}, bf16[2048,768]{1,0:T(8,128)(2,1)S(1)}, bf16[2048,768]{1,0:T(8,128)(2,1)}) fusion(f32[2048,768]{1,0:T(8,128)S(1)} %fusion.16, f32[768]{0:T(1024)S(1)} %dynamic_slice.3, bf16[2048,768]{1,0:T(8,128)(2,1)S(1)} %bitcast.58, bf16[768,768]{1,0:T(8,128)(2,1)S(1)} %copy-done.19), kind=kOutput, calls=%fused_computation.10 | convolution fusion | flops 2461531392 | bytes 16914432 | tf_op jit(solution)/shard_map/sd,fd->sf/dot_general | solution.py:991
  169.7 1.6 copy-done.23
  171.4 4.0 %convolution_convert_fusion = bf16[2048,768]{1,0:T(8,128)(2,1)} fusion(bf16[2048,768]{1,0:T(8,128)(2,1)S(1)} %get-tuple-element.101, bf16[768,768]{1,0:T(8,128)(2,1)S(1)} %copy-done.20), kind=kOutput, calls=%fused_computation.12 | convolution fusion | flops 2417491968 | bytes 7471104 | tf_op jit(solution)/shard_map/sf,df->sd/dot_general | solution.py:997
  175.5 6.2 %convolution_convert_fusion.1 = bf16[2048,768]{1,0:T(8,128)(2,1)} fusion(bf16[2048,768]{1,0:T(8,128)(2,1)} %get-tuple-element.106, bf16[768,768]{1,0:T(8,128)(2,1)S(1)} %copy-done.19), kind=kOutput, calls=%fused_computation.13 | convolution fusion | flops 2417491968 | bytes 7471104 | tf_op jit(solution)/shard_map/dot_general | solution.py:983
  182.0 31.5 %reduce-scatter.5.cloned.1.call-done = bf16[512,768]{1,0:T(8,128)(2,1)} async-done(((bf16[2048,768]{1,0:T(8,128)(2,1)}), bf16[512,768]{1,0:T(8,128)(2,1)}) %reduce-scatter.5.cloned.1.call-update) | async-done | bytes 786448 | tf_op jit(solution)/shard_map/reduce_scatter | solution.py:996
  213.5 1.7 convert_reduce_fusion.1
  215.3 0.9 fusion.9
  216.1 37.8 %reduce-scatter.3.cloned.1.call-done = bf16[512,768]{1,0:T(8,128)(2,1)} async-done(((bf16[2048,768]{1,0:T(8,128)(2,1)}), bf16[512,768]{1,0:T(8,128)(2,1)}) %reduce-scatter.3.cloned.1.call-update) | async-done | bytes 786448 | tf_op jit(solution)/shard_map/reduce_scatter | solution.py:982
  253.9 3.7 multiply_reduce_fusion.1
  257.6 1.1 multiply_convert_fusion.1
  259.0 0.6 broadcast_in_dim.45.up_part
  259.6 7.0 %fusion.18.down_source = f32[768,768]{1,0:T(8,128)} fusion(bf16[2048,768]{1,0:T(8,128)(2,1)} %bitcast.57, bf16[2048,768]{1,0:T(8,128)(2,1)} %get-tuple-element.106), kind=kOutput, calls=%fused_computation.54 | convolution fusion | flops 2415919104 | bytes 8650752 | tf_op jit(solution)/shard_map/sd,sf->df/dot_general | solution.py:992
  266.7 4.2 %fusion.17.up_source = f32[768,768]{1,0:T(8,128)} fusion(bf16[2048,768]{1,0:T(8,128)(2,1)S(1)} %copy-done.18, bf16[2048,768]{1,0:T(8,128)(2,1)S(1)} %copy-done.24), kind=kOutput, calls=%fused_computation.53 | convolution fusion | flops 2415919104 | bytes 8650752 | tf_op jit(solution)/shard_map/sd,sf->df/dot_general | solution.py:994
  270.9 0.6 pad_maximum_fusion
  271.5 16.0 %all-gather.5.cloned.1.call-done = bf16[2048,768]{1,0:T(8,128)(2,1)} async-done(((bf16[512,768]{1,0:T(8,128)(2,1)}), bf16[2048,768]{1,0:T(8,128)(2,1)}) %all-gather.5.cloned.1.call-update) | async-done | bytes 3145744 | tf_op jit(solution)/shard_map/all_gather | solution.py:1006
  287.5 4.1 %convolution_convert_fusion.2 = bf16[192,2048]{1,0:T(8,128)(2,1)} fusion(bf16[192,768]{1,0:T(8,128)(2,1)S(1)} %copy-done.5, bf16[2048,768]{1,0:T(8,128)(2,1)} %all-gather.5.cloned.1.call-done), kind=kOutput, calls=%fused_computation.14 | convolution fusion | flops 604372992 | bytes 4227072 | tf_op jit(solution)/shard_map/sd,cd->cs/dot_general | solution.py:1008
  291.6 1.9 fusion.19.out_source
  293.5 91.5 %shard_map.223 = (f32[512,768]{1,0:T(8,128)}, f32[1,128]{1,0:T(1,128)}, f32[128,576]{1,0:T(8,128)}, f32[1,4608]{1,0:T(1,128)}, f32[1,768]{1,0:T(1,128)}, /*index...) custom-call(bf16[9,64,2048]{2,1,0:T(8,128)(2,1)} %get-tuple-element.36.qkv, ...), custom_call_target="tpu_custom_call" | custom-call | tf_op jit(solution)/shard_map/pallas_call | solution.py:881
  385.0 1.2 copy.47
  386.3 0.9 copy.49
  387.1 1.8 copy.48
  389.0 0.7 copy.50
  389.7 0.7 reduce.4
  390.4 0.6 reduce.5
  391.0 0.6 reduce.6
  391.6 1.1 copy.57
  392.8 0.5 copy.58
  393.3 0.7 copy.59
  394.0 0.7 copy.60
  (63 shorter events, 1.1 us)
Async XLA Ops:
  7.2 6.1 %copy-start.12 = (f32[4608]{0:T(1024)S(1)}, f32[4608]{0:T(1024)}, u32[]{:S(2)}) copy-start(f32[4608]{0:T(1024)} %param.18) | copy-start | bytes 55300
  7.2 6.7 %copy-start.21 = (f32[1,128]{1,0:T(1,128)S(1)}, f32[1,128]{1,0:T(1,128)}, u32[]{:S(2)}) copy-start(f32[1,128]{1,0:T(1,128)} %param.15) | copy-start | bytes 1540
  7.2 7.8 %copy-start.7 = (f32[768,96]{0,1:T(8,128)S(1)}, f32[768,96]{0,1:T(8,128)}, u32[]{:S(2)}) copy-start(f32[768,96]{0,1:T(8,128)} %param.23) | copy-start | bytes 884740
  7.2 8.5 %copy-start.8 = (f32[96,768]{1,0:T(8,128)S(1)}, f32[96,768]{1,0:T(8,128)}, u32[]{:S(2)}) copy-start(f32[96,768]{1,0:T(8,128)} %param.21) | copy-start | bytes 884740
  7.2 148.5 %all-gather.3.cloned.1.call-start = ((), (), s32[]{:S(2)}) async-start(), calls=%async_computation.2 | async-start | bytes 3932160 | tf_op jit(solution)/shard_map/all_gather | solution.py:977
  62.3 61.8 %copy-start = (f32[1,512,768]{2,1,0:T(8,128)S(1)}, f32[1,512,768]{2,1,0:T(8,128)}, u32[]{:S(2)}) copy-start(f32[1,512,768]{2,1,0:T(8,128)} %param.14) | copy-start | bytes 4718596
  127.3 86.2 %reduce-scatter.5.cloned.1.call-start = ((), (), s32[]{:S(2)}) async-start(), calls=%async_computation.4 | async-start | bytes 3932160 | tf_op jit(solution)/shard_map/reduce_scatter | solution.py:996
  155.7 5.1 %copy-start.17 = (bf16[4,512,768]{2,1,0:T(8,128)(2,1)S(1)}, bf16[4,512,768]{2,1,0:T(8,128)(2,1)}, u32[]{:S(2)}) copy-start(bf16[4,512,768]{2,1,0:T(8,128)(2,1)} %get-tuple-element.44) | copy-start | bytes 9437188
  155.7 5.1 %copy-start.19 = (bf16[768,768]{1,0:T(8,128)(2,1)S(1)}, bf16[768,768]{1,0:T(8,128)(2,1)}, u32[]{:S(2)}) copy-start(bf16[768,768]{1,0:T(8,128)(2,1)} %get-tuple-element.41) | copy-start | bytes 3538948
  160.8 10.6 %copy-start.20 = (bf16[768,768]{1,0:T(8,128)(2,1)S(1)}, bf16[768,768]{1,0:T(8,128)(2,1)}, u32[]{:S(2)}) copy-start(bf16[768,768]{1,0:T(8,128)(2,1)} %get-tuple-element.40) | copy-start | bytes 3538948
  169.7 1.6 copy-start.23
  175.4 78.5 %reduce-scatter.3.cloned.1.call-start = ((), (), s32[]{:S(2)}) async-start(), calls=%async_computation.3 | async-start | bytes 3932160 | tf_op jit(solution)/shard_map/reduce_scatter | solution.py:982
  181.8 105.7 %all-gather.5.cloned.1.call-start = ((), (), s32[]{:S(2)}) async-start(), calls=%async_computation.5 | async-start | bytes 3932160 | tf_op jit(solution)/shard_map/all_gather | solution.py:1006
  213.5 1.8 copy-start.2
  215.2 38.7 %copy-start.14 = (f32[768]{0:T(1024)S(1)}, f32[768]{0:T(1024)}, u32[]{:S(2)}) copy-start(f32[768]{0:T(1024)} %param.24) | copy-start | bytes 9220
  257.6 1.4 copy-start.1
  259.6 7.1 %copy-start.18 = (bf16[2048,768]{1,0:T(8,128)(2,1)S(1)}, bf16[2048,768]{1,0:T(8,128)(2,1)}, u32[]{:S(2)}) copy-start(bf16[2048,768]{1,0:T(8,128)(2,1)} %all-gather.3.cloned.1.call-done) | copy-start | bytes 9437188
  259.6 7.1 %copy-start.24 = (bf16[2048,768]{1,0:T(8,128)(2,1)S(1)}, bf16[2048,768]{1,0:T(8,128)(2,1)}, u32[]{:S(2)}) copy-start(bf16[2048,768]{1,0:T(8,128)(2,1)} %copy-done.23) | copy-start | bytes 9437188
  266.7 20.8 %copy-start.5 = (bf16[192,768]{1,0:T(8,128)(2,1)S(1)}, bf16[192,768]{1,0:T(8,128)(2,1)}, u32[]{:S(2)}) copy-start(bf16[192,768]{1,0:T(8,128)(2,1)} %get-tuple-element.37.out_full) | copy-start | bytes 884740
  271.5 20.1 %copy-start.6 = (bf16[3,64,2048]{2,1,0:T(8,128)(2,1)S(1)}, bf16[3,64,2048]{2,1,0:T(8,128)(2,1)}, u32[]{:S(2)}) copy-start(bf16[3,64,2048]{2,1,0:T(8,128)(2,1)} %get-tuple-element.43.mixed_t) | copy-start | bytes 2359300
  287.5 4.1 %copy-start.3 = (bf16[2048,768]{1,0:T(8,128)(2,1)S(1)}, bf16[2048,768]{1,0:T(8,128)(2,1)}, u32[]{:S(2)}) copy-start(bf16[2048,768]{1,0:T(8,128)(2,1)} %all-gather.5.cloned.1.call-done) | copy-start | bytes 9437188
  385.0 4.0 copy-start.11
  385.0 4.7 %copy-start.13 = (f32[1,4608]{1,0:T(1,128)S(1)}, f32[1,4608]{1,0:T(1,128)}, u32[]{:S(2)}) copy-start(f32[1,4608]{1,0:T(1,128)} %get-tuple-element.52) | copy-start | bytes 55300
  385.0 5.4 %copy-start.16 = (f32[1,768]{1,0:T(1,128)S(1)}, f32[1,768]{1,0:T(1,128)}, u32[]{:S(2)}) copy-start(f32[1,768]{1,0:T(1,128)} %get-tuple-element.56) | copy-start | bytes 9220
  385.0 6.0 %copy-start.15 = (f32[1,768]{1,0:T(1,128)S(1)}, f32[1,768]{1,0:T(1,128)}, u32[]{:S(2)}) copy-start(f32[1,768]{1,0:T(1,128)} %get-tuple-element.58) | copy-start | bytes 9220
  385.0 6.6 %copy-start.4 = (f32[512,768]{1,0:T(8,128)S(1)}, f32[512,768]{1,0:T(8,128)}, u32[]{:S(2)}) copy-start(f32[512,768]{1,0:T(8,128)} %get-tuple-element.49) | copy-start | bytes 4718596
  391.6 1.2 copy-start.22
  391.6 1.7 copy-start.10
  391.6 2.4 copy-start.9
Sparse Core Ops, SparseCore 0:
  127.4 28.2 all-gather.2
  175.6 37.8 reduce-scatter.4
  216.0 37.8 reduce-scatter.2
  258.9 28.4 all-gather.4

commit v4 on v3

--- a/solution.py
+++ b/solution.py
@@ -19,21 +19,13 @@
 UNIT = SCALE * math.log2(math.e)
 F32 = jnp.float32
 BF16 = jnp.bfloat16
-VMEM_LIMIT = 60 << 20
+VMEM_LIMIT = 67043328
 
 
 def layer_norm(values):
     center = values - jnp.mean(values, axis=-1, keepdims=True)
     spread = jnp.mean(center * center, axis=-1, keepdims=True)
     return center * lax.rsqrt(spread + EPSILON)
-
-
-def norm_shift(values, shift, scale):
-    return layer_norm(values) * (1.0 + scale) + shift
-
-
-def gelu_tanh(values):
-    return 0.5 * values * (1.0 + jnp.tanh(SLOPE * (values + CUBIC * values * values * values)))
 
 
 def rotary_tables(length):
@@ -351,25 +343,32 @@
     def give_across(self, j, value):
         self.pair(1, j).wait_recv()
         self.far_out[self.at(j), :] = (value + self.pair_in[1, self.at(j), :].astype(F32)).astype(BF16)
-        self.begin(self.cross(j))
+        if self.far_in is not None:
+            self.begin(self.cross(j))
 
     def give_partner(self, j, value):
         self.pair_out[0, self.at(j), :] = value.astype(BF16)
         self.begin(self.pair(0, j))
 
     def give_own(self, j, value):
+        self.kept[self.at(j), :] = value
+
+    def settle(self, j):
         self.pair(0, j).wait_recv()
-        self.kept[self.at(j), :] = value + self.pair_in[0, self.at(j), :].astype(F32)
+        self.kept[self.at(j), :] = self.kept[self.at(j), :] + self.pair_in[0, self.at(j), :].astype(F32)
 
     def result(self, j):
+        self.pair(0, j).wait_recv()
         self.cross(j).wait_recv()
-        return self.kept[self.at(j), :] + self.far_in[self.at(j), :].astype(F32)
+        near = self.kept[self.at(j), :] + self.pair_in[0, self.at(j), :].astype(F32)
+        return near + self.far_in[self.at(j), :].astype(F32)
 
     def close(self):
         for j in range(self.chunks):
             self.pair(0, j).wait_send()
             self.pair(1, j).wait_send()
-            self.cross(j).wait_send()
+            if self.far_in is not None:
+                self.cross(j).wait_send()
 
     @staticmethod
     def scratch(rows, width, chunks):
@@ -667,6 +666,183 @@
     )(qkv, bias, out_full, feed_back, up_shard, down_shard)
 
 
+def feed_kernel(
+    sizes, heads, chunks,
+    tokens, attention, parts, up_full, down_t, up_bias, feed_back_all, cotangent, valid, mixed_t, out_full,
+    middle, middle_back, mixed_back, up_grad, down_grad, out_grad, up_part, sums, feed_far, feed_kept,
+    second_all, hidden_all, before_all, back_all, second_sems, back_sems,
+    pair_out, pair_in, far_out, far_in, kept, scatter_sems, feed_pair_out, feed_pair_in, feed_sems,
+):
+    rows, width = tokens.shape
+    size = rows // chunks
+    length = 4 * rows
+    greet(col_peers())
+    gather = ColumnGather(second_all, chunks, second_sems)
+    gather_back = ColumnGather(back_all, chunks, back_sems)
+    scatter = ColumnScatter(pair_out, pair_in, far_out, far_in, kept, chunks, scatter_sems)
+    feed = ColumnScatter(feed_pair_out, feed_pair_in, feed_far, None, feed_kept, chunks, feed_sems)
+    me = gather.me
+    for j in range(chunks):
+        here = pl.ds(j * size, size)
+        value = tokens[here, :] + parts[2:3, :] * attention[here, :]
+        middle[here, :] = value
+        second_all[me, here, :] = (layer_norm(value) * (1.0 + parts[4:5, :]) + parts[3:4, :]).astype(BF16)
+        gather.start(j)
+    up_part[...] = jnp.zeros_like(up_part)
+
+    def block(i, _):
+        late = lax.div(i, 4)
+        pattern = (1 - late) * lax.div(i, 2) + late * (3 - lax.rem(i, 2))
+        j = (1 - late) * lax.rem(i, 2) + late * (lax.div(i, 2) - 2)
+        slot = flip_by(me, pattern)
+        here = pl.ds(pl.multiple_of(j * size, size), size)
+
+        @pl.when(i == 2)
+        def _():
+            for c in range(chunks):
+                gather.partner(c)
+
+        @pl.when(i == 3)
+        def _():
+            gather.across(0)
+
+        @pl.when(i == 4)
+        def _():
+            gather.diagonal(0)
+
+        @pl.when(i == 6)
+        def _():
+            gather.diagonal(1)
+
+        before = contract(second_all[slot, here, :], up_full[...], 1, 0) + up_bias[...]
+        bend = jnp.tanh(SLOPE * (before + CUBIC * before * before * before))
+        hidden = (0.5 * before * (1.0 + bend)).astype(BF16)
+        slope = 0.5 * (1.0 + bend) + 0.5 * before * (1.0 - bend * bend) * (SLOPE * (1.0 + 3.0 * CUBIC * before * before))
+        hidden_back = contract(feed_back_all[slot, here, :], down_t[...], 1, 0)
+        before_back = (hidden_back * slope).astype(BF16)
+        hidden_all[slot, here, :] = hidden
+        before_all[slot, here, :] = before_back
+        up_part[...] += jnp.sum(before_back.astype(F32), axis=0, keepdims=True)
+        back_value = contract(before_back, up_full[...], 1, 1)
+        feed_value = contract(hidden, down_t[...], 1, 1)
+        for at, (name, c) in enumerate(
+            (("own", 0), ("own", 1), ("partner", 0), ("partner", 1), ("diagonal", 0), ("across", 0), ("diagonal", 1), ("across", 1))
+        ):
+
+            @pl.when(i == at)
+            def _():
+                getattr(scatter, "give_" + name)(c, back_value)
+                getattr(feed, "give_" + name)(c, feed_value)
+                if at == 5:
+                    gather.across(1)
+
+        return 0
+
+    lax.fori_loop(0, 8, block, 0)
+    gate_sum = jnp.zeros((1, width), F32)
+    shift_sum = jnp.zeros((1, width), F32)
+    scale_sum = jnp.zeros((1, width), F32)
+    for j in range(chunks):
+        here = pl.ds(j * size, size)
+        own = middle[here, :]
+        center = own - jnp.mean(own, axis=-1, keepdims=True)
+        inverse = lax.rsqrt(jnp.mean(center * center, axis=-1, keepdims=True) + EPSILON)
+        unit = center * inverse
+        grad = scatter.result(j)
+        scaled = grad * (1.0 + parts[4:5, :])
+        inner = scaled - jnp.mean(scaled, axis=-1, keepdims=True) - unit * jnp.mean(scaled * unit, axis=-1, keepdims=True)
+        total = cotangent[here, :] * valid[here, :] + inverse * inner
+        middle_back[here, :] = total
+        back_all[me, here, :] = (parts[2:3, :] * total).astype(BF16)
+        gather_back.start(j)
+        gate_sum = gate_sum + jnp.sum(total * attention[here, :], axis=0, keepdims=True)
+        shift_sum = shift_sum + jnp.sum(grad, axis=0, keepdims=True)
+        scale_sum = scale_sum + jnp.sum(grad * unit, axis=0, keepdims=True)
+        if j == 0:
+            up_grad[...] = contract(second_all[...].reshape(length, width), before_all[...].reshape(length, -1), 0, 0).astype(BF16)
+        if j == 1:
+            down_grad[...] = contract(feed_back_all[...].reshape(length, width), hidden_all[...].reshape(length, -1), 0, 0).astype(BF16)
+    sums[...] = jnp.concatenate([gate_sum, shift_sum, scale_sum], axis=1)
+    for j in range(chunks):
+        feed.settle(j)
+    gather_back.across(0)
+
+    def mix(i, _):
+        @pl.when(i == 1)
+        def _():
+            for c in range(chunks):
+                gather_back.partner(c)
+
+        @pl.when(i == 2)
+        def _():
+            gather_back.across(1)
+
+        @pl.when(i == 3)
+        def _():
+            for c in range(chunks):
+                gather_back.diagonal(c)
+
+        slot = flip_by(me, i)
+        here = block_at(slot, rows)
+        value = contract(out_full[...], back_all[slot], 1, 1).astype(BF16)
+        for h in range(heads):
+            mixed_back[h, :, here] = value[h * HD : (h + 1) * HD]
+        return 0
+
+    lax.fori_loop(0, 4, mix, 0)
+    out_grad[...] = contract(
+        back_all[...].reshape(length, width), mixed_t[...].reshape(heads * HD, length), 0, 1
+    ).astype(BF16)
+    gather.close()
+    gather_back.close()
+    scatter.close()
+    feed.close()
+
+
+def feed_forward(
+    sizes, heads, tokens, attention, parts, up_full, down_t, up_bias, feed_back_all, cotangent, valid, mixed_t, out_full
+):
+    rows, width = tokens.shape
+    hidden = up_full.shape[1]
+    length = 4 * rows
+    local = heads * HD
+    chunks = 2
+    vmem = pl.BlockSpec(memory_space=pltpu.VMEM)
+    own = jax.ShapeDtypeStruct((rows, width), F32)
+    return pl.pallas_call(
+        functools.partial(feed_kernel, sizes, heads, chunks),
+        out_shape=[
+            own,
+            own,
+            jax.ShapeDtypeStruct((heads, HD, length), BF16),
+            jax.ShapeDtypeStruct((width, hidden), BF16),
+            jax.ShapeDtypeStruct((width, hidden), BF16),
+            jax.ShapeDtypeStruct((width, local), BF16),
+            jax.ShapeDtypeStruct((1, hidden), F32),
+            jax.ShapeDtypeStruct((1, 3 * width), F32),
+            jax.ShapeDtypeStruct((rows, width), BF16),
+            own,
+        ],
+        in_specs=[vmem] * 11,
+        out_specs=[vmem] * 10,
+        scratch_shapes=[
+            pltpu.VMEM((4, rows, width), BF16),
+            pltpu.VMEM((4, rows, hidden), BF16),
+            pltpu.VMEM((4, rows, hidden), BF16),
+            pltpu.VMEM((4, rows, width), BF16),
+            ColumnGather.semaphores(chunks),
+            ColumnGather.semaphores(chunks),
+            *ColumnScatter.scratch(rows, width, chunks),
+            pltpu.VMEM((2, rows, width), BF16),
+            pltpu.VMEM((2, rows, width), BF16),
+            pltpu.SemaphoreType.DMA((2, 3, chunks)),
+        ],
+        compiler_params=pltpu.CompilerParams(
+            vmem_limit_bytes=VMEM_LIMIT, collective_id=3, has_side_effects=True
+        ),
+    )(tokens, attention, parts, up_full, down_t, up_bias, feed_back_all, cotangent, valid, mixed_t, out_full)
+
+
 def contract_exact(left, right, left_axis, right_axis):
     return lax.dot_general(
         left,
@@ -681,12 +857,13 @@
     sizes, heads, chunks,
     qkv, bias, log_total, mixed_t, back_t, cosine, sine, normed, in_t, up_source, down_source, out_source,
     tokens, middle_back, parts, others, down_part, up_part, condition_all, condition_weight,
-    tokens_back, condition_back, condition_grad, bias_grad, up_bias, down_bias, in_grad, out_grad, up_grad, down_grad,
+    middle, feed_far, feed_kept, cotangent, valid, down_bias_in,
+    output, tokens_back, condition_back, condition_grad, bias_grad, up_bias, down_bias, in_grad, out_grad, up_grad, down_grad,
     turned, query, key, value, back, key_sum, value_sum, in_source,
     in_total, in_out, in_in, in_sems, up_total, up_out, up_in, up_sems,
     down_total, down_out, down_in, down_sems, out_total, out_out, out_in, out_sems,
     pair_out, pair_in, far_out, far_in, kept, col_sems,
-    line_out, line_in, up_all, pieces, arrived, backs, collected, tiny_sems, line_sems,
+    line_out, line_in, up_all, pieces, arrived, backs, collected, tiny_sems, line_sems, feed_in, feed_sems,
 ):
     count = sizes["dp"] * sizes["row"]
     number = shard_number(sizes)
@@ -720,6 +897,8 @@
     def line_copy(k):
         return send_copy(line_out.at[k], line_in.at[k], line_sems.at[0, k], line_sems.at[1, k], (near, far)[k])
 
+    feed_copy = send_copy(feed_far, feed_in, feed_sems.at[0], feed_sems.at[1], far)
+    feed_copy.start()
     scatter_up.start(0)
     scatter_down.start(0)
     scatter_out.start(0)
@@ -774,7 +953,7 @@
     scatter_out.advance(2)
     in_source[...] = contract(
         normed[...], turned[...].reshape(3 * heads * HD, length), 0, 1
-    )
+    ).astype(BF16)
     scatter_in.start(0)
     size = rows // chunks
 
@@ -798,6 +977,13 @@
     scatter_in.advance(2)
     shift_sum = jnp.zeros((1, width), F32)
     scale_sum = jnp.zeros((1, width), F32)
+    gate_sum = jnp.zeros((1, width), F32)
+    feed_copy.wait_recv()
+    for j in range(chunks):
+        here = pl.ds(j * size, size)
+        feed = feed_kept[here, :] + feed_in[here, :].astype(F32) + down_bias_in[...]
+        output[here, :] = middle[here, :] + parts[5:6, :] * feed
+        gate_sum = gate_sum + jnp.sum(cotangent[here, :] * valid[here, :] * feed, axis=0, keepdims=True)
     for j in range(chunks):
         here = pl.ds(j * size, size)
         own = tokens[here, :]
@@ -810,7 +996,7 @@
         tokens_back[here, :] = middle_back[here, :] + inverse * inner
         shift_sum = shift_sum + jnp.sum(grad, axis=0, keepdims=True)
         scale_sum = scale_sum + jnp.sum(grad * unit, axis=0, keepdims=True)
-    line_out[0] = jnp.concatenate([shift_sum, scale_sum, others[...], down_part[...]], axis=1)
+    line_out[0] = jnp.concatenate([shift_sum, scale_sum, others[...], gate_sum, down_part[...]], axis=1)
     line_copy(0).start()
     scatter_in.advance(3)
     steps = len(scatter_in.steps)
@@ -862,13 +1048,15 @@
         back_copy(i, peers[i][0], number).wait_send()
     for k in range(2):
         line_copy(k).wait_send()
+    feed_copy.wait_send()
     for one in (scatter_up, scatter_down, scatter_out, scatter_in):
         one.close()
     column.close()
 
 
 def finish(sizes, heads, qkv, bias, log_total, mixed_t, back_t, cosine, sine, normed, in_t, up_source, down_source,
-           out_source, tokens, middle_back, parts, others, down_part, up_part, condition_all, condition_weight):
+           out_source, tokens, middle_back, parts, others, down_part, up_part, condition_all, condition_weight,
+           middle, feed_far, feed_kept, cotangent, valid, down_bias):
     count = sizes["dp"] * sizes["row"]
     length = qkv.shape[2]
     rows, width = tokens.shape
@@ -882,6 +1070,7 @@
         functools.partial(finish_kernel, sizes, heads, chunks),
         out_shape=[
             jax.ShapeDtypeStruct((rows, width), F32),
+            jax.ShapeDtypeStruct((rows, width), F32),
             jax.ShapeDtypeStruct((1, cond), F32),
             jax.ShapeDtypeStruct((cond, piece), F32),
             jax.ShapeDtypeStruct((1, 6 * width), F32),
@@ -892,8 +1081,8 @@
             jax.ShapeDtypeStruct((share, hidden), F32),
             jax.ShapeDtypeStruct((share, hidden), F32),
         ],
-        in_specs=[vmem] * 20,
-        out_specs=[vmem] * 10,
+        in_specs=[vmem] * 26,
+        out_specs=[vmem] * 11,
         scratch_shapes=[
             pltpu.VMEM((3 * heads, HD, length), BF16),
             pltpu.VMEM((heads, AUG, length), BF16),
@@ -902,7 +1091,7 @@
             pltpu.VMEM((heads, AUG, length), BF16),
             pltpu.VMEM((heads, HD, length), F32),
             pltpu.VMEM((heads, HD, length), F32),
-            pltpu.VMEM((width, 3 * local), F32),
+            pltpu.VMEM((width, 3 * local), BF16),
             *ShardScatter.scratch(count, share, 3 * local),
             *ShardScatter.scratch(count, share, hidden),
             *ShardScatter.scratch(count, share, hidden),
@@ -917,12 +1106,15 @@
             pltpu.VMEM((count, 1, cond + piece), F32),
             pltpu.SemaphoreType.DMA((2, 3, count - 1)),
             pltpu.SemaphoreType.DMA((2, 2)),
+            pltpu.VMEM((rows, width), BF16),
+            pltpu.SemaphoreType.DMA((2,)),
         ],
         compiler_params=pltpu.CompilerParams(
             vmem_limit_bytes=VMEM_LIMIT, collective_id=2, has_side_effects=True
         ),
     )(qkv, bias, log_total, mixed_t, back_t, cosine, sine, normed, in_t, up_source, down_source, out_source,
-      tokens, middle_back, parts, others, down_part, up_part, condition_all, condition_weight)
+      tokens, middle_back, parts, others, down_part, up_part, condition_all, condition_weight,
+      middle, feed_far, feed_kept, cotangent, valid, down_bias)
 
 
 def shards(
@@ -967,53 +1159,22 @@
     attention, mixed_t, log_total, feed_back_blocks, up_full, down_t = attend(
         sizes, heads, qkv, bias, out_full, feed_back, up_shard, down_shard
     )
-    mixed_rows = mixed_t.reshape(local_width, length_all)
-    down_full = down_t.T
-    feed_back_all = feed_back_blocks.reshape(length_all, width)
-    middle = own_rows + parts[2] * attention
-    second, second_pull = jax.vjp(norm_shift, middle, parts[3], parts[4])
-    second_low = second.astype(BF16)
     hidden_cols = up_full.shape[1]
-    second_all = lax.all_gather(second_low, "col", axis=0, tiled=True)
     bias_part = lax.dynamic_slice_in_dim(up_bias, column_index * hidden_cols, hidden_cols)
-    before = jnp.dot(second_all, up_full, preferred_element_type=F32) + bias_part
-    hidden, gelu_pull = jax.vjp(gelu_tanh, before)
-    hidden_low = hidden.astype(BF16)
-    feed = lax.psum_scatter(
-        jnp.dot(hidden_low, down_full, preferred_element_type=F32).astype(BF16),
-        "col",
-        scatter_dimension=0,
-        tiled=True,
-    ).astype(F32)
-    result = middle + parts[5] * (feed + down_bias)
-    incoming = cotangent[0] * valid[:, None]
-    gate_feed = jnp.sum(incoming * (feed + down_bias), axis=0)
-    hidden_back = jnp.einsum("sd,fd->sf", feed_back_all, down_full, preferred_element_type=F32)
-    down_grad = jnp.einsum("sd,sf->df", feed_back_all, hidden_low, preferred_element_type=F32)
-    before_back = gelu_pull(hidden_back)[0].astype(BF16)
-    up_grad = jnp.einsum("sd,sf->df", second_all, before_back, preferred_element_type=F32)
-    up_bias_part = jnp.sum(before_back.astype(F32), axis=0)
-    second_back = lax.psum_scatter(
-        jnp.einsum("sf,df->sd", before_back, up_full, preferred_element_type=F32).astype(BF16),
-        "col",
-        scatter_dimension=0,
-        tiled=True,
-    ).astype(F32)
-    middle_part, shift_feed, scale_feed = second_pull(second_back)
-    middle_back = incoming + middle_part
-    gate_attention = jnp.sum(middle_back * attention, axis=0)
-    attention_back = (parts[2] * middle_back).astype(BF16)
-    attention_back_all = lax.all_gather(attention_back, "col", axis=0, tiled=True)
-    out_grad = jnp.einsum("sd,cs->dc", attention_back_all, mixed_rows, preferred_element_type=F32)
-    mixed_back = jnp.einsum("sd,cd->cs", attention_back_all, out_full, preferred_element_type=F32)
-    others = jnp.concatenate([gate_attention, shift_feed, scale_feed, gate_feed])[None]
     (
-        tokens_back, condition_back, condition_grad, bias_grad, up_bias_grad, down_bias_grad,
+        middle, middle_back, mixed_back, up_grad, down_grad, out_grad, up_bias_part, others, feed_far, feed_kept
+    ) = feed_forward(
+        sizes, heads, own_rows, attention, parts, up_full, down_t, bias_part[None], feed_back_blocks,
+        cotangent[0], valid[:, None], mixed_t, out_full,
+    )
+    (
+        result, tokens_back, condition_back, condition_grad, bias_grad, up_bias_grad, down_bias_grad,
         in_grad, out_grad, up_grad, down_grad,
     ) = finish(
-        sizes, heads, qkv, bias, log_total, mixed_t, mixed_back.astype(BF16).reshape(heads, HD, length_all),
+        sizes, heads, qkv, bias, log_total, mixed_t, mixed_back,
         cosine, sine, normed_all, in_t, up_grad, down_grad, out_grad, own_rows, middle_back, parts,
-        others, down_bias_part, up_bias_part[None], condition_all, weight_low,
+        others, down_bias_part, up_bias_part, condition_all, weight_low,
+        middle, feed_far, feed_kept, cotangent[0], valid[:, None], down_bias[None],
     )
     return (
         result[None],

time: 408 us -> 295 us (0.72); the launches traced: 402 us -> 294 us
  waiting for transfers between devices: 113 us -> 0 us
  Pallas kernels: 197 us -> 267 us
  matrix products: 41.6 us -> 0 us
  between operations: 15.2 us -> 1.4 us
  other arithmetic: 18.2 us -> 9.39 us
    reduce_scatter x2 -> x0, waiting for transfers between devices: 69.3 us -> none  [the longest x1 37.8 us: shards(): lax.psum_scatter(jnp.dot(hidden_low, down_full, preferred_element_type=F3...]
    pallas_call x0 -> x1, Pallas kernels: none -> 64.6 us  [feed_forward(): pl.pallas_call(functools.partial(feed_kernel, sizes, heads, chunks), out_...]
    all_gather x2 -> x0, waiting for transfers between devices: 43.4 us -> none  [the longest x1 27.4 us: shards(): second_all = lax.all_gather(second_low, 'col', axis=0, tiled=True)]
    dot_general x8 -> x0, matrix products: 41.6 us -> none  [the longest x1 8.96 us: shards(): jnp.einsum('sd,fd->sf', feed_back_all, down_full, preferred_element_type=...]
    reduce_sum x5 -> x0, other arithmetic: 8.28 us -> none  [the longest x1 3.7 us: shards(): gate_attention = jnp.sum(middle_back * attention, axis=0)]
    pallas_call x1, Pallas kernels: 91.5 us -> 96 us  [finish(): pl.pallas_call(functools.partial(finish_kernel, sizes, heads, chunks), ou...]
    unnamed x59 -> x28, local copies, waits for them, and re-layouts: 11.9 us -> 11.1 us
  transfers between devices with their start and end apart: 4 -> 0, of which waited for: 4 -> 0; matrix products, arithmetic and copies ran while one was open for 6% -> 0% of each run, Pallas kernels for 0% -> 0%
where the time goes in v4:
time: 295 us; the launch traced here: 294 us
  Pallas kernels  267 us (91%)
  local copies, waits for them, and re-layouts  17.2 us (6%)
  other arithmetic  9.39 us (3%)
    pallas_call x1, Pallas kernels, finish(): pl.pallas_call(functools.partial(finish_kernel, sizes, heads, chunks), ou...  96 us
    pallas_call x1, Pallas kernels, feed_forward(): pl.pallas_call(functools.partial(feed_kernel, sizes, heads, chunks), out_...  64.6 us
    pallas_call x1, Pallas kernels, attend(): pl.pallas_call(functools.partial(attention_kernel, sizes, heads, chunks),...  61.5 us
    pallas_call x1, Pallas kernels, start(): pl.pallas_call(functools.partial(start_kernel, sizes, heads, chunks), out...  44.3 us
    unnamed x28, local copies, waits for them, and re-layouts  11.1 us

profile of v4, /device:TPU:0, one launch (start us, length us, event | category | flops | bytes accessed | tf_op | source)
XLA Modules:
  0.0 294.5 jit_solution(18325500516186624189)
XLA Ops:
  0.6 0.0 copy-start.4
  0.7 1.2 convert_convert_fusion.condition
  1.9 1.8 copy.31.condition_weight
  3.6 1.3 broadcast_in_dim.27.condition_bias
  5.0 1.0 convert_element_type.40
  5.9 0.2 copy.32
  6.1 0.8 copy.34.in_shard
  6.9 0.0 copy-done.4
  6.9 0.7 copy.33
  8.3 0.7 fusion.valid
  9.0 44.3 %shard_map.221 = (f32[6,768]{1,0:T(8,128)}, bf16[4,512,768]{2,1,0:T(8,128)(2,1)}, bf16[9,64,2048]{2,1,0:T(8,128)(2,1)}, bf16[192,768]{1,0:T(8,128)(2,1)}, bf16[5...) custom-call(f32[1,128]{1,0:T(1,128)} %convert_convert_fusion.condition, ...), custom_call_target="tpu_custom_call" | custom-call | tf_op jit(solution)/shard_map/pallas_call | solution.py:538
  53.3 0.6 compare_select_fusion.bias
  53.9 1.6 convert_element_type.45.up_shard
  55.6 1.6 convert_bitcast_fusion.down_shard
  57.2 61.5 %shard_map.222 = (f32[512,768]{1,0:T(8,128)}, bf16[3,64,2048]{2,1,0:T(8,128)(2,1)}, f32[3,1,2048]{2,1,0:T(1,128)}, bf16[4,512,768]{2,1,0:T(8,128)(2,1)}, bf16[76...) custom-call(bf16[9,64,2048]{2,1,0:T(8,128)(2,1)} %get-tuple-element.46.qkv, f32[1,2048]{1,0:T(1,128)} %compare_select_fusion.bias, ...), custom_call_target="tpu_custom_call" | custom-call | tf_op jit(solution)/shard_map/pallas_call | solution.py:643
  118.7 0.8 dynamic_slice.3
  119.5 0.6 broadcast_in_dim.30.up_bias
  120.1 64.6 %shard_map.223 = (f32[512,768]{1,0:T(8,128)}, f32[512,768]{1,0:T(8,128)}, bf16[3,64,2048]{2,1,0:T(8,128)(2,1)}, bf16[768,768]{1,0:T(8,128)(2,1)}, bf16[768,768]{...) custom-call(f32[512,768]{1,0:T(8,128)} %bitcast.18, ...), custom_call_target="tpu_custom_call" | custom-call | tf_op jit(solution)/shard_map/pallas_call | solution.py:812
  184.7 1.3 broadcast_in_dim.31.down_bias_in
  186.0 96.0 %shard_map.224 = (f32[512,768]{1,0:T(8,128)}, f32[512,768]{1,0:T(8,128)}, f32[1,128]{1,0:T(1,128)}, f32[128,576]{1,0:T(8,128)}, f32[1,4608]{1,0:T(1,128)}, /*ind...) custom-call(bf16[9,64,2048]{2,1,0:T(8,128)(2,1)} %get-tuple-element., ...), custom_call_target="tpu_custom_call" | custom-call | tf_op jit(solution)/shard_map/pallas_call | solution.py:1069
  282.1 0.0 copy-start.5
  282.1 0.0 copy-start.7
  282.1 0.0 copy-start.6
  282.1 0.0 copy-start.1
  282.1 2.0 copy.36
  284.1 1.4 reduce
  285.4 1.1 copy.35
  286.5 0.9 copy.37
  287.4 0.0 copy-done.5
  287.4 0.7 copy.38
  288.2 0.0 copy-done.7
  288.2 0.6 reduce.1
  288.8 0.0 copy-done.6
  288.8 0.6 reduce.2
  289.4 0.0 copy-done.1
  289.4 0.0 copy-start
  289.4 1.1 copy.45
  290.5 0.8 copy-done
  291.4 0.0 copy-start.8
  291.4 0.0 copy-start.3
  291.4 0.0 copy-start.2
  291.4 1.1 copy.46
  292.5 0.0 copy-done.8
  292.5 0.5 copy.47
  293.0 0.0 copy-done.3
  293.0 0.7 copy.48
  293.7 0.0 copy-done.2
  293.7 0.7 copy.49
Async XLA Ops:
  0.6 6.3 %copy-start.4 = (f32[192,96]{1,0:T(8,128)S(1)}, f32[192,96]{1,0:T(8,128)}, u32[]{:S(2)}) copy-start(f32[192,96]{1,0:T(8,128)} %param.20) | copy-start | bytes 221188
  282.1 5.3 %copy-start.5 = (f32[96,192]{1,0:T(8,128)S(1)}, f32[96,192]{1,0:T(8,128)}, u32[]{:S(2)}) copy-start(f32[96,192]{1,0:T(8,128)} %get-tuple-element.76) | copy-start | bytes 221188
  282.1 6.1 %copy-start.7 = (f32[1,768]{1,0:T(1,128)S(1)}, f32[1,768]{1,0:T(1,128)}, u32[]{:S(2)}) copy-start(f32[1,768]{1,0:T(1,128)} %get-tuple-element.78) | copy-start | bytes 9220
  282.1 6.7 %copy-start.6 = (f32[1,768]{1,0:T(1,128)S(1)}, f32[1,768]{1,0:T(1,128)}, u32[]{:S(2)}) copy-start(f32[1,768]{1,0:T(1,128)} %get-tuple-element.80) | copy-start | bytes 9220
  282.1 7.3 %copy-start.1 = (f32[512,768]{1,0:T(8,128)S(1)}, f32[512,768]{1,0:T(8,128)}, u32[]{:S(2)}) copy-start(f32[512,768]{1,0:T(8,128)} %get-tuple-element.70) | copy-start | bytes 4718596
  289.4 2.0 copy-start
  291.4 1.2 copy-start.8
  291.4 1.7 copy-start.3
  291.4 2.4 copy-start.2

commit v5 on v4

--- a/solution.py
+++ b/solution.py
@@ -146,6 +146,17 @@
     return [{axis: flip(lax.axis_index(axis), bit)} for axis, bit, _ in doubling(sizes)]
 
 
+def neighbour_peers(sizes):
+    z = lax.axis_index("dp")
+    n, m = sizes["dp"], sizes["row"]
+    peers = [{"dp": lax.rem(z + 1, n)}, {"dp": lax.rem(z + n - 1, n)}]
+    bit = m // 2
+    while bit:
+        peers.append({"row": flip(lax.axis_index("row"), bit)})
+        bit //= 2
+    return peers
+
+
 def col_peers():
     me = lax.axis_index("col")
     return [{"col": flip(me, 1)}, {"col": flip(me, 2)}]
@@ -153,52 +164,124 @@
 
 class ShardGather:
     def __init__(self, sizes, shard, full, sems):
-        self.steps = doubling(sizes)
+        self.n, self.m = sizes["dp"], sizes["row"]
         self.rows = shard.shape[0]
         self.shard, self.full, self.sems = shard, full, sems
-        self.me = shard_number(sizes)
-
-    def slot(self, number):
-        return self.full.at[pl.ds(pl.multiple_of(number * self.rows, self.rows), self.rows), :]
-
-    def copies(self, k, arriving):
-        axis, bit, stride = self.steps[k]
-        peer = {axis: flip(lax.axis_index(axis), bit)}
-        out = []
-        for i, kept in enumerate(subsets([s[2] for s in self.steps[:k]])):
-            number = flips(self.me, kept + ((stride,) if arriving else ()))
-            source = self.slot(number)
-            if not arriving and not kept:
-                source = self.shard
-            at = 2**k - 1 + i
-            out.append(send_copy(source, self.slot(number), self.sems.at[0, at], self.sems.at[1, at], peer))
+        self.z, self.y = lax.axis_index("dp"), lax.axis_index("row")
+
+    def slot(self, z, y):
+        return self.full.at[pl.ds(pl.multiple_of((z * self.m + y) * self.rows, self.rows), self.rows), :]
+
+    def held(self, side, h):
+        z = self.z - side * h
+        return z, (z >= 0) if side > 0 else (z < self.n)
+
+    def onward(self, side):
+        return (self.z + 1 < self.n) if side > 0 else (self.z > 0)
+
+    def stream(self, side, h, arriving):
+        z, _ = self.held(side, h if arriving else h - 1)
+        at = (h - 1) + (self.n - 1 if side < 0 else 0)
+        source = self.slot(z, self.y) if arriving or h > 1 else self.shard
+        peer = {"dp": self.z + (side if not arriving else -side)}
+        return send_copy(source, self.slot(z, self.y), self.sems.at[0, at], self.sems.at[1, at], peer)
+
+    def over(self, side, h, arriving):
+        z, _ = self.held(side, h)
+        bit = self.m // 2
+        at = 2 * (self.n - 1) + h + (self.n - 1 if side < 0 and h else 0)
+        there = self.slot(z, flip(self.y, bit) if arriving else self.y)
+        source = self.shard if h == 0 and not arriving else there
+        return send_copy(source, there, self.sems.at[0, at], self.sems.at[1, at], {"row": flip(self.y, bit)})
+
+    def keep(self):
+        self.slot(self.z, self.y)[...] = self.shard[...]
+
+    def start(self):
+        for side in (1, -1):
+
+            @pl.when(self.onward(side))
+            def _():
+                self.stream(side, 1, False).start()
+
+        self.over(1, 0, False).start()
+
+    def advance(self, h):
+        if h >= self.n:
+            return
+        for side in (1, -1):
+            _, here = self.held(side, h)
+
+            @pl.when(here)
+            def _():
+                self.stream(side, h, True).wait_recv()
+
+            if h + 1 < self.n:
+
+                @pl.when(jnp.logical_and(here, self.onward(side)))
+                def _():
+                    self.stream(side, h + 1, False).start()
+
+            @pl.when(here)
+            def _():
+                self.over(side, h, False).start()
+
+    def others(self):
+        out, held, at = [], (self.m // 2,), 4 * self.n - 3
+        bit = self.m // 4
+        while bit:
+            kept = subsets(held)
+            out.append((bit, kept, at))
+            at += self.n * len(kept)
+            held = held + (bit,)
+            bit //= 2
         return out
 
-    def keep(self):
-        self.slot(self.me)[...] = self.shard[...]
-
-    def start(self, k):
-        for copy in self.copies(k, False):
-            copy.start()
-
-    def arrived(self, k):
-        for copy in self.copies(k, True):
-            copy.wait_recv()
-
-    def advance(self, k):
-        if 0 < k <= len(self.steps):
-            self.arrived(k - 1)
-        if k < len(self.steps):
-            self.start(k)
+    def spread(self, bit, kept, at, arriving):
+        peer = {"row": flip(self.y, bit)}
+        for z in range(self.n):
+            for i, bits in enumerate(kept):
+                there = self.slot(z, flips(self.y, bits + ((bit,) if arriving else ())))
+                k = at + z * len(kept) + i
+                yield send_copy(there, there, self.sems.at[0, k], self.sems.at[1, k], peer)
+
+    def finish(self):
+        self.over(1, 0, True).wait_recv()
+        for side in (1, -1):
+            for h in range(1, self.n):
+
+                @pl.when(self.held(side, h)[1])
+                def _():
+                    self.over(side, h, True).wait_recv()
+
+        for step in self.others():
+            for copy in self.spread(*step, False):
+                copy.start()
+            for copy in self.spread(*step, True):
+                copy.wait_recv()
 
     def close(self):
-        for k in range(len(self.steps)):
-            for copy in self.copies(k, False):
+        self.over(1, 0, False).wait_send()
+        for side in (1, -1):
+            for h in range(1, self.n):
+                _, here = self.held(side, h)
+
+                @pl.when(jnp.logical_and(self.held(side, h - 1)[1], self.onward(side)))
+                def _():
+                    self.stream(side, h, False).wait_send()
+
+                @pl.when(here)
+                def _():
+                    self.over(side, h, False).wait_send()
+
+        for step in self.others():
+            for copy in self.spread(*step, False):
                 copy.wait_send()
 
     @staticmethod
-    def semaphores(count):
-        return pltpu.SemaphoreType.DMA((2, count - 1))
+    def semaphores(sizes):
+        n, m = sizes["dp"], sizes["row"]
+        return pltpu.SemaphoreType.DMA((2, 4 * n - 3 + n * max(m - 2, 0)))
 
 
 class ShardScatter:
@@ -424,8 +507,8 @@
 
     for i in range(count - 1):
         condition_copy(i, number).start()
-    gather_in.start(0)
-    gather_out.start(0)
+    gather_in.start()
+    gather_out.start()
     condition_all[number] = condition[...]
     gather_in.keep()
     gather_out.keep()
@@ -461,6 +544,8 @@
         gather_col.start(j)
     gather_in.advance(2)
     gather_out.advance(2)
+    gather_in.advance(3)
+    gather_out.advance(3)
     total = jnp.zeros((1, width), F32)
     for j in range(chunks):
         here = pl.ds(j * size, size)
@@ -468,10 +553,11 @@
         feed_back[here, :] = value.astype(BF16)
         total = total + jnp.sum(value, axis=0, keepdims=True)
     bias_part[...] = total
-    steps = len(gather_in.steps)
-    for k in range(3, steps + 1):
+    for k in range(4, sizes["dp"]):
         gather_in.advance(k)
         gather_out.advance(k)
+    gather_in.finish()
+    gather_out.finish()
     in_t[...] = in_full[...].astype(F32).T.astype(BF16)
     out_full[...] = out_t[...].astype(F32).T.astype(BF16)
 
@@ -556,8 +642,8 @@
             pltpu.VMEM((width, local), BF16),
             pltpu.VMEM((rows, width), F32),
             pltpu.SemaphoreType.DMA((4, count - 1)),
-            ShardGather.semaphores(count),
-            ShardGather.semaphores(count),
+            ShardGather.semaphores(sizes),
+            ShardGather.semaphores(sizes),
             ColumnGather.semaphores(chunks),
         ],
         compiler_params=pltpu.CompilerParams(
@@ -570,18 +656,21 @@
     sizes, heads, chunks,
     qkv, bias, out_full, feed_back, up_shard, down_shard,
     attention, mixed_t, log_total, feed_back_all, up_full, down_t,
-    query, key, pair_out, pair_in, far_out, far_in, kept, sems_scatter, sems_col, sems_up, sems_down,
+    query, key, up_low, down_low,
+    pair_out, pair_in, far_out, far_in, kept, sems_scatter, sems_col, sems_up, sems_down,
 ):
     rows = feed_back.shape[0]
     length = qkv.shape[2]
-    greet(doubling_peers(sizes) + col_peers())
-    gather_up = ShardGather(sizes, up_shard, up_full, sems_up)
-    gather_down = ShardGather(sizes, down_shard, down_t, sems_down)
+    up_low[...] = up_shard[...].astype(BF16)
+    down_low[...] = down_shard[...].T.astype(BF16)
+    greet(neighbour_peers(sizes) + col_peers())
+    gather_up = ShardGather(sizes, up_low, up_full, sems_up)
+    gather_down = ShardGather(sizes, down_low, down_t, sems_down)
     gather_col = ColumnGather(feed_back_all, chunks, sems_col)
     scatter = ColumnScatter(pair_out, pair_in, far_out, far_in, kept, 1, sems_scatter)
     me = gather_col.me
-    gather_up.start(0)
-    gather_down.start(0)
+    gather_up.start()
+    gather_down.start()
     feed_back_all[me] = feed_back[...]
     for j in range(chunks):
         gather_col.start(j)
@@ -598,7 +687,6 @@
         return 0
 
     lax.fori_loop(0, length // rows, prepare, 0)
-    steps = len(gather_up.steps)
 
     def step(i, _):
         here = block_at(flip_by(me, 3 - i), rows)
@@ -614,18 +702,21 @@
                 if order < 3:
                     gather_up.advance(order + 1)
                     gather_down.advance(order + 1)
+                if order == 2:
+                    for j in range(chunks):
+                        gather_col.across(j)
 
         return 0
 
     lax.fori_loop(0, 4, step, 0)
-    for k in range(4, steps + 1):
+    for k in range(4, sizes["dp"]):
         gather_up.advance(k)
         gather_down.advance(k)
     for j in range(chunks):
-        gather_col.across(j)
-    for j in range(chunks):
         gather_col.partner(j)
         gather_col.diagonal(j)
+    gather_up.finish()
+    gather_down.finish()
     attention[...] = scatter.result(0)
     gather_up.close()
     gather_down.close()
@@ -655,10 +746,12 @@
         scratch_shapes=[
             pltpu.VMEM((heads, AUG, length), BF16),
             pltpu.VMEM((heads, length, AUG), BF16),
+            pltpu.VMEM((width // count, hidden), BF16),
+            pltpu.VMEM((width // count, hidden), BF16),
             *ColumnScatter.scratch(rows, width, 1),
             ColumnGather.semaphores(chunks),
-            ShardGather.semaphores(count),
-            ShardGather.semaphores(count),
+            ShardGather.semaphores(sizes),
+            ShardGather.semaphores(sizes),
         ],
         compiler_params=pltpu.CompilerParams(
             vmem_limit_bytes=VMEM_LIMIT, collective_id=1, has_side_effects=True
@@ -951,30 +1044,28 @@
     lax.fori_loop(0, 4, finish_block, 0)
     scatter_down.advance(2)
     scatter_out.advance(2)
+    size = rows // chunks
+
+    def part_of(slot, j):
+        start_at = pl.multiple_of(slot * rows + j * size, size)
+        block = turned[:, :, pl.ds(start_at, size)].reshape(3 * heads * HD, size)
+        return contract(block, in_t[...], 0, 0)
+
+    for j in range(chunks):
+        column.give_diagonal(j, part_of(flips(me, (1, 2)), j))
+    for j in range(chunks):
+        column.give_across(j, part_of(flip(me, 2), j))
     in_source[...] = contract(
         normed[...], turned[...].reshape(3 * heads * HD, length), 0, 1
     ).astype(BF16)
     scatter_in.start(0)
-    size = rows // chunks
-
-    def part_of(slot, j):
-        start_at = pl.multiple_of(slot * rows + j * size, size)
-        block = turned[:, :, pl.ds(start_at, size)].reshape(3 * heads * HD, size)
-        return contract(block, in_t[...], 0, 0)
-
-    for j in range(chunks):
-        column.give_diagonal(j, part_of(flips(me, (1, 2)), j))
-    for j in range(chunks):
-        column.give_across(j, part_of(flip(me, 2), j))
     scatter_up.advance(3)
     for j in range(chunks):
         column.give_partner(j, part_of(flip(me, 1), j))
-    scatter_in.advance(1)
     for j in range(chunks):
         column.give_own(j, part_of(me, j))
     scatter_down.advance(3)
     scatter_out.advance(3)
-    scatter_in.advance(2)
     shift_sum = jnp.zeros((1, width), F32)
     scale_sum = jnp.zeros((1, width), F32)
     gate_sum = jnp.zeros((1, width), F32)
@@ -984,6 +1075,7 @@
         feed = feed_kept[here, :] + feed_in[here, :].astype(F32) + down_bias_in[...]
         output[here, :] = middle[here, :] + parts[5:6, :] * feed
         gate_sum = gate_sum + jnp.sum(cotangent[here, :] * valid[here, :] * feed, axis=0, keepdims=True)
+    scatter_in.advance(1)
     for j in range(chunks):
         here = pl.ds(j * size, size)
         own = tokens[here, :]
@@ -998,10 +1090,10 @@
         scale_sum = scale_sum + jnp.sum(grad * unit, axis=0, keepdims=True)
     line_out[0] = jnp.concatenate([shift_sum, scale_sum, others[...], gate_sum, down_part[...]], axis=1)
     line_copy(0).start()
-    scatter_in.advance(3)
+    scatter_in.advance(2)
     steps = len(scatter_in.steps)
     for k in range(4, steps + 1):
-        for one in (scatter_up, scatter_down, scatter_out, scatter_in):
+        for one in (scatter_up, scatter_down, scatter_out):
             one.advance(k)
     line_copy(0).wait_recv()
     line_out[1] = line_out[0] + line_in[0]
@@ -1009,7 +1101,6 @@
     up_grad[...] = scatter_up.result()
     down_grad[...] = scatter_down.result()
     out_grad[...] = scatter_out.result()
-    in_grad[...] = scatter_in.result()
     for i in range(count - 1):
         up_copy(i, peers[i][0]).wait_recv()
     up_bias[...] = jnp.sum(jnp.concatenate([up_all[b] for b in range(count)], axis=0), axis=0, keepdims=True)
@@ -1033,6 +1124,9 @@
     for i in range(count - 1):
         back_copy(i, peers[i][0], number).start()
     collected[number] = backs[number]
+    for k in range(3, steps + 1):
+        scatter_in.advance(k)
+    in_grad[...] = scatter_in.result()
     conditions = jnp.concatenate([condition_all[b] for b in range(count)], axis=0)
     condition_grad[...] = contract_exact(conditions, mine, 0, 0)
     for i in range(count - 1):
@@ -1141,8 +1235,6 @@
     heads = local_width // HD
     in_shard = attention_in.reshape(attention_in.shape[0], 3 * local_width).astype(BF16)
     out_shard = attention_out.T.astype(BF16)
-    up_shard = up_weight.astype(BF16)
-    down_shard = down_weight.T.astype(BF16)
     condition_low = condition.astype(BF16)
     weight_low = condition_weight.astype(BF16)
     own_rows = tokens[0]
@@ -1157,7 +1249,7 @@
     )
     normed_all = normed_blocks.reshape(length_all, width)
     attention, mixed_t, log_total, feed_back_blocks, up_full, down_t = attend(
-        sizes, heads, qkv, bias, out_full, feed_back, up_shard, down_shard
+        sizes, heads, qkv, bias, out_full, feed_back, up_weight, down_weight
     )
     hidden_cols = up_full.shape[1]
     bias_part = lax.dynamic_slice_in_dim(up_bias, column_index * hidden_cols, hidden_cols)

time: 295 us -> 268 us (0.908)
  Pallas kernels: 267 us -> 241 us
  other arithmetic: 9.39 us -> 6.11 us
    pallas_call x1, Pallas kernels: 61.5 us -> 43.5 us  [attend(): pl.pallas_call(functools.partial(attention_kernel, sizes, heads, chunks),...]
    pallas_call x1, Pallas kernels: 44.3 us -> 39.1 us  [start(): pl.pallas_call(functools.partial(start_kernel, sizes, heads, chunks), out...]
    convert_element_type x2 -> x0, other arithmetic: 3.28 us -> none  [the longest x1 1.64 us: shards(): down_shard = down_weight.T.astype(BF16)]
    unnamed x28 -> x29, local copies, waits for them, and re-layouts: 11.1 us -> 13 us
where the time goes in v5:
time: 268 us; the launch traced here: 267 us
  Pallas kernels  241 us (90%)
  local copies, waits for them, and re-layouts  19 us (7%)
  other arithmetic  6.11 us (2%)
    pallas_call x1, Pallas kernels, finish(): pl.pallas_call(functools.partial(finish_kernel, sizes, heads, chunks), ou...  94.1 us
    pallas_call x1, Pallas kernels, feed_forward(): pl.pallas_call(functools.partial(feed_kernel, sizes, heads, chunks), out_...  63.9 us
    pallas_call x1, Pallas kernels, attend(): pl.pallas_call(functools.partial(attention_kernel, sizes, heads, chunks),...  43.5 us
    pallas_call x1, Pallas kernels, start(): pl.pallas_call(functools.partial(start_kernel, sizes, heads, chunks), out...  39.1 us
    unnamed x29, local copies, waits for them, and re-layouts  13 us

profile of v5, /device:TPU:0, one launch (start us, length us, event | category | flops | bytes accessed | tf_op | source)
XLA Modules:
  0.0 267.2 jit_solution(14408918824467283900)
XLA Ops:
  0.6 0.0 copy-start.4
  0.7 1.2 convert_convert_fusion.condition
  1.9 1.8 copy.32.condition_weight
  3.6 1.3 broadcast_in_dim.27.condition_bias
  5.0 1.0 convert_element_type.32
  5.9 0.2 copy.33
  6.1 0.8 copy.35.in_shard
  6.9 0.0 copy-done.4
  6.9 0.7 copy.34
  8.3 0.7 fusion.valid
  9.0 39.1 %shard_map.221 = (f32[6,768]{1,0:T(8,128)}, bf16[4,512,768]{2,1,0:T(8,128)(2,1)}, bf16[9,64,2048]{2,1,0:T(8,128)(2,1)}, bf16[192,768]{1,0:T(8,128)(2,1)}, bf16[5...) custom-call(f32[1,128]{1,0:T(1,128)} %convert_convert_fusion.condition, ...), custom_call_target="tpu_custom_call" | custom-call | tf_op jit(solution)/shard_map/pallas_call | solution.py:624
  48.2 0.6 compare_select_fusion.bias
  48.8 1.9 copy.36.down_shard
  50.7 43.5 %shard_map.222 = (f32[512,768]{1,0:T(8,128)}, bf16[3,64,2048]{2,1,0:T(8,128)(2,1)}, f32[3,1,2048]{2,1,0:T(1,128)}, bf16[4,512,768]{2,1,0:T(8,128)(2,1)}, bf16[76...) custom-call(bf16[9,64,2048]{2,1,0:T(8,128)(2,1)} %get-tuple-element.46.qkv, f32[1,2048]{1,0:T(1,128)} %compare_select_fusion.bias, ...), custom_call_target="tpu_custom_call" | custom-call | tf_op jit(solution)/shard_map/pallas_call | solution.py:734
  94.2 0.8 dynamic_slice.3
  95.0 0.6 broadcast_in_dim.30.up_bias
  95.6 63.9 %shard_map.223 = (f32[512,768]{1,0:T(8,128)}, f32[512,768]{1,0:T(8,128)}, bf16[3,64,2048]{2,1,0:T(8,128)(2,1)}, bf16[768,768]{1,0:T(8,128)(2,1)}, bf16[768,768]{...) custom-call(f32[512,768]{1,0:T(8,128)} %bitcast.16, ...), custom_call_target="tpu_custom_call" | custom-call | tf_op jit(solution)/shard_map/pallas_call | solution.py:905
  159.5 1.3 broadcast_in_dim.31.down_bias_in
  160.7 94.1 %shard_map.224 = (f32[512,768]{1,0:T(8,128)}, f32[512,768]{1,0:T(8,128)}, f32[1,128]{1,0:T(1,128)}, f32[128,576]{1,0:T(8,128)}, f32[1,4608]{1,0:T(1,128)}, /*ind...) custom-call(bf16[9,64,2048]{2,1,0:T(8,128)(2,1)} %get-tuple-element., ...), custom_call_target="tpu_custom_call" | custom-call | tf_op jit(solution)/shard_map/pallas_call | solution.py:1163
  254.8 0.0 copy-start.5
  254.8 0.0 copy-start.7
  254.8 0.0 copy-start.6
  254.8 0.0 copy-start.1
  254.8 2.0 copy.38
  256.8 1.4 reduce
  258.2 1.1 copy.37
  259.3 0.9 copy.39
  260.1 0.0 copy-done.5
  260.1 0.7 copy.40
  260.9 0.0 copy-done.7
  260.9 0.6 reduce.1
  261.5 0.0 copy-done.6
  261.5 0.6 reduce.2
  262.1 0.0 copy-done.1
  262.1 0.0 copy-start
  262.1 1.1 copy.47
  263.2 0.8 copy-done
  264.1 0.0 copy-start.8
  264.1 0.0 copy-start.3
  264.1 0.0 copy-start.2
  264.1 1.1 copy.48
  265.2 0.0 copy-done.8
  265.2 0.5 copy.49
  265.7 0.0 copy-done.3
  265.7 0.7 copy.50
  266.5 0.0 copy-done.2
  266.5 0.7 copy.51
Async XLA Ops:
  0.6 6.3 %copy-start.4 = (f32[192,96]{1,0:T(8,128)S(1)}, f32[192,96]{1,0:T(8,128)}, u32[]{:S(2)}) copy-start(f32[192,96]{1,0:T(8,128)} %param.20) | copy-start | bytes 221188
  254.8 5.3 %copy-start.5 = (f32[96,192]{1,0:T(8,128)S(1)}, f32[96,192]{1,0:T(8,128)}, u32[]{:S(2)}) copy-start(f32[96,192]{1,0:T(8,128)} %get-tuple-element.76) | copy-start | bytes 221188
  254.8 6.1 %copy-start.7 = (f32[1,768]{1,0:T(1,128)S(1)}, f32[1,768]{1,0:T(1,128)}, u32[]{:S(2)}) copy-start(f32[1,768]{1,0:T(1,128)} %get-tuple-element.78) | copy-start | bytes 9220
  254.8 6.7 %copy-start.6 = (f32[1,768]{1,0:T(1,128)S(1)}, f32[1,768]{1,0:T(1,128)}, u32[]{:S(2)}) copy-start(f32[1,768]{1,0:T(1,128)} %get-tuple-element.80) | copy-start | bytes 9220
  254.8 7.3 %copy-start.1 = (f32[512,768]{1,0:T(8,128)S(1)}, f32[512,768]{1,0:T(8,128)}, u32[]{:S(2)}) copy-start(f32[512,768]{1,0:T(8,128)} %get-tuple-element.70) | copy-start | bytes 4718596
  262.1 2.0 copy-start
  264.1 1.2 copy-start.8
  264.1 1.7 copy-start.3
  264.1 2.4 copy-start.2

commit v6 on v5

--- a/solution.py
+++ b/solution.py
@@ -98,6 +98,10 @@
 MESH = pl.DeviceIdType.MESH
 
 
+def local_copies(sources, targets, sems):
+    return [pltpu.make_async_copy(a, b, sems.at[i]) for i, (a, b) in enumerate(zip(sources, targets))]
+
+
 def flip(index, bit):
     return index + bit - 2 * bit * lax.rem(lax.div(index, bit), 2)
 
@@ -482,14 +486,16 @@
 
 def start_kernel(
     sizes, heads, chunks,
-    condition, condition_weight, condition_bias, tokens, in_shard, out_shard, cosine, sine, cotangent, valid,
+    condition, condition_weight, vectors, tokens, in_weight, out_weight, cosine, sine, cotangent, valid,
     modulation, normed, qkv, out_full, feed_back, bias_part, in_t, condition_all,
-    pieces, arrived, in_full, out_t, unit, sems_tiny, sems_in, sems_out, sems_col,
+    in_shard, out_shard, pieces, arrived, in_full, out_t, unit, sems_tiny, sems_in, sems_out, sems_col,
 ):
     count = sizes["dp"] * sizes["row"]
     number = shard_number(sizes)
     rows, width = tokens.shape
     others = other_peers(sizes)
+    in_shard[...] = jnp.concatenate([in_weight[t] for t in range(3)], axis=1).astype(BF16)
+    out_shard[...] = out_weight[...].T.astype(BF16)
     greet([peer for _, peer in others] + col_peers())
     gather_in = ShardGather(sizes, in_shard, in_full, sems_in)
     gather_out = ShardGather(sizes, out_shard, out_t, sems_out)
@@ -523,7 +529,7 @@
     for i in range(count - 1):
         condition_copy(i, others[i][0]).wait_recv()
     stacked = jnp.concatenate([condition_all[b] for b in range(count)], axis=0)
-    product = contract(stacked.astype(BF16), condition_weight[...], 1, 0)
+    product = contract(stacked.astype(BF16), condition_weight[...].astype(BF16), 1, 1)
     for b in range(count):
         pieces[b] = product[b : b + 1]
     for i in range(count - 1):
@@ -533,7 +539,7 @@
     gather_out.advance(1)
     for i in range(count - 1):
         piece_copy(i, number, others[i][0]).wait_recv()
-    line = jnp.concatenate([arrived[b] for b in range(count)], axis=1) + condition_bias[...]
+    line = jnp.concatenate([arrived[b] for b in range(count)], axis=1) + vectors[:, : 6 * width]
     parts = [line[:, t * width : (t + 1) * width] for t in range(6)]
     for t in range(6):
         modulation[t : t + 1, :] = parts[t]
@@ -613,13 +619,13 @@
     return out
 
 
-def start(sizes, heads, condition, condition_weight, condition_bias, tokens, in_shard, out_shard, cosine, sine, cotangent, valid):
+def start(sizes, heads, condition, condition_weight, vectors, tokens, in_weight, out_weight, cosine, sine, cotangent, valid):
     count = sizes["dp"] * sizes["row"]
     rows, width = tokens.shape
     length = cosine.shape[1]
     chunks = 2
     vmem = pl.BlockSpec(memory_space=pltpu.VMEM)
-    piece = condition_weight.shape[1]
+    piece = condition_weight.shape[0]
     local = heads * HD
     return pl.pallas_call(
         functools.partial(start_kernel, sizes, heads, chunks),
@@ -636,6 +642,8 @@
         in_specs=[vmem] * 10,
         out_specs=[vmem] * 8,
         scratch_shapes=[
+            pltpu.VMEM((width // count, 3 * local), BF16),
+            pltpu.VMEM((width // count, local), BF16),
             pltpu.VMEM((count, 1, piece), F32),
             pltpu.VMEM((count, 1, piece), F32),
             pltpu.VMEM((width, 3 * local), BF16),
@@ -649,7 +657,7 @@
         compiler_params=pltpu.CompilerParams(
             vmem_limit_bytes=VMEM_LIMIT, collective_id=0, has_side_effects=True
         ),
-    )(condition, condition_weight, condition_bias, tokens, in_shard, out_shard, cosine, sine, cotangent, valid)
+    )(condition, condition_weight, vectors, tokens, in_weight, out_weight, cosine, sine, cotangent, valid)
 
 
 def attention_kernel(
@@ -662,7 +670,7 @@
     rows = feed_back.shape[0]
     length = qkv.shape[2]
     up_low[...] = up_shard[...].astype(BF16)
-    down_low[...] = down_shard[...].T.astype(BF16)
+    down_low[...] = down_shard[...].astype(BF16)
     greet(neighbour_peers(sizes) + col_peers())
     gather_up = ShardGather(sizes, up_low, up_full, sems_up)
     gather_down = ShardGather(sizes, down_low, down_t, sems_down)
@@ -761,13 +769,27 @@
 
 def feed_kernel(
     sizes, heads, chunks,
-    tokens, attention, parts, up_full, down_t, up_bias, feed_back_all, cotangent, valid, mixed_t, out_full,
-    middle, middle_back, mixed_back, up_grad, down_grad, out_grad, up_part, sums, feed_far, feed_kept,
+    tokens, attention, parts, vectors, valid, up_far, down_far, feed_back_far, cotangent_far, mixed_far, out_far,
+    mixed_back, out_grad, up_part, sums, middle_to, middle_back_to, up_to, down_to, feed_far_to, feed_kept_to,
     second_all, hidden_all, before_all, back_all, second_sems, back_sems,
     pair_out, pair_in, far_out, far_in, kept, scatter_sems, feed_pair_out, feed_pair_in, feed_sems,
+    up_full, down_t, feed_back_all, cotangent, mixed_t, out_full,
+    middle, middle_back, up_grad, down_grad, feed_far, feed_kept, load_sems, store_sems,
 ):
     rows, width = tokens.shape
     size = rows // chunks
+    loads = local_copies(
+        (up_far, down_far, feed_back_far, cotangent_far, mixed_far, out_far),
+        (up_full, down_t, feed_back_all, cotangent, mixed_t, out_full),
+        load_sems,
+    )
+    stores = local_copies(
+        (middle, feed_far, middle_back, up_grad, down_grad, feed_kept),
+        (middle_to, feed_far_to, middle_back_to, up_to, down_to, feed_kept_to),
+        store_sems,
+    )
+    for copy in loads:
+        copy.start()
     length = 4 * rows
     greet(col_peers())
     gather = ColumnGather(second_all, chunks, second_sems)
@@ -782,6 +804,8 @@
         second_all[me, here, :] = (layer_norm(value) * (1.0 + parts[4:5, :]) + parts[3:4, :]).astype(BF16)
         gather.start(j)
     up_part[...] = jnp.zeros_like(up_part)
+    for copy in loads:
+        copy.wait()
 
     def block(i, _):
         late = lax.div(i, 4)
@@ -807,7 +831,7 @@
         def _():
             gather.diagonal(1)
 
-        before = contract(second_all[slot, here, :], up_full[...], 1, 0) + up_bias[...]
+        before = contract(second_all[slot, here, :], up_full[...], 1, 0) + vectors[:, 6 * width : 6 * width + up_part.shape[1]]
         bend = jnp.tanh(SLOPE * (before + CUBIC * before * before * before))
         hidden = (0.5 * before * (1.0 + bend)).astype(BF16)
         slope = 0.5 * (1.0 + bend) + 0.5 * before * (1.0 - bend * bend) * (SLOPE * (1.0 + 3.0 * CUBIC * before * before))
@@ -832,6 +856,8 @@
         return 0
 
     lax.fori_loop(0, 8, block, 0)
+    stores[0].start()
+    stores[1].start()
     gate_sum = jnp.zeros((1, width), F32)
     shift_sum = jnp.zeros((1, width), F32)
     scale_sum = jnp.zeros((1, width), F32)
@@ -859,6 +885,8 @@
     for j in range(chunks):
         feed.settle(j)
     gather_back.across(0)
+    for copy in stores[2:5]:
+        copy.start()
 
     def mix(i, _):
         @pl.when(i == 1)
@@ -868,6 +896,7 @@
 
         @pl.when(i == 2)
         def _():
+            stores[5].start()
             gather_back.across(1)
 
         @pl.when(i == 3)
@@ -886,6 +915,8 @@
     out_grad[...] = contract(
         back_all[...].reshape(length, width), mixed_t[...].reshape(heads * HD, length), 0, 1
     ).astype(BF16)
+    for copy in stores:
+        copy.wait()
     gather.close()
     gather_back.close()
     scatter.close()
@@ -893,7 +924,7 @@
 
 
 def feed_forward(
-    sizes, heads, tokens, attention, parts, up_full, down_t, up_bias, feed_back_all, cotangent, valid, mixed_t, out_full
+    sizes, heads, tokens, attention, parts, up_full, down_t, vectors, feed_back_all, cotangent, valid, mixed_t, out_full
 ):
     rows, width = tokens.shape
     hidden = up_full.shape[1]
@@ -901,23 +932,25 @@
     local = heads * HD
     chunks = 2
     vmem = pl.BlockSpec(memory_space=pltpu.VMEM)
+    far = pl.BlockSpec(memory_space=pl.ANY)
     own = jax.ShapeDtypeStruct((rows, width), F32)
+    late = (up_full, down_t, feed_back_all, cotangent, mixed_t, out_full)
     return pl.pallas_call(
         functools.partial(feed_kernel, sizes, heads, chunks),
         out_shape=[
-            own,
-            own,
             jax.ShapeDtypeStruct((heads, HD, length), BF16),
-            jax.ShapeDtypeStruct((width, hidden), BF16),
-            jax.ShapeDtypeStruct((width, hidden), BF16),
             jax.ShapeDtypeStruct((width, local), BF16),
             jax.ShapeDtypeStruct((1, hidden), F32),
             jax.ShapeDtypeStruct((1, 3 * width), F32),
+            own,
+            own,
+            jax.ShapeDtypeStruct((width, hidden), BF16),
+            jax.ShapeDtypeStruct((width, hidden), BF16),
             jax.ShapeDtypeStruct((rows, width), BF16),
             own,
         ],
-        in_specs=[vmem] * 11,
-        out_specs=[vmem] * 10,
+        in_specs=[vmem] * 5 + [far] * 6,
+        out_specs=[vmem] * 4 + [far] * 6,
         scratch_shapes=[
             pltpu.VMEM((4, rows, width), BF16),
             pltpu.VMEM((4, rows, hidden), BF16),
@@ -929,11 +962,20 @@
             pltpu.VMEM((2, rows, width), BF16),
             pltpu.VMEM((2, rows, width), BF16),
             pltpu.SemaphoreType.DMA((2, 3, chunks)),
+            *[pltpu.VMEM(one.shape, one.dtype) for one in late],
+            pltpu.VMEM((rows, width), F32),
+            pltpu.VMEM((rows, width), F32),
+            pltpu.VMEM((width, hidden), BF16),
+            pltpu.VMEM((width, hidden), BF16),
+            pltpu.VMEM((rows, width), BF16),
+            pltpu.VMEM((rows, width), F32),
+            pltpu.SemaphoreType.DMA((6,)),
+            pltpu.SemaphoreType.DMA((6,)),
         ],
         compiler_params=pltpu.CompilerParams(
             vmem_limit_bytes=VMEM_LIMIT, collective_id=3, has_side_effects=True
         ),
-    )(tokens, attention, parts, up_full, down_t, up_bias, feed_back_all, cotangent, valid, mixed_t, out_full)
+    )(tokens, attention, parts, vectors, valid, *late)
 
 
 def contract_exact(left, right, left_axis, right_axis):
@@ -948,27 +990,36 @@
 
 def finish_kernel(
     sizes, heads, chunks,
-    qkv, bias, log_total, mixed_t, back_t, cosine, sine, normed, in_t, up_source, down_source, out_source,
-    tokens, middle_back, parts, others, down_part, up_part, condition_all, condition_weight,
-    middle, feed_far, feed_kept, cotangent, valid, down_bias_in,
-    output, tokens_back, condition_back, condition_grad, bias_grad, up_bias, down_bias, in_grad, out_grad, up_grad, down_grad,
+    qkv, bias, log_total, mixed_t, back_t, cosine, sine, up_source, down_source, out_source,
+    parts, others, down_part, up_part, condition_all, condition_weight, feed_far, valid, vectors,
+    normed_far, in_far, tokens_far, middle_back_far, middle_far, feed_kept_far, cotangent_far,
+    output_to, tokens_back_to, condition_back, condition_grad, bias_grad, up_bias, down_bias, in_grad, out_grad, up_grad, down_grad,
     turned, query, key, value, back, key_sum, value_sum, in_source,
     in_total, in_out, in_in, in_sems, up_total, up_out, up_in, up_sems,
     down_total, down_out, down_in, down_sems, out_total, out_out, out_in, out_sems,
     pair_out, pair_in, far_out, far_in, kept, col_sems,
     line_out, line_in, up_all, pieces, arrived, backs, collected, tiny_sems, line_sems, feed_in, feed_sems,
+    normed, in_t, tokens, middle_back, middle, feed_kept, cotangent, output, tokens_back, load_sems, store_sems,
+    condition_low, weight_low,
 ):
     count = sizes["dp"] * sizes["row"]
     number = shard_number(sizes)
     length = qkv.shape[2]
     rows, width = tokens.shape
     half = HD // 2
-    piece = condition_weight.shape[1]
-    cond = condition_weight.shape[0]
+    piece, cond = condition_weight.shape
     peers = other_peers(sizes)
-    greet([peer for _, peer in peers] + col_peers())
     me = lax.axis_index("col")
     near, far = col_peers()
+    greet([peer for _, peer in peers] + [near, far, {"col": flips(me, (1, 2))}])
+    loads = local_copies(
+        (normed_far, in_far, tokens_far, middle_back_far, middle_far, feed_kept_far, cotangent_far),
+        (normed, in_t, tokens, middle_back, middle, feed_kept, cotangent),
+        load_sems,
+    )
+    stores = local_copies((output, tokens_back), (output_to, tokens_back_to), store_sems)
+    for copy in loads:
+        copy.start()
     scatter_up = ShardScatter(sizes, up_source, up_total, up_out, up_in, up_sems)
     scatter_down = ShardScatter(sizes, down_source, down_total, down_out, down_in, down_sems)
     scatter_out = ShardScatter(sizes, out_source, out_total, out_out, out_in, out_sems)
@@ -987,8 +1038,12 @@
     def back_copy(i, mine, slot):
         return tiny(2, i, backs.at[mine], collected.at[slot])
 
-    def line_copy(k):
-        return send_copy(line_out.at[k], line_in.at[k], line_sems.at[0, k], line_sems.at[1, k], (near, far)[k])
+    def line_copy(k, arriving):
+        other = flips(me, [bit for bit in (1, 2) if k & bit])
+        slot = other if arriving else me
+        return send_copy(
+            line_out, line_in.at[slot], line_sems.at[0, k - 1], line_sems.at[1, k - 1], {"col": other}
+        )
 
     feed_copy = send_copy(feed_far, feed_in, feed_sems.at[0], feed_sems.at[1], far)
     feed_copy.start()
@@ -1006,6 +1061,8 @@
 
     for h in range(heads):
         prepare_backward(heads, h, rows, length, qkv, bias, log_total, mixed_t, back_t, query, key, value, back)
+    condition_low[...] = jnp.concatenate([condition_all[b] for b in range(count)], axis=0).astype(BF16)
+    weight_low[...] = condition_weight[...].astype(BF16)
     key_sum[...] = jnp.zeros_like(key_sum)
     value_sum[...] = jnp.zeros_like(value_sum)
 
@@ -1042,6 +1099,8 @@
         return 0
 
     lax.fori_loop(0, 4, finish_block, 0)
+    for copy in loads:
+        copy.wait()
     scatter_down.advance(2)
     scatter_out.advance(2)
     size = rows // chunks
@@ -1072,7 +1131,7 @@
     feed_copy.wait_recv()
     for j in range(chunks):
         here = pl.ds(j * size, size)
-        feed = feed_kept[here, :] + feed_in[here, :].astype(F32) + down_bias_in[...]
+        feed = feed_kept[here, :] + feed_in[here, :].astype(F32) + vectors[:, vectors.shape[1] - width :]
         output[here, :] = middle[here, :] + parts[5:6, :] * feed
         gate_sum = gate_sum + jnp.sum(cotangent[here, :] * valid[here, :] * feed, axis=0, keepdims=True)
     scatter_in.advance(1)
@@ -1088,24 +1147,26 @@
         tokens_back[here, :] = middle_back[here, :] + inverse * inner
         shift_sum = shift_sum + jnp.sum(grad, axis=0, keepdims=True)
         scale_sum = scale_sum + jnp.sum(grad * unit, axis=0, keepdims=True)
-    line_out[0] = jnp.concatenate([shift_sum, scale_sum, others[...], gate_sum, down_part[...]], axis=1)
-    line_copy(0).start()
+    line_out[...] = jnp.concatenate([shift_sum, scale_sum, others[...], gate_sum, down_part[...]], axis=1)
+    for k in (2, 3, 1):
+        line_copy(k, False).start()
+    line_in[me] = line_out[...]
     scatter_in.advance(2)
+    for copy in stores:
+        copy.start()
     steps = len(scatter_in.steps)
     for k in range(4, steps + 1):
         for one in (scatter_up, scatter_down, scatter_out):
             one.advance(k)
-    line_copy(0).wait_recv()
-    line_out[1] = line_out[0] + line_in[0]
-    line_copy(1).start()
     up_grad[...] = scatter_up.result()
     down_grad[...] = scatter_down.result()
     out_grad[...] = scatter_out.result()
     for i in range(count - 1):
         up_copy(i, peers[i][0]).wait_recv()
     up_bias[...] = jnp.sum(jnp.concatenate([up_all[b] for b in range(count)], axis=0), axis=0, keepdims=True)
-    line_copy(1).wait_recv()
-    line = line_out[1] + line_in[1]
+    for k in (1, 2, 3):
+        line_copy(k, True).wait_recv()
+    line = (line_in[0] + line_in[1]) + (line_in[2] + line_in[3])
     split = 6 * width
     for b in range(count):
         pieces[b] = jnp.concatenate([line[:, b * piece : (b + 1) * piece], line[:, split:]], axis=1)
@@ -1118,7 +1179,7 @@
     mine = stacked[:, :piece]
     down_bias[...] = jnp.sum(stacked[:, piece:], axis=0, keepdims=True)
     bias_piece = jnp.sum(mine, axis=0, keepdims=True)
-    back_rows = contract_exact(mine, condition_weight[...].astype(F32), 1, 1)
+    back_rows = contract_exact(mine, weight_low[...].astype(F32), 1, 0)
     for b in range(count):
         backs[b] = jnp.concatenate([back_rows[b : b + 1], bias_piece], axis=1)
     for i in range(count - 1):
@@ -1127,8 +1188,7 @@
     for k in range(3, steps + 1):
         scatter_in.advance(k)
     in_grad[...] = scatter_in.result()
-    conditions = jnp.concatenate([condition_all[b] for b in range(count)], axis=0)
-    condition_grad[...] = contract_exact(conditions, mine, 0, 0)
+    condition_grad[...] = contract_exact(condition_low[...].astype(F32), mine, 0, 0).T
     for i in range(count - 1):
         back_copy(i, number, peers[i][0]).wait_recv()
     gathered = [collected[b] for b in range(count)]
@@ -1140,8 +1200,10 @@
         up_copy(i, number).wait_send()
         piece_copy(i, peers[i][0], number).wait_send()
         back_copy(i, peers[i][0], number).wait_send()
-    for k in range(2):
-        line_copy(k).wait_send()
+    for k in (1, 2, 3):
+        line_copy(k, False).wait_send()
+    for copy in stores:
+        copy.wait()
     feed_copy.wait_send()
     for one in (scatter_up, scatter_down, scatter_out, scatter_in):
         one.close()
@@ -1150,15 +1212,17 @@
 
 def finish(sizes, heads, qkv, bias, log_total, mixed_t, back_t, cosine, sine, normed, in_t, up_source, down_source,
            out_source, tokens, middle_back, parts, others, down_part, up_part, condition_all, condition_weight,
-           middle, feed_far, feed_kept, cotangent, valid, down_bias):
+           middle, feed_far, feed_kept, cotangent, valid, vectors):
     count = sizes["dp"] * sizes["row"]
     length = qkv.shape[2]
     rows, width = tokens.shape
     chunks = 2
     local = heads * HD
     hidden = up_source.shape[1]
-    cond, piece = condition_weight.shape
+    piece, cond = condition_weight.shape
     share = width // count
+    late = (normed, in_t, tokens, middle_back, middle, feed_kept, cotangent)
+    far = pl.BlockSpec(memory_space=pl.ANY)
     vmem = pl.BlockSpec(memory_space=pltpu.VMEM)
     return pl.pallas_call(
         functools.partial(finish_kernel, sizes, heads, chunks),
@@ -1166,7 +1230,7 @@
             jax.ShapeDtypeStruct((rows, width), F32),
             jax.ShapeDtypeStruct((rows, width), F32),
             jax.ShapeDtypeStruct((1, cond), F32),
-            jax.ShapeDtypeStruct((cond, piece), F32),
+            jax.ShapeDtypeStruct((piece, cond), F32),
             jax.ShapeDtypeStruct((1, 6 * width), F32),
             jax.ShapeDtypeStruct((1, hidden), F32),
             jax.ShapeDtypeStruct((1, width), F32),
@@ -1175,8 +1239,8 @@
             jax.ShapeDtypeStruct((share, hidden), F32),
             jax.ShapeDtypeStruct((share, hidden), F32),
         ],
-        in_specs=[vmem] * 26,
-        out_specs=[vmem] * 11,
+        in_specs=[vmem] * 16 + [far] + [vmem] * 2 + [far] * len(late),
+        out_specs=[far] * 2 + [vmem] * 9,
         scratch_shapes=[
             pltpu.VMEM((3 * heads, HD, length), BF16),
             pltpu.VMEM((heads, AUG, length), BF16),
@@ -1191,24 +1255,62 @@
             *ShardScatter.scratch(count, share, hidden),
             *ShardScatter.scratch(count, share, local),
             *ColumnScatter.scratch(rows, width, chunks),
-            pltpu.VMEM((2, 1, 7 * width), F32),
-            pltpu.VMEM((2, 1, 7 * width), F32),
+            pltpu.VMEM((1, 7 * width), F32),
+            pltpu.VMEM((4, 1, 7 * width), F32),
             pltpu.VMEM((count, 1, hidden), F32),
             pltpu.VMEM((count, 1, piece + width), F32),
             pltpu.VMEM((count, 1, piece + width), F32),
             pltpu.VMEM((count, 1, cond + piece), F32),
             pltpu.VMEM((count, 1, cond + piece), F32),
             pltpu.SemaphoreType.DMA((2, 3, count - 1)),
-            pltpu.SemaphoreType.DMA((2, 2)),
+            pltpu.SemaphoreType.DMA((2, 3)),
             pltpu.VMEM((rows, width), BF16),
             pltpu.SemaphoreType.DMA((2,)),
+            *[pltpu.VMEM(one.shape, one.dtype) for one in late],
+            pltpu.VMEM((rows, width), F32),
+            pltpu.VMEM((rows, width), F32),
+            pltpu.SemaphoreType.DMA((len(late),)),
+            pltpu.SemaphoreType.DMA((2,)),
+            pltpu.VMEM((count, cond), BF16),
+            pltpu.VMEM((piece, cond), BF16),
         ],
         compiler_params=pltpu.CompilerParams(
             vmem_limit_bytes=VMEM_LIMIT, collective_id=2, has_side_effects=True
         ),
-    )(qkv, bias, log_total, mixed_t, back_t, cosine, sine, normed, in_t, up_source, down_source, out_source,
-      tokens, middle_back, parts, others, down_part, up_part, condition_all, condition_weight,
-      middle, feed_far, feed_kept, cotangent, valid, down_bias)
+    )(qkv, bias, log_total, mixed_t, back_t, cosine, sine, up_source, down_source, out_source,
+      parts, others, down_part, up_part, condition_all, condition_weight, feed_far, valid, vectors, *late)
+
+
+def emit_kernel(heads, output, tokens_back, condition_grad, in_grad, out_grad, up_grad, down_grad, *rest):
+    output_to, tokens_to, condition_to, in_to, out_to, up_to, down_to = rest[4:11]
+    for one, to in zip(rest[:3], rest[11:14]):
+        to[...] = one[...].reshape(to.shape)
+    rest[14][...] = rest[3][...]
+    output_to[...] = output[...]
+    tokens_to[...] = tokens_back[...]
+    condition_to[...] = condition_grad[...]
+    local = heads * HD
+    for t in range(3):
+        in_to[t] = in_grad[:, t * local : (t + 1) * local]
+    out_to[...] = out_grad[...].T
+    up_to[...] = up_grad[...]
+    down_to[...] = down_grad[...]
+
+
+def emit(heads, *arrays):
+    output, tokens_back, condition_grad, in_grad, out_grad, up_grad, down_grad = arrays[:7]
+    share, local = out_grad.shape
+    vmem = pl.BlockSpec(memory_space=pltpu.VMEM)
+    shapes = [
+        output.shape, tokens_back.shape, condition_grad.shape, (3, share, local), (local, share),
+        up_grad.shape, down_grad.shape, *[one.shape[1:] for one in arrays[7:10]], arrays[10].shape,
+    ]
+    return pl.pallas_call(
+        functools.partial(emit_kernel, heads),
+        out_shape=[jax.ShapeDtypeStruct(one, F32) for one in shapes],
+        in_specs=[vmem] * 11,
+        out_specs=[vmem] * 11,
+    )(*arrays)
 
 
 def shards(
@@ -1233,30 +1335,27 @@
     length_all = rows * columns
     local_width = attention_in.shape[2]
     heads = local_width // HD
-    in_shard = attention_in.reshape(attention_in.shape[0], 3 * local_width).astype(BF16)
-    out_shard = attention_out.T.astype(BF16)
-    condition_low = condition.astype(BF16)
-    weight_low = condition_weight.astype(BF16)
     own_rows = tokens[0]
     length = lengths[0]
     position = column_index * rows + jnp.arange(rows)
     valid = (position < length).astype(F32)
     bias = jnp.where(jnp.arange(length_all) < length, 0.0, MASKED).astype(F32)[None]
     cosine, sine = (jnp.asarray(table) for table in rotary_tables(length_all))
+    hidden_cols = up_weight.shape[1]
+    bias_part = lax.dynamic_slice_in_dim(up_bias, column_index * hidden_cols, hidden_cols)
+    vectors = jnp.concatenate([condition_bias, bias_part, down_bias])[None]
     parts, normed_blocks, qkv, out_full, feed_back, down_bias_part, in_t, condition_all = start(
-        sizes, heads, condition_low.astype(F32), weight_low, condition_bias[None], own_rows,
-        in_shard, out_shard, cosine, sine, cotangent[0], valid[:, None],
+        sizes, heads, condition, condition_weight.T, vectors, own_rows,
+        jnp.transpose(attention_in, (1, 0, 2)), attention_out, cosine, sine, cotangent[0], valid[:, None],
     )
     normed_all = normed_blocks.reshape(length_all, width)
     attention, mixed_t, log_total, feed_back_blocks, up_full, down_t = attend(
-        sizes, heads, qkv, bias, out_full, feed_back, up_weight, down_weight
+        sizes, heads, qkv, bias, out_full, feed_back, up_weight, down_weight.T
     )
-    hidden_cols = up_full.shape[1]
-    bias_part = lax.dynamic_slice_in_dim(up_bias, column_index * hidden_cols, hidden_cols)
     (
-        middle, middle_back, mixed_back, up_grad, down_grad, out_grad, up_bias_part, others, feed_far, feed_kept
+        mixed_back, out_grad, up_bias_part, others, middle, middle_back, up_grad, down_grad, feed_far, feed_kept
     ) = feed_forward(
-        sizes, heads, own_rows, attention, parts, up_full, down_t, bias_part[None], feed_back_blocks,
+        sizes, heads, own_rows, attention, parts, up_full, down_t, vectors, feed_back_blocks,
         cotangent[0], valid[:, None], mixed_t, out_full,
     )
     (
@@ -1265,21 +1364,28 @@
     ) = finish(
         sizes, heads, qkv, bias, log_total, mixed_t, mixed_back,
         cosine, sine, normed_all, in_t, up_grad, down_grad, out_grad, own_rows, middle_back, parts,
-        others, down_bias_part, up_bias_part, condition_all, weight_low,
-        middle, feed_far, feed_kept, cotangent[0], valid[:, None], down_bias[None],
+        others, down_bias_part, up_bias_part, condition_all, condition_weight.T,
+        middle, feed_far, feed_kept, cotangent[0], valid[:, None], vectors,
+    )
+    (
+        result, tokens_back, condition_grad, in_grad, out_grad, up_grad, down_grad,
+        bias_grad, up_bias_grad, down_bias_grad, condition_back,
+    ) = emit(
+        heads, result, tokens_back, condition_grad, in_grad, out_grad, up_grad, down_grad,
+        bias_grad, up_bias_grad, down_bias_grad, condition_back,
     )
     return (
         result[None],
         tokens_back[None],
         condition_back,
-        condition_grad,
-        bias_grad[0],
-        in_grad.reshape(attention_in.shape),
-        out_grad.T,
+        condition_grad.T,
+        bias_grad,
+        jnp.transpose(in_grad, (1, 0, 2)),
+        out_grad,
         up_grad,
-        up_bias_grad[0],
+        up_bias_grad,
         down_grad.T,
-        down_bias_grad[0],
+        down_bias_grad,
     )
 
 

time: 268 us -> 241 us (0.90)
  local copies, waits for them, and re-layouts: 19 us -> 0.78 us
  Pallas kernels: 241 us -> 236 us
  other arithmetic: 6.11 us -> 2.7 us
    unnamed x29 -> x0, local copies, waits for them, and re-layouts: 13 us -> none
    pallas_call x1, Pallas kernels: 63.9 us -> 59.1 us  [feed_forward(): pl.pallas_call(functools.partial(feed_kernel, sizes, heads, chunks), out_...]
    pallas_call x1, Pallas kernels: 94.1 us -> 89.3 us  [finish(): pl.pallas_call(functools.partial(finish_kernel, sizes, heads, chunks), ou...]
    pallas_call x0 -> x1, Pallas kernels: none -> 4.45 us  [emit(): pl.pallas_call(functools.partial(emit_kernel, heads), out_shape=[jax.Shap...]
    broadcast_in_dim x3 -> x0, local copies, waits for them, and re-layouts: 3.2 us -> none  [the longest x1 1.35 us: shards(): condition_bias[None]]
where the time goes in v6:
time: 241 us
  Pallas kernels  236 us (98%)
  other arithmetic  2.7 us (1%)
    pallas_call x1, Pallas kernels, finish(): pl.pallas_call(functools.partial(finish_kernel, sizes, heads, chunks), ou...  89.3 us
    pallas_call x1, Pallas kernels, feed_forward(): pl.pallas_call(functools.partial(feed_kernel, sizes, heads, chunks), out_...  59.1 us
    pallas_call x1, Pallas kernels, attend(): pl.pallas_call(functools.partial(attention_kernel, sizes, heads, chunks),...  43.4 us
    pallas_call x1, Pallas kernels, start(): pl.pallas_call(functools.partial(start_kernel, sizes, heads, chunks), out...  39.4 us

profile of v6, /device:TPU:0, one launch (start us, length us, event | category | flops | bytes accessed | tf_op | source)
XLA Modules:
  0.0 240.6 jit_solution(18119809569058041889)
XLA Ops:
  1.3 0.8 dynamic_slice.3
  2.1 0.6 compare_select_fusion.bias
  2.7 1.4 pad_maximum_fusion
  4.0 0.7 fusion.valid
  4.8 39.4 %shard_map.221 = (f32[6,768]{1,0:T(8,128)}, bf16[4,512,768]{2,1,0:T(8,128)(2,1)}, bf16[9,64,2048]{2,1,0:T(8,128)(2,1)}, bf16[192,768]{1,0:T(8,128)(2,1)}, bf16[5...) custom-call(f32[1,128]{1,0:T(1,128)} %condition.1, ...), custom_call_target="tpu_custom_call" | custom-call | tf_op jit(solution)/shard_map/pallas_call | solution.py:630
  44.2 43.4 %shard_map.222 = (f32[512,768]{1,0:T(8,128)}, bf16[3,64,2048]{2,1,0:T(8,128)(2,1)}, f32[3,1,2048]{2,1,0:T(1,128)}, bf16[4,512,768]{2,1,0:T(8,128)(2,1)}, bf16[76...) custom-call(bf16[9,64,2048]{2,1,0:T(8,128)(2,1)} %get-tuple-element.57.qkv, f32[1,2048]{1,0:T(1,128)} %compare_select_fusion.bias, ...), custom_call_target="tpu_custom_call" | custom-call | tf_op jit(solution)/shard_map/pallas_call | solution.py:742
  87.6 59.1 %shard_map.223 = (bf16[3,64,2048]{2,1,0:T(8,128)(2,1)}, bf16[768,192]{1,0:T(8,128)(2,1)}, f32[1,768]{1,0:T(1,128)}, f32[1,2304]{1,0:T(1,128)}, f32[512,768]{1,0:...) custom-call(f32[512,768]{1,0:T(8,128)} %bitcast.16, ...), custom_call_target="tpu_custom_call" | custom-call | tf_op jit(solution)/shard_map/pallas_call | solution.py:938
  146.7 89.3 %shard_map.224 = (f32[512,768]{1,0:T(8,128)}, f32[512,768]{1,0:T(8,128)}, f32[1,128]{1,0:T(1,128)}, f32[576,128]{1,0:T(8,128)}, f32[1,4608]{1,0:T(1,128)}, /*ind...) custom-call(bf16[9,64,2048]{2,1,0:T(8,128)(2,1)} %get-tuple-element., ...), custom_call_target="tpu_custom_call" | custom-call | tf_op jit(solution)/shard_map/pallas_call | solution.py:1227
  236.0 4.4 %shard_map.225 = (f32[512,768]{1,0:T(8,128)}, f32[512,768]{1,0:T(8,128)}, f32[576,128]{1,0:T(8,128)}, f32[3,96,192]{2,1,0:T(8,128)}, f32[192,96]{1,0:T(8,128)}, ...) custom-call(f32[512,768]{1,0:T(8,128)} %get-tuple-element.81.output,, ...), custom_call_target="tpu_custom_call" | custom-call | tf_op jit(solution)/shard_map/pallas_call | solution.py:1308

commit v7 on v6

--- a/solution.py
+++ b/solution.py
@@ -1101,8 +1101,6 @@
     lax.fori_loop(0, 4, finish_block, 0)
     for copy in loads:
         copy.wait()
-    scatter_down.advance(2)
-    scatter_out.advance(2)
     size = rows // chunks
 
     def part_of(slot, j):
@@ -1110,13 +1108,16 @@
         block = turned[:, :, pl.ds(start_at, size)].reshape(3 * heads * HD, size)
         return contract(block, in_t[...], 0, 0)
 
-    for j in range(chunks):
-        column.give_diagonal(j, part_of(flips(me, (1, 2)), j))
-    for j in range(chunks):
-        column.give_across(j, part_of(flip(me, 2), j))
+    for j in range(chunks + 1):
+        if j < chunks:
+            column.give_diagonal(j, part_of(flips(me, (1, 2)), j))
+        if j > 0:
+            column.give_across(j - 1, part_of(flip(me, 2), j - 1))
+    scatter_down.advance(2)
+    scatter_out.advance(2)
     in_source[...] = contract(
-        normed[...], turned[...].reshape(3 * heads * HD, length), 0, 1
-    ).astype(BF16)
+        turned[...].reshape(3 * heads * HD, length), normed[...], 1, 0
+    ).T.astype(BF16)
     scatter_in.start(0)
     scatter_up.advance(3)
     for j in range(chunks):
@@ -1216,7 +1217,7 @@
     count = sizes["dp"] * sizes["row"]
     length = qkv.shape[2]
     rows, width = tokens.shape
-    chunks = 2
+    chunks = 4
     local = heads * HD
     hidden = up_source.shape[1]
     piece, cond = condition_weight.shape

time: 241 us -> 239 us (level)
  no operation moved by 1% of the time
where the time goes in v7:
time: 239 us
  Pallas kernels  234 us (98%)
  other arithmetic  2.7 us (1%)
    pallas_call x1, Pallas kernels, finish(): pl.pallas_call(functools.partial(finish_kernel, sizes, heads, chunks), ou...  87.7 us
    pallas_call x1, Pallas kernels, feed_forward(): pl.pallas_call(functools.partial(feed_kernel, sizes, heads, chunks), out_...  59.1 us
    pallas_call x1, Pallas kernels, attend(): pl.pallas_call(functools.partial(attention_kernel, sizes, heads, chunks),...  43.4 us
    pallas_call x1, Pallas kernels, start(): pl.pallas_call(functools.partial(start_kernel, sizes, heads, chunks), out...  39.4 us

profile of v7, /device:TPU:0, one launch (start us, length us, event | category | flops | bytes accessed | tf_op | source)
XLA Modules:
  0.0 239.0 jit_solution(17664587569244148053)
XLA Ops:
  1.3 0.8 dynamic_slice.3
  2.1 0.6 compare_select_fusion.bias
  2.7 1.4 pad_maximum_fusion
  4.0 0.7 fusion.valid
  4.8 39.4 %shard_map.221 = (f32[6,768]{1,0:T(8,128)}, bf16[4,512,768]{2,1,0:T(8,128)(2,1)}, bf16[9,64,2048]{2,1,0:T(8,128)(2,1)}, bf16[192,768]{1,0:T(8,128)(2,1)}, bf16[5...) custom-call(f32[1,128]{1,0:T(1,128)} %condition.1, ...), custom_call_target="tpu_custom_call" | custom-call | tf_op jit(solution)/shard_map/pallas_call | solution.py:630
  44.2 43.4 %shard_map.222 = (f32[512,768]{1,0:T(8,128)}, bf16[3,64,2048]{2,1,0:T(8,128)(2,1)}, f32[3,1,2048]{2,1,0:T(1,128)}, bf16[4,512,768]{2,1,0:T(8,128)(2,1)}, bf16[76...) custom-call(bf16[9,64,2048]{2,1,0:T(8,128)(2,1)} %get-tuple-element.57.qkv, f32[1,2048]{1,0:T(1,128)} %compare_select_fusion.bias, ...), custom_call_target="tpu_custom_call" | custom-call | tf_op jit(solution)/shard_map/pallas_call | solution.py:742
  87.6 59.1 %shard_map.223 = (bf16[3,64,2048]{2,1,0:T(8,128)(2,1)}, bf16[768,192]{1,0:T(8,128)(2,1)}, f32[1,768]{1,0:T(1,128)}, f32[1,2304]{1,0:T(1,128)}, f32[512,768]{1,0:...) custom-call(f32[512,768]{1,0:T(8,128)} %bitcast.16, ...), custom_call_target="tpu_custom_call" | custom-call | tf_op jit(solution)/shard_map/pallas_call | solution.py:938
  146.7 87.7 %shard_map.224 = (f32[512,768]{1,0:T(8,128)}, f32[512,768]{1,0:T(8,128)}, f32[1,128]{1,0:T(1,128)}, f32[576,128]{1,0:T(8,128)}, f32[1,4608]{1,0:T(1,128)}, /*ind...) custom-call(bf16[9,64,2048]{2,1,0:T(8,128)(2,1)} %get-tuple-element., ...), custom_call_target="tpu_custom_call" | custom-call | tf_op jit(solution)/shard_map/pallas_call | solution.py:1228
  234.4 4.4 %shard_map.225 = (f32[512,768]{1,0:T(8,128)}, f32[512,768]{1,0:T(8,128)}, f32[576,128]{1,0:T(8,128)}, f32[3,96,192]{2,1,0:T(8,128)}, f32[192,96]{1,0:T(8,128)}, ...) custom-call(f32[512,768]{1,0:T(8,128)} %get-tuple-element.81.output,, ...), custom_call_target="tpu_custom_call" | custom-call | tf_op jit(solution)/shard_map/pallas_call | solution.py:1309
